TPU v7x, 32 devices: a whole 2x2x4 slice. The times are simulated.
32 devices in a mesh: gx: 2 (over x), gy: 4 (over y, core), gz: 4 (over z).
Axes of the slice: x: 2, y: 2, z: 4, core: 2. Of those that a mesh axis runs over, the one named last changes fastest.
Arguments:
- fluidity: float32 [16, 192, 1024], P('gx', 'gy', 'gz'), may hold values from -6 to 6
- local_fluidity: float32 [16, 192, 1024], P('gx', 'gy', 'gz'), may hold values from -12 to 18
- element_coef: float32 [2, 24, 128], P('gx', 'gy', 'gz'), may hold values from 0.2 to 2
- fdm_basis: float32 [8, 8], replicated, may hold values from -2 to 2
- fdm_values: float32 [8], replicated, may hold values from 0.5 to 40
- coarse_inverse: float32 [32, 32], P(('gx', 'gy', 'gz')), may hold values from -1 to 1
Outputs:
- correction: float32 [16, 192, 1024], P('gx', 'gy', 'gz')
All inputs are finite; a program needn't handle non-finite values.
Results may differ from a plain program's by a relative error of at most 0.0001.
Values sent between devices are 32-bit elements; how exact they have to be, the bound alone decides.
No kernel may reach another device: no remote copies, remote signals or barrier semaphores. Data moves between devices by JAX's collectives and lax.ppermute only.
A program may use at most 64 MiB of HBM per device.

v0:
```python
import jax
import jax.numpy as jnp
import numpy as np
from jax import lax
from jax.sharding import PartitionSpec as P

NP = 8


HALF_WIDTH = 3.0
HIGHEST = lax.Precision.HIGHEST
GLL_EIGHT = (
    -1.0,
    -0.8717401485096066,
    -0.5917001814331423,
    -0.2092992179024789,
    0.2092992179024789,
    0.5917001814331423,
    0.8717401485096066,
    1.0,
)


def extended(block, sides, width):
    for axis, dim in sides:
        count = lax.axis_size(axis)
        forward = [(i, i + 1) for i in range(count - 1)]
        forward.append((count - 1, 0))
        backward = [(target, source) for source, target in forward]
        low = lax.ppermute(
            lax.slice_in_dim(block, block.shape[dim] - width, None, axis=dim), axis, forward
        )
        high = lax.ppermute(lax.slice_in_dim(block, 0, width, axis=dim), axis, backward)
        block = jnp.concatenate([low, block, high], axis=dim)
    return block


def gll_tables():
    degree = NP - 1
    gll_nodes = np.array(GLL_EIGHT)
    previous = np.ones(NP)
    current = gll_nodes * 1.0
    for order in range(2, degree + 1):
        following = ((2 * order - 1) * gll_nodes * current - (order - 1) * previous) / order
        previous = current
        current = following
    weights = 2.0 / (degree * (degree + 1) * current * current)
    identity = np.eye(NP)
    spacing = gll_nodes[:, None] - gll_nodes[None, :] + identity
    derivative = current[:, None] / current[None, :] / spacing * (1.0 - identity)
    end_value = degree * (degree + 1) / 4.0
    end_values = np.concatenate([np.array([-end_value]), np.zeros(NP - 2), np.array([end_value])])
    derivative = derivative + identity * end_values[None, :]
    return (jnp.asarray(weights, dtype=jnp.float32), jnp.asarray(derivative, dtype=jnp.float32))


def share_vector(length):
    position = jnp.arange(length) % NP
    return jnp.where((position == 0) | (position == NP - 1), 1.0, 2.0).astype(jnp.float32) ** (-1)


def slice_along(tensor, dimension, window):
    index_list = [slice(None)] * tensor.ndim
    index_list[dimension] = window
    return tensor[tuple(index_list)]


def fold_dimension(padded, dimension):
    length = padded.shape[dimension] - 2
    middle = slice_along(padded, dimension, slice(1, length + 1))
    before = slice_along(padded, dimension, slice(0, length))
    beyond = slice_along(padded, dimension, slice(2, length + 2))
    bcast_shape = [1] * padded.ndim
    bcast_shape[dimension] = length
    position = (jnp.arange(length) % NP).reshape(bcast_shape)
    return (
        middle + jnp.where(position == 0, before, 0.0) + jnp.where(position == NP - 1, beyond, 0.0)
    )


def assemble(padded):
    return fold_dimension(fold_dimension(fold_dimension(padded, 0), 1), 2)


def apply_matrix(matrix, tensor, dimension):
    size_x, size_y, size_z = tensor.shape
    if dimension == 0:
        split_view = tensor.reshape(size_x // NP, NP, size_y, size_z)
        return jnp.einsum("ab,ebyz->eayz", matrix, split_view, precision=HIGHEST).reshape(
            tensor.shape
        )
    if dimension == 1:
        split_view = tensor.reshape(size_x, size_y // NP, NP, size_z)
        return jnp.einsum("ab,xebz->xeaz", matrix, split_view, precision=HIGHEST).reshape(
            tensor.shape
        )
    block_diag = jnp.kron(jnp.eye(size_z // NP, dtype=jnp.float32), matrix.T)
    return jnp.dot(tensor, block_diag, precision=HIGHEST)


def expand_coef(coeffs):
    return jnp.repeat(jnp.repeat(jnp.repeat(coeffs, NP, 0), NP, 1), NP, 2)


def element_terms(current, target, coef_field, weights, derivative):
    size_x, size_y, size_z = current.shape
    mass_diag = (
        jnp.tile(weights, size_x // NP)[:, None, None]
        * jnp.tile(weights, size_y // NP)[None, :, None]
        * jnp.tile(weights, size_z // NP)[None, None, :]
    )
    flux_scale = mass_diag * coef_field
    stiffness = jnp.zeros(current.shape, jnp.float32)
    for dimension in range(3):
        gradient = apply_matrix(derivative, current, dimension)
        stiffness = stiffness + apply_matrix(derivative.T, flux_scale * gradient, dimension)
    return HALF_WIDTH**3 * mass_diag * (target - current) - HALF_WIDTH * stiffness


def fdm_solve(residual, coef_field, fdm_basis, fdm_values):
    size_x, size_y, size_z = residual.shape
    spectra = (
        jnp.tile(fdm_values, size_x // NP)[:, None, None]
        + jnp.tile(fdm_values, size_y // NP)[None, :, None]
        + jnp.tile(fdm_values, size_z // NP)[None, None, :]
    )
    transformed = residual
    for dimension in range(3):
        transformed = apply_matrix(fdm_basis.T, transformed, dimension)
    transformed = transformed / (coef_field * spectra + 1.0)
    for dimension in range(3):
        transformed = apply_matrix(fdm_basis, transformed, dimension)
    return transformed


def dirichlet_mask(size_x, size_z):
    total_x = lax.axis_size("gx") * size_x
    total_z = lax.axis_size("gz") * size_z
    index_x = lax.axis_index("gx") * size_x + jnp.arange(size_x, dtype=jnp.int32)
    index_z = lax.axis_index("gz") * size_z + jnp.arange(size_z, dtype=jnp.int32)
    keep_x = ((index_x > 0) & (index_x < total_x - 1)).astype(jnp.float32)
    keep_z = ((index_z > 0) & (index_z < total_z - 1)).astype(jnp.float32)
    return keep_x[:, None, None] * keep_z[None, None, :]


def on_device(fluidity, local_fluidity, element_coef, fdm_basis, fdm_values, coarse_inverse):
    weights, derivative = gll_tables()
    size_x, size_y, size_z = fluidity.shape
    points = size_x * size_y * size_z
    mask = dirichlet_mask(size_x, size_z)
    coef_field = expand_coef(element_coef)
    local_terms = element_terms(fluidity, local_fluidity, coef_field, weights, derivative)
    padded = extended(local_terms, (("gx", 0), ("gy", 1), ("gz", 2)), 1)
    share = (
        share_vector(size_x)[:, None, None]
        * share_vector(size_y)[None, :, None]
        * share_vector(size_z)[None, None, :]
    )
    residual = assemble(padded) * mask
    block_sum = jnp.sum(residual * share) / points
    coarse_total = lax.all_gather(block_sum.reshape(1), ("gx", "gy", "gz"), axis=0, tiled=True)
    coarse_value = jnp.dot(coarse_inverse[0], coarse_total, precision=HIGHEST)
    combined = fdm_solve(residual, coef_field, fdm_basis, fdm_values) + share * coarse_value
    padded_out = extended(combined, (("gx", 0), ("gy", 1), ("gz", 2)), 1)
    return assemble(padded_out) * mask


def solution(mesh):
    return jax.shard_map(
        on_device,
        mesh=mesh,
        in_specs=(
            P("gx", "gy", "gz"),
            P("gx", "gy", "gz"),
            P("gx", "gy", "gz"),
            P(),
            P(),
            P(("gx", "gy", "gz"), None),
        ),
        out_specs=P("gx", "gy", "gz"),
        check_vma=False,
    )
```

profile of v0, /device:TPU:0, one launch (start us, length us, event | category | flops | bytes accessed | tf_op | source)
XLA Modules:
  0.0 134.2 jit_solution(11269377286063536513)
XLA Ops:
  0.0 0.8 copy.39
  0.8 0.7 copy.78
  1.6 0.3 broadcast_in_dim.144
  1.9 0.4 broadcast_in_dim.147
  2.5 0.5 fusion
  3.0 0.5 convolution_bitcast_fusion.3
  4.0 6.7 %broadcast_multiply_fusion.2 = (f32[32,8,32,8]{3,2,1,0:T(8,128)}, f32[32,8,32,8]{3,2,1,0:T(8,128)}, f32[32,8,32,8]{3,2,1,0:T(8,128)}, f32[32,8,32,8]{3,2,1,0:T(8,128)}) fusion(f32[8,8]{1,0:T(8,128)S(1)} %copy-done.7, f32[32,32]{1,0:T(8,128)S(1)} %fusion.30, f32[8,8]{1,0:T(8,128)S(1)} %copy-done.2, f32[8,8]{1,0:T(8,128)S(1)} %copy.39, f32[8,8]{1,0:T(8,128)S(1)} %copy-done.8), kind=kLoop, calls=%fused_computation.2 | loop fusion | flops 262144 | bytes 1053696 | tf_op jit(solution)/shard_map/jit(kron)/mul | solution.py:97
  10.7 4.0 %reshape.342 = f32[256,256,1]{1,0,2:T(8,128)S(1)} reshape(f32[32,8,32,8]{3,2,1,0:T(8,128)} %get-tuple-element.22) | data formatting | bytes 524288 | tf_op jit(solution)/shard_map/jit(kron)/mul | solution.py:97
  14.8 0.7 fusion.6
  15.4 0.7 fusion.2
  16.1 4.0 %reshape.343 = f32[256,256,1]{1,0,2:T(8,128)S(1)} reshape(f32[32,8,32,8]{3,2,1,0:T(8,128)} %get-tuple-element.19) | data formatting | bytes 524288 | tf_op jit(solution)/shard_map/jit(kron)/mul | solution.py:97
  20.2 0.5 fusion.1
  20.7 0.5 copy-done.1
  21.1 0.9 fusion.4
  22.1 3.0 %collective-permute-start.1 = (f32[1,48,256]{2,0,1:T(1,128)S(1)}, f32[1,48,256]{2,0,1:T(1,128)S(1)}, u32[]{:S(2)}, u32[]{:S(2)}) collective-permute-start(f32[1,48,256]{2,0,1:T(1,128)S(1)} %get-tuple-element.18), channel_id=1, source_target_pairs={{16,0},{0,16},{17,1},{1,17},{18,2},{2,18},{19,3},{3,19},{20,4},{4,... | collective-permute-start | bytes 147464 | tf_op jit(solution)/shard_map/ppermute | solution.py:33
  25.6 1.6 %collective-permute-done.1 = f32[1,48,256]{2,0,1:T(1,128)S(1)} collective-permute-done((f32[1,48,256]{2,0,1:T(1,128)S(1)}, f32[1,48,256]{2,0,1:T(1,128)S(1)}, u32[]{:S(2)}, u32[]{:S(2)}) %collective-permute-start.1) | collective-permute-done | bytes 49184 | tf_op jit(solution)/shard_map/ppermute | solution.py:33
  27.2 2.0 %collective-permute-done = f32[1,48,256]{2,0,1:T(1,128)S(1)} collective-permute-done((f32[1,48,256]{2,0,1:T(1,128)S(1)}, f32[1,48,256]{2,0,1:T(1,128)S(1)}, u32[]{:S(2)}, u32[]{:S(2)}) %collective-permute-start) | collective-permute-done | bytes 49184 | tf_op jit(solution)/shard_map/ppermute | solution.py:30
  29.4 0.3 collective-permute-start.2
  29.8 1.1 collective-permute-done.3
  30.9 1.8 %collective-permute-done.2 = f32[10,1,256]{2,0,1:T(8,128)S(1)} collective-permute-done((f32[10,1,256]{2,0,1:T(8,128)S(1)}, f32[10,1,256]{2,0,1:T(8,128)S(1)}, u32[]{:S(2)}, u32[]{:S(2)}) %collective-permute-start.2) | collective-permute-done | bytes 10272 | tf_op jit(solution)/shard_map/ppermute | solution.py:30
  33.0 3.6 %collective-permute-start.5 = (f32[10,50,1]{2,0,1:T(8,128)S(1)}, f32[10,50,1]{2,0,1:T(8,128)S(1)}, u32[]{:S(2)}, u32[]{:S(2)}) collective-permute-start(f32[10,50,1]{2,0,1:T(8,128)S(1)} %get-tuple-element.10), channel_id=1, source_target_pairs={{1,0},{2,1},{3,2},{0,3},{5,4},{6,5},{7,6},{4,7},{9,8},{10,9},{11,1... | collective-permute-start | bytes 6008 | tf_op jit(solution)/shard_map/ppermute | solution.py:33
  36.7 4.0 %reshape.349 = f32[256,256,1]{1,0,2:T(8,128)S(1)} reshape(f32[32,8,32,8]{3,2,1,0:T(8,128)} %get-tuple-element.21) | data formatting | bytes 524288 | tf_op jit(solution)/shard_map/jit(kron)/mul | solution.py:97
  40.7 4.0 %reshape.346 = f32[256,256,1]{1,0,2:T(8,128)S(1)} reshape(f32[32,8,32,8]{3,2,1,0:T(8,128)} %get-tuple-element.20) | data formatting | bytes 524288 | tf_op jit(solution)/shard_map/jit(kron)/mul | solution.py:97
  44.8 1.7 %collective-permute-done.5 = f32[10,50,1]{2,0,1:T(8,128)S(1)} collective-permute-done((f32[10,50,1]{2,0,1:T(8,128)S(1)}, f32[10,50,1]{2,0,1:T(8,128)S(1)}, u32[]{:S(2)}, u32[]{:S(2)}) %collective-permute-start.5) | collective-permute-done | bytes 2032 | tf_op jit(solution)/shard_map/ppermute | solution.py:33
  46.5 8.7 %collective-permute-done.4 = f32[10,50,1]{2,0,1:T(8,128)S(1)} collective-permute-done((f32[10,50,1]{2,0,1:T(8,128)S(1)}, f32[10,50,1]{2,0,1:T(8,128)S(1)}, u32[]{:S(2)}, u32[]{:S(2)}) %collective-permute-start.4) | collective-permute-done | bytes 2032 | tf_op jit(solution)/shard_map/ppermute | solution.py:30
  55.2 0.9 pad_maximum_fusion
  56.5 0.9 fusion.16
  57.4 0.5 fusion.35
  57.9 0.6 convolution_bitcast_fusion.1
  58.5 0.7 convolution_divide_fusion
  59.2 0.5 fusion.33
  60.4 0.6 convolution_bitcast_fusion
  61.0 39.4 %all-reduce = f32[32]{0:T(128)S(1)} all-reduce(f32[32]{0:T(128)S(1)} %dynamic-update-slice), channel_id=1, replica_groups=mesh['gx'=2,'gy'=4,'gz'=4] {'gx','gy','gz'}, use_global_device_ids=true, to_apply=%add | all-reduce | flops 32 | bytes 256
  100.4 0.6 fusion.40
  101.0 1.3 convolution_add_fusion
  102.4 2.3 %collective-permute-start.7 = (f32[1,48,256]{2,0,1:T(1,128)S(1)}, f32[1,48,256]{2,0,1:T(1,128)S(1)}, u32[]{:S(2)}, u32[]{:S(2)}) collective-permute-start(f32[1,48,256]{2,0,1:T(1,128)S(1)} %get-tuple-element.16), channel_id=1, source_target_pairs={{16,0},{0,16},{17,1},{1,17},{18,2},{2,18},{19,3},{3,19},{20,4},{4,... | collective-permute-start | bytes 147464 | tf_op jit(solution)/shard_map/ppermute | solution.py:33
  104.8 2.0 %collective-permute-done.7 = f32[1,48,256]{2,0,1:T(1,128)S(1)} collective-permute-done((f32[1,48,256]{2,0,1:T(1,128)S(1)}, f32[1,48,256]{2,0,1:T(1,128)S(1)}, u32[]{:S(2)}, u32[]{:S(2)}) %collective-permute-start.7) | collective-permute-done | bytes 49184 | tf_op jit(solution)/shard_map/ppermute | solution.py:33
  106.8 2.0 %collective-permute-done.6 = f32[1,48,256]{2,0,1:T(1,128)S(1)} collective-permute-done((f32[1,48,256]{2,0,1:T(1,128)S(1)}, f32[1,48,256]{2,0,1:T(1,128)S(1)}, u32[]{:S(2)}, u32[]{:S(2)}) %collective-permute-start.6) | collective-permute-done | bytes 49184 | tf_op jit(solution)/shard_map/ppermute | solution.py:30
  108.9 0.5 collective-permute-start.8
  109.4 0.9 collective-permute-done.9
  110.3 1.8 %collective-permute-done.8 = f32[10,1,256]{2,0,1:T(8,128)S(1)} collective-permute-done((f32[10,1,256]{2,0,1:T(8,128)S(1)}, f32[10,1,256]{2,0,1:T(8,128)S(1)}, u32[]{:S(2)}, u32[]{:S(2)}) %collective-permute-start.8) | collective-permute-done | bytes 10272 | tf_op jit(solution)/shard_map/ppermute | solution.py:30
  112.4 1.6 %collective-permute-start.11 = (f32[10,50,1]{2,0,1:T(8,128)S(1)}, f32[10,50,1]{2,0,1:T(8,128)S(1)}, u32[]{:S(2)}, u32[]{:S(2)}) collective-permute-start(f32[10,50,1]{2,0,1:T(8,128)S(1)} %get-tuple-element.8), channel_id=1, source_target_pairs={{1,0},{2,1},{3,2},{0,3},{5,4},{6,5},{7,6},{4,7},{9,8},{10,9},{11,1... | collective-permute-start | bytes 6008 | tf_op jit(solution)/shard_map/ppermute | solution.py:33
  114.0 0.5 collective-permute-start.10
  114.5 10.2 %collective-permute-done.11 = f32[10,50,1]{2,0,1:T(8,128)S(1)} collective-permute-done((f32[10,50,1]{2,0,1:T(8,128)S(1)}, f32[10,50,1]{2,0,1:T(8,128)S(1)}, u32[]{:S(2)}, u32[]{:S(2)}) %collective-permute-start.11) | collective-permute-done | bytes 2032 | tf_op jit(solution)/shard_map/ppermute | solution.py:33
  124.7 7.1 %collective-permute-done.10 = f32[10,50,1]{2,0,1:T(8,128)S(1)} collective-permute-done((f32[10,50,1]{2,0,1:T(8,128)S(1)}, f32[10,50,1]{2,0,1:T(8,128)S(1)}, u32[]{:S(2)}, u32[]{:S(2)}) %collective-permute-start.10) | collective-permute-done | bytes 2032 | tf_op jit(solution)/shard_map/ppermute | solution.py:30
  131.8 0.9 pad_maximum_fusion.1
  133.1 0.3 fusion.18
  133.3 0.9 copy.41
  (65 shorter events, 3.3 us)
Async XLA Ops:
  0.0 2.3 %copy-start.5 = (f32[8]{0:T(128)S(1)}, f32[8]{0:T(128)}, u32[]{:S(2)}) copy-start(f32[8]{0:T(128)} %constant.101.clone) | copy-start | bytes 100
  0.0 2.4 %copy-start.4 = (f32[8,8,1,1]{1,0,3,2:T(8,128)S(1)}, f32[8,8,1,1]{1,0,3,2:T(8,128)}, u32[]{:S(2)}) copy-start(f32[8,8,1,1]{1,0,3,2:T(8,128)} %constant.112) | copy-start | bytes 772
  0.0 2.4 %copy-start = (f32[8,48,256]{2,1,0:T(8,128)S(1)}, f32[8,48,256]{2,1,0:T(8,128)}, u32[]{:S(2)}) copy-start(f32[8,48,256]{2,1,0:T(8,128)} %param.8) | copy-start | bytes 1179652
  2.5 1.5 %copy-start.2 = (f32[8,8]{1,0:T(8,128)S(1)}, f32[8,8]{1,0:T(8,128)}, u32[]{:S(2)}) copy-start(f32[8,8]{1,0:T(8,128)} %param.11) | copy-start | bytes 772
  2.5 1.5 %copy-start.7 = (f32[8,8]{1,0:T(8,128)S(1)}, f32[8,8]{1,0:T(8,128)}, u32[]{:S(2)}) copy-start(f32[8,8]{1,0:T(8,128)} %constant.102.clone) | copy-start | bytes 772
  2.5 1.5 %copy-start.8 = (f32[8,8]{1,0:T(8,128)S(1)}, f32[8,8]{1,0:T(8,128)}, u32[]{:S(2)}) copy-start(f32[8,8]{1,0:T(8,128)} %constant.105) | copy-start | bytes 772
  10.7 4.0 %copy-start.3 = (f32[8,8,1]{1,0,2:T(8,128)S(1)}, f32[8,8,1]{1,0,2:T(8,128)}, u32[]{:S(2)}) copy-start(f32[8,8,1]{1,0,2:T(8,128)} %constant.111) | copy-start | bytes 772
  20.1 1.0 copy-start.1
  21.1 4.1 %copy-start.6 = (f32[8]{0:T(128)S(1)}, f32[8]{0:T(128)}, u32[]{:S(2)}) copy-start(f32[8]{0:T(128)} %param.12) | copy-start | bytes 100
  22.1 5.1 %collective-permute-start.1 = (f32[1,48,256]{2,0,1:T(1,128)S(1)}, f32[1,48,256]{2,0,1:T(1,128)S(1)}, u32[]{:S(2)}, u32[]{:S(2)}) collective-permute-start(f32[1,48,256]{2,0,1:T(1,128)S(1)} %get-tuple-element.18), channel_id=1, source_target_pairs={{16,0},{0,16},{17,1},{1,17},{18,2},{2,18},{19,3},{3,19},{20,4},{4,... | collective-permute-start | bytes 147464 | tf_op jit(solution)/shard_map/ppermute | solution.py:33
  25.1 4.1 %collective-permute-start = (f32[1,48,256]{2,0,1:T(1,128)S(1)}, f32[1,48,256]{2,0,1:T(1,128)S(1)}, u32[]{:S(2)}, u32[]{:S(2)}) collective-permute-start(f32[1,48,256]{2,0,1:T(1,128)S(1)} %get-tuple-element.17), channel_id=1, source_target_pairs={{0,16},{16,0},{1,17},{17,1},{2,18},{18,2},{3,19},{19,3},{4,20},{20... | collective-permute-start | bytes 147464 | tf_op jit(solution)/shard_map/ppermute | solution.py:30
  29.2 1.7 %collective-permute-start.3 = (f32[10,1,256]{2,0,1:T(8,128)S(1)}, f32[10,1,256]{2,0,1:T(8,128)S(1)}, u32[]{:S(2)}, u32[]{:S(2)}) collective-permute-start(f32[10,1,256]{2,0,1:T(8,128)S(1)} %get-tuple-element.14), channel_id=1, source_target_pairs={{4,0},{8,4},{12,8},{0,12},{5,1},{9,5},{13,9},{1,13},{6,2},{10,6},{... | collective-permute-start | bytes 30728 | tf_op jit(solution)/shard_map/ppermute | solution.py:33
  29.4 3.2 %collective-permute-start.2 = (f32[10,1,256]{2,0,1:T(8,128)S(1)}, f32[10,1,256]{2,0,1:T(8,128)S(1)}, u32[]{:S(2)}, u32[]{:S(2)}) collective-permute-start(f32[10,1,256]{2,0,1:T(8,128)S(1)} %get-tuple-element.13), channel_id=1, source_target_pairs={{0,4},{4,8},{8,12},{12,0},{1,5},{5,9},{9,13},{13,1},{2,6},{6,10},{... | collective-permute-start | bytes 30728 | tf_op jit(solution)/shard_map/ppermute | solution.py:30
  33.0 13.5 %collective-permute-start.5 = (f32[10,50,1]{2,0,1:T(8,128)S(1)}, f32[10,50,1]{2,0,1:T(8,128)S(1)}, u32[]{:S(2)}, u32[]{:S(2)}) collective-permute-start(f32[10,50,1]{2,0,1:T(8,128)S(1)} %get-tuple-element.10), channel_id=1, source_target_pairs={{1,0},{2,1},{3,2},{0,3},{5,4},{6,5},{7,6},{4,7},{9,8},{10,9},{11,1... | collective-permute-start | bytes 6008 | tf_op jit(solution)/shard_map/ppermute | solution.py:33
  36.6 18.6 %collective-permute-start.4 = (f32[10,50,1]{2,0,1:T(8,128)S(1)}, f32[10,50,1]{2,0,1:T(8,128)S(1)}, u32[]{:S(2)}, u32[]{:S(2)}) collective-permute-start(f32[10,50,1]{2,0,1:T(8,128)S(1)} %get-tuple-element.9), channel_id=1, source_target_pairs={{0,1},{1,2},{2,3},{3,0},{4,5},{5,6},{6,7},{7,4},{8,9},{9,10},{10,1... | collective-permute-start | bytes 6008 | tf_op jit(solution)/shard_map/ppermute | solution.py:30
  59.2 41.2 %copy-start.9 = (f32[1,32]{1,0:T(1,128)S(1)}, f32[1,32]{1,0:T(1,128)}, u32[]{:S(2)}) copy-start(f32[1,32]{1,0:T(1,128)} %param.13) | copy-start | bytes 388
  102.4 4.4 %collective-permute-start.7 = (f32[1,48,256]{2,0,1:T(1,128)S(1)}, f32[1,48,256]{2,0,1:T(1,128)S(1)}, u32[]{:S(2)}, u32[]{:S(2)}) collective-permute-start(f32[1,48,256]{2,0,1:T(1,128)S(1)} %get-tuple-element.16), channel_id=1, source_target_pairs={{16,0},{0,16},{17,1},{1,17},{18,2},{2,18},{19,3},{3,19},{20,4},{4,... | collective-permute-start | bytes 147464 | tf_op jit(solution)/shard_map/ppermute | solution.py:33
  104.7 4.1 %collective-permute-start.6 = (f32[1,48,256]{2,0,1:T(1,128)S(1)}, f32[1,48,256]{2,0,1:T(1,128)S(1)}, u32[]{:S(2)}, u32[]{:S(2)}) collective-permute-start(f32[1,48,256]{2,0,1:T(1,128)S(1)} %get-tuple-element.15), channel_id=1, source_target_pairs={{0,16},{16,0},{1,17},{17,1},{2,18},{18,2},{3,19},{19,3},{4,20},{20... | collective-permute-start | bytes 147464 | tf_op jit(solution)/shard_map/ppermute | solution.py:30
  108.8 1.5 %collective-permute-start.9 = (f32[10,1,256]{2,0,1:T(8,128)S(1)}, f32[10,1,256]{2,0,1:T(8,128)S(1)}, u32[]{:S(2)}, u32[]{:S(2)}) collective-permute-start(f32[10,1,256]{2,0,1:T(8,128)S(1)} %get-tuple-element.12), channel_id=1, source_target_pairs={{4,0},{8,4},{12,8},{0,12},{5,1},{9,5},{13,9},{1,13},{6,2},{10,6},{... | collective-permute-start | bytes 30728 | tf_op jit(solution)/shard_map/ppermute | solution.py:33
  108.9 3.2 %collective-permute-start.8 = (f32[10,1,256]{2,0,1:T(8,128)S(1)}, f32[10,1,256]{2,0,1:T(8,128)S(1)}, u32[]{:S(2)}, u32[]{:S(2)}) collective-permute-start(f32[10,1,256]{2,0,1:T(8,128)S(1)} %get-tuple-element.11), channel_id=1, source_target_pairs={{0,4},{4,8},{8,12},{12,0},{1,5},{5,9},{9,13},{13,1},{2,6},{6,10},{... | collective-permute-start | bytes 30728 | tf_op jit(solution)/shard_map/ppermute | solution.py:30
  112.4 12.3 %collective-permute-start.11 = (f32[10,50,1]{2,0,1:T(8,128)S(1)}, f32[10,50,1]{2,0,1:T(8,128)S(1)}, u32[]{:S(2)}, u32[]{:S(2)}) collective-permute-start(f32[10,50,1]{2,0,1:T(8,128)S(1)} %get-tuple-element.8), channel_id=1, source_target_pairs={{1,0},{2,1},{3,2},{0,3},{5,4},{6,5},{7,6},{4,7},{9,8},{10,9},{11,1... | collective-permute-start | bytes 6008 | tf_op jit(solution)/shard_map/ppermute | solution.py:33
  114.0 17.8 %collective-permute-start.10 = (f32[10,50,1]{2,0,1:T(8,128)S(1)}, f32[10,50,1]{2,0,1:T(8,128)S(1)}, u32[]{:S(2)}, u32[]{:S(2)}) collective-permute-start(f32[10,50,1]{2,0,1:T(8,128)S(1)} %get-tuple-element.7), channel_id=1, source_target_pairs={{0,1},{1,2},{2,3},{3,0},{4,5},{5,6},{6,7},{7,4},{8,9},{9,10},{10,1... | collective-permute-start | bytes 6008 | tf_op jit(solution)/shard_map/ppermute | solution.py:30
where the time goes:
time: 135 us; the launch traced here: 134 us
  waiting for transfers between devices  40.9 us (30%)
  blocking collectives  39.4 us (29%)
  local copies, waits for them, and re-layouts  21 us (16%)
  starting transfers between devices  12.4 us (9%)
  other arithmetic  11.8 us (9%)
  matrix products  7.75 us (6%)
    unnamed x1, blocking collectives  39.4 us
    ppermute x6, waiting for transfers between devices, extended(): lax.ppermute(lax.slice_in_dim(block, block.shape[dim] - width, None, axis...  23.4 us
    ppermute x6, waiting for transfers between devices, extended(): lax.ppermute(lax.slice_in_dim(block, 0, width, axis=dim), axis, backward)  17.5 us
    mul x4, local copies, waits for them, and re-layouts, apply_matrix(): block_diag = jnp.kron(jnp.eye(size_z // NP, dtype=jnp.float32), matrix.T)  16.1 us
    ppermute x6, starting transfers between devices, extended(): lax.ppermute(lax.slice_in_dim(block, 0, width, axis=dim), axis, backward)  10.9 us
    mul x1, other arithmetic, apply_matrix(): block_diag = jnp.kron(jnp.eye(size_z // NP, dtype=jnp.float32), matrix.T)  6.72 us
    dot_general x4, matrix products, apply_matrix(): return jnp.dot(tensor, block_diag, precision=HIGHEST)  3.49 us
  transfers between devices with their start and end apart: 12, of which 12 were waited for; matrix products, arithmetic and copies ran while one was open for 6% of the time, Pallas kernels for 0%

commit v1 on v0

v1 whole, which is shorter than its diff:
```python
import functools

import jax
import jax.numpy as jnp
import numpy as np
from jax import lax
from jax.experimental import pallas as pl
from jax.experimental.pallas import tpu as pltpu
from jax.sharding import PartitionSpec as P

NP = 8
HALF_WIDTH = 3.0
HIGHEST = lax.Precision.HIGHEST
AXES = ("gx", "gy", "gz")
LANES = 128
GLL_EIGHT = (
    -1.0,
    -0.8717401485096066,
    -0.5917001814331423,
    -0.2092992179024789,
    0.2092992179024789,
    0.5917001814331423,
    0.8717401485096066,
    1.0,
)


def gll_tables():
    degree = NP - 1
    gll_nodes = np.array(GLL_EIGHT)
    previous = np.ones(NP)
    current = gll_nodes * 1.0
    for order in range(2, degree + 1):
        following = ((2 * order - 1) * gll_nodes * current - (order - 1) * previous) / order
        previous = current
        current = following
    weights = 2.0 / (degree * (degree + 1) * current * current)
    identity = np.eye(NP)
    spacing = gll_nodes[:, None] - gll_nodes[None, :] + identity
    derivative = current[:, None] / current[None, :] / spacing * (1.0 - identity)
    end_value = degree * (degree + 1) / 4.0
    end_values = np.concatenate([np.array([-end_value]), np.zeros(NP - 2), np.array([end_value])])
    return weights, derivative + identity * end_values[None, :]


WEIGHTS, DERIVATIVE = gll_tables()
STIFF = (DERIVATIVE.T * WEIGHTS[None, :]) @ DERIVATIVE / WEIGHTS[:, None]


def dot(a, b, contract=((1,), (0,))):
    return lax.dot_general(
        a, b, (contract, ((), ())), precision=HIGHEST, preferred_element_type=jnp.float32
    )


def iota(shape, dim):
    return lax.broadcasted_iota(jnp.int32, shape, dim)


def is_even(axis):
    return lax.rem(lax.axis_index(axis), 2) == 0


def is_last(axis):
    return lax.axis_index(axis) == lax.axis_size(axis) - 1


def low_high(received, axis):
    if len(received) == 1:
        return received[0], received[0]
    even = is_even(axis)
    return jnp.where(even, received[1], received[0]), jnp.where(even, received[0], received[1])


def pair_payloads(low, high, axis, count):
    even = is_even(axis)
    payloads = [jnp.where(even, high, low)]
    if count > 1:
        payloads.append(jnp.where(even, low, high))
    return payloads


def merge(own, received):
    return jnp.where(own == 0.0, received, own)


def coarse_weight(position, length, first, last, offset):
    node = position % NP
    edge = (node == 0) | (node == NP - 1)
    at_low, at_high = position == 0, position == length - 1
    own = jnp.where(edge, jnp.where(at_low | at_high, 1.0, 2.0), 0.5)
    own = jnp.where((at_low & first) | (at_high & last), 0.0, own)
    low = jnp.where(at_low & jnp.logical_not(first), 1.0, 0.0)
    high = jnp.where(at_high & jnp.logical_not(last), 1.0, 0.0)
    return jnp.where(offset == 0, own, jnp.where(offset < 0, low, high))


def never():
    return jnp.bool_(False)


def z_weights(length, block, shape, position_dim):
    k = lax.axis_index("gz")
    offset = block - k
    value = coarse_weight(iota(shape, position_dim), length, k == 0, is_last("gz"), offset)
    return jnp.where(jnp.abs(offset) <= 1, value, 0.0)


def xy_weights(length_y, shape, y_dim, place, at_x, size_x):
    count = lax.axis_size("gy")
    i, j = lax.axis_index("gx"), lax.axis_index("gy")
    off_x = place // count - i
    off_y = lax.rem(place % count - j + count + 1, count) - 1
    y = coarse_weight(iota(shape, y_dim), length_y, False, False, off_y)
    x = coarse_weight(
        jnp.full(shape, at_x, jnp.int32), size_x, i == 0, is_last("gx"), off_x
    )
    return jnp.where((jnp.abs(off_x) <= 1) & (jnp.abs(off_y) <= 1), x * y, 0.0)


def store_faces(field_ref, yf_ref, zf_ref):
    size_x, size_y, size_z = field_ref.shape
    lane = iota((size_y, LANES), 1)
    low = jnp.zeros((size_y, LANES), jnp.float32)
    high = low
    for x in range(size_x):
        yf_ref[0, x : x + 1, :] = field_ref[x, 0:1, :]
        yf_ref[1, x : x + 1, :] = field_ref[x, size_y - 1 : size_y, :]
        low = jnp.where(lane == x, field_ref[x, :, 0:1], low)
        high = jnp.where(lane == x, field_ref[x, :, size_z - 1 : size_z], high)
    zf_ref[0] = low
    zf_ref[1] = high


def terms_kernel(gossip, pairs_x, u_ref, l_ref, coef_ref, cinv_ref, const_ref, t_ref, yf_ref, zf_ref, *outs):
    size_x, size_y, size_z = u_ref.shape
    x_refs = outs[:pairs_x]
    stiff_z = const_ref[0:size_z, :]
    stiff_y = const_ref[size_z : size_z + size_y, 0:size_y]
    mass = const_ref[size_z + size_y : size_z + size_y + NP, :]
    spread = (iota((size_z // NP, size_z), 0) == iota((size_z // NP, size_z), 1) // NP).astype(jnp.float32)
    coef = dot(coef_ref[0], spread) * HALF_WIDTH
    t_ref[...] = dot(u_ref[...].reshape(size_x * size_y, size_z), stiff_z).reshape(u_ref.shape)
    for x in range(size_x):
        t_ref[x] += dot(stiff_y, u_ref[x])
    for e in range(size_y // NP):
        rows = slice(e * NP, (e + 1) * NP)
        u = [u_ref[b, rows, :] for b in range(NP)]
        scale = coef[e : e + 1, :]
        for a in range(NP):
            total = t_ref[a, rows, :]
            for b in range(NP):
                total = total + float(STIFF[a, b]) * u[b]
            source = HALF_WIDTH**3 * (l_ref[a, rows, :] - u[a])
            t_ref[a, rows, :] = (float(WEIGHTS[a]) * mass) * (source - scale * total)
    store_faces(t_ref, yf_ref, zf_ref)
    faces = pair_payloads(t_ref[0], t_ref[size_x - 1], "gx", pairs_x)
    for ref, face in zip(x_refs, faces):
        ref[0:size_y, :] = face
    if gossip:
        tab = coarse_tables(t_ref, cinv_ref)
        outs[pairs_x][...] = tab
        x_refs[0][size_y:, :] = tab


def coarse_tables(t_ref, cinv_ref):
    size_x, size_y, size_z = t_ref.shape
    count_z = lax.axis_size("gz")
    rows = lax.axis_size("gx") * lax.axis_size("gy")
    device = (lax.axis_index("gx") * lax.axis_size("gy") + lax.axis_index("gy")) * count_z + lax.axis_index("gz")
    middle = t_ref[1]
    for x in range(2, size_x - 1):
        middle = middle + t_ref[x]
    total = jnp.zeros((rows, size_z), jnp.float32)
    for at_x, plane in ((0, t_ref[0]), (1, middle), (size_x - 1, t_ref[size_x - 1])):
        w = xy_weights(size_y, (rows, size_y), 1, iota((rows, size_y), 0), at_x, size_x)
        total = total + dot(w, plane)
    lane = iota((size_z, LANES), 1)
    w = z_weights(size_z, lane % count_z, (size_z, LANES), 0)
    points = size_x * size_y * size_z
    part = dot(total, jnp.where(lane // count_z == device, w, 0.0)) / points
    width = rows * count_z
    row = jnp.broadcast_to(cinv_ref[...], (rows, width))
    row = jnp.where(iota((rows, width), 1) // count_z == iota((rows, width), 0), row, 0.0)
    lane = iota((width, LANES), 1)
    place = (lane // count_z == device) & (lane % count_z == iota((width, LANES), 0) % count_z)
    inverse = dot(row, place.astype(jnp.float32))
    return jnp.concatenate([part, inverse], axis=1)


def coarse_planes(tab, size_x, size_y, size_z):
    count_z = lax.axis_size("gz")
    rows = tab.shape[0]
    same = (iota((LANES, LANES), 0) % count_z == iota((LANES, LANES), 1) % count_z).astype(jnp.float32)
    rhs = dot(tab[:, :LANES], same)
    value = jnp.sum(rhs * tab[:, LANES:], axis=0, keepdims=True)
    value = jnp.broadcast_to(value, (rows, LANES))
    value = jnp.where(iota((rows, LANES), 1) // (count_z * count_z) == iota((rows, LANES), 0), value, 0.0)
    shape = (LANES, size_z)
    line = dot(value, z_weights(size_z, (iota(shape, 0) // count_z) % count_z, shape, 1))
    planes = []
    for at_x in (0, 1, size_x - 1):
        w = xy_weights(size_y, (size_y, rows), 0, iota((size_y, rows), 1), at_x, size_x)
        planes.append(dot(w, line))
    return planes


def y_kernel(gossip, pairs_x, extra, yf_ref, tab_ref, *refs):
    size_x, size_z = yf_ref.shape[1:]
    x_refs, refs = refs[:pairs_x], refs[pairs_x:]
    extra_refs, refs = refs[:extra], refs[extra:]
    size_y = x_refs[0].shape[0] - (NP if gossip else 0)
    row = iota((size_x, size_z), 0)
    faces = []
    for side, at in ((0, 0), (1, size_y - 1)):
        x_low, x_high = low_high([r[at : at + 1, :] for r in x_refs], "gx")
        face = yf_ref[side]
        faces.append(face + jnp.where(row == 0, x_low, 0.0) + jnp.where(row == size_x - 1, x_high, 0.0))
    for ref, face in zip(refs, pair_payloads(faces[0], faces[1], "gy", 2)):
        ref[0:size_x, :] = face
    if gossip:
        tab = merge(tab_ref[...], x_refs[0][size_y:, :])
        for r in extra_refs:
            tab = merge(tab, r[...])
        refs[0][size_x:, :] = tab
        refs[1][size_x:, :] = tab
        refs[2][...] = tab


def z_kernel(gossip, pairs_x, zf_ref, tab_ref, *refs):
    size_y = zf_ref.shape[1]
    x_refs, y_refs, refs = refs[:pairs_x], refs[pairs_x : pairs_x + 2], refs[pairs_x + 2 :]
    size_x = y_refs[0].shape[0] - (NP if gossip else 0)
    size_z = y_refs[0].shape[1]
    lane = iota((size_y, LANES), 1)
    row = iota((size_y, LANES), 0)
    diagonal = iota((size_x, LANES), 0) == iota((size_x, LANES), 1)
    faces = []
    for side, at in ((0, 0), (1, size_z - 1)):
        x_low, x_high = low_high([r[0:size_y, at : at + 1] for r in x_refs], "gx")
        y_low, y_high = low_high([r[0:size_x, at : at + 1] for r in y_refs], "gy")
        face = zf_ref[side]
        face = face + jnp.where(lane == 0, x_low, 0.0) + jnp.where(lane == size_x - 1, x_high, 0.0)
        for at_y, column in ((0, y_low), (size_y - 1, y_high)):
            line = jnp.sum(jnp.where(diagonal, column, 0.0), axis=0, keepdims=True)
            face = face + jnp.where(row == at_y, line, 0.0)
        faces.append(face)
    for ref, face in zip(refs, pair_payloads(faces[0], faces[1], "gz", 2)):
        ref[0:size_y, :] = face
    if gossip:
        tab = tab_ref[...]
        for r in y_refs:
            tab = merge(tab, r[size_x:, :])
        for ref in refs[:2]:
            ref[size_y : size_y + NP, :] = tab[:, :LANES]
            ref[size_y + NP :, :] = tab[:, LANES:]
        refs[2][...] = tab


def with_halo(plane, x, size_x, x_halo, y_halo, z_halo):
    size_y, size_z = plane.shape
    if x == 0:
        plane = plane + x_halo[0]
    if x == size_x - 1:
        plane = plane + x_halo[1]
    row, lane = iota(plane.shape, 0), iota(plane.shape, 1)
    plane = plane + jnp.where(row == 0, y_halo[0][x : x + 1, :], 0.0)
    plane = plane + jnp.where(row == size_y - 1, y_halo[1][x : x + 1, :], 0.0)
    plane = plane + jnp.where(lane == 0, z_halo[0][:, x : x + 1], 0.0)
    plane = plane + jnp.where(lane == size_z - 1, z_halo[1][:, x : x + 1], 0.0)
    keep = jnp.logical_not(((lane == 0) & (lax.axis_index("gz") == 0)) | ((lane == size_z - 1) & is_last("gz")))
    if x == 0:
        keep = keep & (lax.axis_index("gx") != 0)
    if x == size_x - 1:
        keep = keep & jnp.logical_not(is_last("gx"))
    return jnp.where(keep, plane, 0.0)


def halos(shape, x_refs, y_refs, z_refs):
    size_x, size_y, _ = shape
    x_halo = low_high([r[0:size_y, :] for r in x_refs], "gx")
    y_halo = low_high([r[0:size_x, :] for r in y_refs], "gy")
    z_halo = low_high([r[0:size_y, :] for r in z_refs], "gz")
    return x_halo, y_halo, z_halo


def merged_table(tab_ref, z_refs, size_y):
    tab = tab_ref[...]
    for r in z_refs:
        tab = merge(tab, jnp.concatenate([r[size_y : size_y + NP, :], r[size_y + NP :, :]], axis=1))
    return tab


def prepare_kernel(basis_ref, values_ref, scalar_ref, coef_ref, pz_ref, pzt_ref, py_ref, pyt_ref, inv_ref):
    size_x, size_y, size_z = inv_ref.shape

    def folded(length, transposed):
        pick = (iota((length, NP), 0) % NP == iota((length, NP), 1)).astype(jnp.float32)
        basis = basis_ref[...]
        left = dot(pick, basis, ((1,), (1 if transposed else 0,)))
        wide = dot(left, pick, ((1,), (1,)))
        row, col = iota((length, length), 0), iota((length, length), 1)
        wide = jnp.where(row // NP == col // NP, wide, 0.0)
        dim, at = (1, col) if transposed else (0, row)
        after = pltpu.roll(wide, length - 1, dim)
        before = pltpu.roll(wide, 1, dim)
        wide = wide + jnp.where((at % NP == NP - 1) & (at != length - 1), after, 0.0)
        return wide + jnp.where((at % NP == 0) & (at != 0), before, 0.0)

    pz_ref[...] = folded(size_z, False)
    pzt_ref[...] = folded(size_z, True)
    py_ref[...] = folded(size_y, False)
    pyt_ref[...] = folded(size_y, True)
    spread = (iota((size_z // NP, size_z), 0) == iota((size_z // NP, size_z), 1) // NP).astype(jnp.float32)
    coef = dot(coef_ref[0], spread)
    pick = (iota((NP, size_z), 0) == iota((NP, size_z), 1) % NP).astype(jnp.float32)
    along_z = dot(values_ref[...], pick)
    diagonal = iota((NP, NP), 0) == iota((NP, NP), 1)
    along_y = jnp.sum(jnp.where(diagonal, values_ref[...], 0.0), axis=1, keepdims=True)
    along = along_y + along_z
    for e in range(size_y // NP):
        for a in range(NP):
            inv_ref[a, e * NP : (e + 1) * NP, :] = 1.0 / (coef[e : e + 1, :] * (along + scalar_ref[0, a]) + 1.0)


def solve_kernel(gossip, pairs_x, t_ref, basis_ref, pz_ref, pzt_ref, py_ref, pyt_ref, inv_ref, tab_ref, *refs):
    shape = size_x, size_y, size_z = t_ref.shape
    x_refs, y_refs, z_refs = refs[:pairs_x], refs[pairs_x : pairs_x + 2], refs[pairs_x + 2 : pairs_x + 4]
    y_ref, yf_ref, zf_ref, *outs = refs[pairs_x + 4 :]
    scratch = outs[-1]
    x_halo, y_halo, z_halo = halos(shape, x_refs, y_refs, z_refs)
    for x in range(size_x):
        plane = with_halo(t_ref[x], x, size_x, x_halo, y_halo, z_halo)
        y_ref[x] = dot(pyt_ref[...], plane)
    flat = (size_x * size_y, size_z)
    scratch[...] = dot(y_ref[...].reshape(flat), pz_ref[...]).reshape(shape)
    for e in range(size_y // NP):
        rows = slice(e * NP, (e + 1) * NP)
        r = [scratch[b, rows, :] for b in range(NP)]
        s = []
        for a in range(NP):
            total = basis_ref[0, a] * r[0]
            for b in range(1, NP):
                total = total + basis_ref[b, a] * r[b]
            s.append(total * inv_ref[a, rows, :])
        for a in range(NP):
            total = basis_ref[a, 0] * s[0]
            for b in range(1, NP):
                total = total + basis_ref[a, b] * s[b]
            scratch[a, rows, :] = total
    scratch[...] = dot(scratch[...].reshape(flat), pzt_ref[...]).reshape(shape)
    for x in range(size_x):
        y_ref[x] = dot(py_ref[...], scratch[x])
    store_faces(y_ref, yf_ref, zf_ref)
    for ref, face in zip(outs[:pairs_x], pair_payloads(y_ref[0], y_ref[size_x - 1], "gx", pairs_x)):
        ref[0:size_y, :] = face
    if gossip:
        tab = merged_table(tab_ref, z_refs, size_y)
        outs[pairs_x][...] = tab
        outs[0][size_y:, :] = tab


def final_kernel(gossip, pairs_x, s_ref, tab_ref, *refs):
    shape = size_x, size_y, size_z = s_ref.shape
    x_refs, y_refs, z_refs = refs[:pairs_x], refs[pairs_x : pairs_x + 2], refs[pairs_x + 2 : pairs_x + 4]
    out_ref = refs[-1]
    if gossip:
        coarse = coarse_planes(merged_table(tab_ref, z_refs, size_y), *shape)
    else:
        coarse = [tab_ref[c] for c in range(3)]
    x_halo, y_halo, z_halo = halos(shape, x_refs, y_refs, z_refs)
    for x in range(size_x):
        plane = s_ref[x] + coarse[0 if x == 0 else 2 if x == size_x - 1 else 1]
        out_ref[x] = with_halo(plane, x, size_x, x_halo, y_halo, z_halo)


VMEM = pl.BlockSpec(memory_space=pltpu.VMEM)
SMEM = pl.BlockSpec(memory_space=pltpu.SMEM)


def call(kernel, name, inputs, shapes, scratch=(), smem=()):
    return pl.pallas_call(
        kernel,
        name=name,
        out_shape=[jax.ShapeDtypeStruct(s, jnp.float32) for s in shapes],
        in_specs=[SMEM if n in smem else VMEM for n in range(len(inputs))],
        out_specs=[VMEM] * len(shapes),
        scratch_shapes=[pltpu.VMEM(s, jnp.float32) for s in scratch],
    )(*inputs)


def pair_permutations(sizes, dim):
    count = sizes[dim]
    result = []
    for odd in range(1 if count == 2 and dim != 1 else 2):
        pairs = []
        for place in np.ndindex(*sizes):
            other = list(place)
            step = 1 if place[dim] % 2 == odd else -1
            moved = place[dim] + step
            if dim == 1 or 0 <= moved < count:
                other[dim] = moved % count
            else:
                other[1] = place[1] ^ 1
            pairs.append((int(np.ravel_multi_index(place, sizes)), int(np.ravel_multi_index(other, sizes))))
        result.append(pairs)
    return result


def coarse_by_sums(terms, coarse_inverse):
    shape = terms.shape
    sides = []
    weights = []
    for dim, axis in enumerate(AXES):
        count, at = lax.axis_size(axis), lax.axis_index(axis)
        position = jnp.arange(shape[dim])
        first, last = (False, False) if dim == 1 else (at == 0, at == count - 1)
        weights.append(jnp.stack([coarse_weight(position, shape[dim], first, last, o) for o in (-1, 0, 1)]))
        block = at + jnp.arange(-1, 2)
        block = block % count if dim == 1 else block
        sides.append((block[:, None] == jnp.arange(count)[None, :]).astype(jnp.float32))
    part = jnp.einsum("xyz,ax,by,cz->abc", terms, *weights, precision=HIGHEST) / terms.size
    rhs = jnp.einsum("abc,ai,bj,ck->ijk", part, *sides, precision=HIGHEST)
    rhs = lax.psum(rhs, AXES)
    inverse = lax.all_gather(coarse_inverse, AXES, axis=0, tiled=True)
    value = jnp.dot(inverse, rhs.reshape(-1), precision=HIGHEST).reshape(rhs.shape)
    near = jnp.einsum("ijk,ai,bj,ck->abc", value, *sides, precision=HIGHEST)
    classes = weights[0][:, jnp.array([0, 1, shape[0] - 1])]
    return jnp.einsum("abc,ax,by,cz->xyz", near, classes, weights[1], weights[2], precision=HIGHEST)


def on_device(sizes, fluidity, local_fluidity, element_coef, fdm_basis, fdm_values, coarse_inverse):
    shape = size_x, size_y, size_z = fluidity.shape
    gossip = sizes == (2, 4, 4)
    extra_rows = NP if gossip else 0
    perms = [pair_permutations(sizes, dim) for dim in range(3)]
    pairs_x = len(perms[0])

    const = np.zeros((size_z + size_y + NP, size_z), np.float32)
    const[:size_z] = np.kron(np.eye(size_z // NP), STIFF.T)
    const[size_z : size_z + size_y, :size_y] = np.kron(np.eye(size_y // NP), STIFF)
    const[size_z + size_y :] = WEIGHTS[:, None] * np.tile(WEIGHTS, size_z // NP)[None, :]

    face_shapes = [(2, size_x, size_z), (2, size_y, LANES)]
    x_shapes = [(size_y + extra_rows, size_z)] * pairs_x
    tab_shapes = [(NP, size_z)] if gossip else []

    def send(payloads, pairs):
        return [lax.ppermute(p, AXES, q) for p, q in zip(payloads, pairs)]

    def exchange(y_faces, z_faces, x_payloads, tab, extra):
        x_got = send(x_payloads, perms[0])
        extra_got = send([tab] * len(extra), extra)
        y_out = call(
            functools.partial(y_kernel, gossip, pairs_x, len(extra)),
            "y_faces",
            [y_faces, tab, *x_got, *extra_got],
            [(size_x + extra_rows, size_z)] * 2 + tab_shapes,
        )
        y_got = send(y_out[:2], perms[1])
        tab = y_out[-1] if gossip else tab
        z_out = call(
            functools.partial(z_kernel, gossip, pairs_x),
            "z_faces",
            [z_faces, tab, *x_got, *y_got],
            [(size_y + 2 * extra_rows, LANES)] * 2 + tab_shapes,
        )
        z_got = send(z_out[:2], perms[2])
        tab = z_out[-1] if gossip else tab
        return [*x_got, *y_got, *z_got], tab

    terms, y_faces, z_faces, *rest = call(
        functools.partial(terms_kernel, gossip, pairs_x),
        "terms",
        [fluidity, local_fluidity, element_coef, coarse_inverse, const],
        [shape] + face_shapes + x_shapes + tab_shapes,
    )
    tab = rest[-1]
    extra = [perms[2][0]] if gossip else []
    got, tab = exchange(y_faces, z_faces, rest[:pairs_x], tab, extra)
    values = fdm_values.reshape(1, NP)
    operators = call(
        prepare_kernel,
        "operators",
        [fdm_basis, values, values, element_coef],
        [(size_z, size_z)] * 2 + [(size_y, size_y)] * 2 + [shape],
        smem=(2,),
    )
    solved, y_faces, z_faces, *rest = call(
        functools.partial(solve_kernel, gossip, pairs_x),
        "solve",
        [terms, fdm_basis, *operators, tab, *got],
        [shape] + face_shapes + x_shapes + tab_shapes,
        scratch=[shape],
        smem=(1,),
    )
    got, tab = exchange(y_faces, z_faces, rest[:pairs_x], rest[-1], [])
    coarse = tab if gossip else coarse_by_sums(terms, coarse_inverse)
    return call(
        functools.partial(final_kernel, gossip, pairs_x), "final", [solved, coarse, *got], [shape]
    )[0]


def solution(mesh):
    sizes = tuple(mesh.shape[axis] for axis in AXES)
    return jax.shard_map(
        functools.partial(on_device, sizes),
        mesh=mesh,
        in_specs=(
            P("gx", "gy", "gz"),
            P("gx", "gy", "gz"),
            P("gx", "gy", "gz"),
            P(),
            P(),
            P(("gx", "gy", "gz"), None),
        ),
        out_specs=P("gx", "gy", "gz"),
        check_vma=False,
    )
```

time: 135 us -> 50.4 us (0.37)
  blocking collectives: 39.4 us -> 0 us
  waiting for transfers between devices: 40.9 us -> 11.7 us
  Pallas kernels: 0 us -> 20 us
  local copies, waits for them, and re-layouts: 21 us -> 4.95 us
  other arithmetic: 11.8 us -> 0 us
  matrix products: 7.75 us -> 0 us
    unnamed x1 -> x0, blocking collectives: 39.4 us -> none
    ppermute x12 -> x11, waiting for transfers between devices: 40.9 us -> 11.7 us  [send(): return [lax.ppermute(p, AXES, q) for p, q in zip(payloads, pairs)]]
    pallas_call x0 -> x8, Pallas kernels: none -> 20 us  [call(): pl.pallas_call(kernel, name=name, out_shape=[jax.ShapeDtypeStruct(s, jnp....]
    mul x7 -> x0, local copies, waits for them, and re-layouts: 17.2 us -> none  [the longest x4 16.1 us: apply_matrix(): block_diag = jnp.kron(jnp.eye(size_z // NP, dtype=jnp.float32), matrix.T)]
    dot_general x12 -> x0, matrix products: 7.75 us -> none  [the longest x4 3.49 us: apply_matrix(): return jnp.dot(tensor, block_diag, precision=HIGHEST)]
    mul x6 -> x0, other arithmetic: 7.28 us -> none  [the longest x1 6.72 us: apply_matrix(): block_diag = jnp.kron(jnp.eye(size_z // NP, dtype=jnp.float32), matrix.T)]
    unnamed x24 -> x23, local copies, waits for them, and re-layouts: 1.39 us -> 4.95 us
    concatenate x4 -> x0, other arithmetic: 2.05 us -> none  [extended(): block = jnp.concatenate([low, block, high], axis=dim)]
  transfers between devices with their start and end apart: 12 -> 11, of which waited for: 12 -> 5; matrix products, arithmetic and copies ran while one was open for 6% -> 0% of each run, Pallas kernels for 0% -> 6%
where the time goes in v1:
time: 50.4 us; the launch traced here: 49.9 us
  Pallas kernels  20 us (40%)
  starting transfers between devices  13.3 us (26%)
  waiting for transfers between devices  11.7 us (23%)
  local copies, waits for them, and re-layouts  4.95 us (10%)
    pallas_call x8, Pallas kernels, call(): pl.pallas_call(kernel, name=name, out_shape=[jax.ShapeDtypeStruct(s, jnp....  20 us
    ppermute x11, starting transfers between devices, send(): return [lax.ppermute(p, AXES, q) for p, q in zip(payloads, pairs)]  13.3 us
    ppermute x11, waiting for transfers between devices, send(): return [lax.ppermute(p, AXES, q) for p, q in zip(payloads, pairs)]  11.7 us
    unnamed x23, local copies, waits for them, and re-layouts  4.95 us
  transfers between devices with their start and end apart: 11, of which 5 were waited for; matrix products, arithmetic and copies ran while one was open for 0% of the time, Pallas kernels for 6%

profile of v1, /device:TPU:0, one launch (start us, length us, event | category | flops | bytes accessed | tf_op | source)
XLA Modules:
  0.0 49.9 jit_solution(8677262408595871833)
XLA Ops:
  0.0 1.3 %copy.8.coef_ref = f32[1,6,32]{2,1,0:T(8,128)} copy(f32[1,6,32]{2,0,1:T(1,128)} %param.9) | data formatting | bytes 1536 | tf_op args[2]
  1.3 3.4 %terms.1 = (f32[8,48,256]{2,1,0:T(8,128)}, f32[2,8,256]{2,1,0:T(8,128)}, f32[2,48,128]{2,1,0:T(8,128)}, f32[56,256]{1,0:T(8,128)}, f32[8,256]{1,0:T(8,128)}) custom-call(f32[8,48,256]{2,1,0:T(8,128)} %u_ref.1, f32[8,48,256]{2,1,0:T(8,128)} %l_ref.1, f32[1,6,32]{2,1,0:T(8,128)} %copy.8.coef_ref, f32[1,32]{1,0:T(1,128)} %cinv_ref.1, ...), custom_call_target="tpu_custom_call" | custom-call | tf_op jit(solution)/shard_map/terms/pallas_call | solution.py:382
  4.6 2.9 %collective-permute-start = (f32[56,256]{1,0:T(8,128)}, f32[56,256]{1,0:T(8,128)S(1)}, u32[]{:S(2)}, u32[]{:S(2)}) collective-permute-start(f32[56,256]{1,0:T(8,128)} %get-tuple-element.41), channel_id=1, source_target_pairs={{0,16},{1,17},{2,18},{3,19},{4,20},{5,21},{6,22},{7,23},{8,24},{9,... | collective-permute-start | bytes 172040 | tf_op jit(solution)/shard_map/ppermute | solution.py:449
  7.6 1.6 %collective-permute-start.1 = (f32[8,256]{1,0:T(8,128)}, f32[8,256]{1,0:T(8,128)S(1)}, u32[]{:S(2)}, u32[]{:S(2)}) collective-permute-start(f32[8,256]{1,0:T(8,128)} %get-tuple-element.40.tab_ref), channel_id=1, source_target_pairs={{0,1},{1,0},{2,3},{3,2},{4,5},{5,4},{6,7},{7,6},{8,9},{9,8},{10,11... | collective-permute-start | bytes 24584 | tf_op jit(solution)/shard_map/ppermute | solution.py:449
  9.2 2.3 %collective-permute-done.1.refs_1_ = f32[8,256]{1,0:T(8,128)S(1)} collective-permute-done((f32[8,256]{1,0:T(8,128)}, f32[8,256]{1,0:T(8,128)S(1)}, u32[]{:S(2)}, u32[]{:S(2)}) %collective-permute-start.1) | collective-permute-done | bytes 8224 | tf_op jit(solution)/shard_map/ppermute | solution.py:449
  11.4 0.0 copy-start.10
  11.4 0.0 collective-permute-done.refs_0_
  11.5 0.0 copy-start
  11.5 0.6 %copy-done.10 = f32[8,256]{1,0:T(8,128)} copy-done((f32[8,256]{1,0:T(8,128)}, f32[8,256]{1,0:T(8,128)S(1)}, u32[]{:S(2)}) %copy-start.10) | copy-done | bytes 8216
  12.0 0.0 copy-done
  12.1 1.5 %y_faces.2 = (f32[16,256]{1,0:T(8,128)}, f32[16,256]{1,0:T(8,128)}, f32[8,256]{1,0:T(8,128)}) custom-call(f32[2,8,256]{2,1,0:T(8,128)} %get-tuple-element.39.yf_ref, f32[8,256]{1,0:T(8,128)} %get-tuple-element.40.tab_ref, f32[56,256]{1,0:T(8,128)} %copy-done, f32[8,256]{1,0:T(8,128)} %copy-done.10), custom_call_target="tpu_custom_call" | custom-call | tf_op jit(solution)/shard_map/y_faces/pallas_call | solution.py:382
  13.6 0.0 collective-permute-start.2
  13.6 1.6 %collective-permute-start.3 = (f32[16,256]{1,0:T(8,128)}, f32[16,256]{1,0:T(8,128)S(1)}, u32[]{:S(2)}, u32[]{:S(2)}) collective-permute-start(f32[16,256]{1,0:T(8,128)} %get-tuple-element.44), channel_id=1, source_target_pairs={{0,12},{1,13},{2,14},{3,15},{4,8},{5,9},{6,10},{7,11},{8,4},{9,5},... | collective-permute-start | bytes 49160 | tf_op jit(solution)/shard_map/ppermute | solution.py:449
  15.2 0.0 collective-permute-done.2.refs_1_
  15.2 0.0 copy-start.2
  15.2 1.7 %collective-permute-done.3.refs_2_ = f32[16,256]{1,0:T(8,128)S(1)} collective-permute-done((f32[16,256]{1,0:T(8,128)}, f32[16,256]{1,0:T(8,128)S(1)}, u32[]{:S(2)}, u32[]{:S(2)}) %collective-permute-start.3) | collective-permute-done | bytes 16416 | tf_op jit(solution)/shard_map/ppermute | solution.py:449
  16.9 0.0 copy-start.3
  16.9 0.0 copy-done.2
  16.9 0.6 %copy-done.3 = f32[16,256]{1,0:T(8,128)} copy-done((f32[16,256]{1,0:T(8,128)}, f32[16,256]{1,0:T(8,128)S(1)}, u32[]{:S(2)}) %copy-start.3) | copy-done | bytes 16408
  17.5 1.6 %z_faces.2 = (f32[64,128]{1,0:T(8,128)}, f32[64,128]{1,0:T(8,128)}, f32[8,256]{1,0:T(8,128)}) custom-call(f32[2,48,128]{2,1,0:T(8,128)} %get-tuple-element.38.zf_ref, f32[8,256]{1,0:T(8,128)} %get-tuple-element.42.tab_ref, f32[56,256]{1,0:T(8,128)} %copy-done, f32[16,256]{1,0:T(8,128)} %copy-done.2, f32[16,256]{1,0:T(8,128)} %copy-done.3), custom_call_target="tpu_custom_call" | custom-call | tf_op jit(solution)/shard_map/z_faces/pallas_call | solution.py:382
  19.1 1.6 %collective-permute-start.4 = (f32[64,128]{1,0:T(8,128)}, f32[64,128]{1,0:T(8,128)S(1)}, u32[]{:S(2)}, u32[]{:S(2)}) collective-permute-start(f32[64,128]{1,0:T(8,128)} %get-tuple-element.46), channel_id=1, source_target_pairs={{0,1},{1,0},{2,3},{3,2},{4,5},{5,4},{6,7},{7,6},{8,9},{9,8},{10,11... | collective-permute-start | bytes 98312 | tf_op jit(solution)/shard_map/ppermute | solution.py:449
  20.7 0.2 collective-permute-start.5
  20.9 3.2 %operators.1 = (f32[256,256]{1,0:T(8,128)}, f32[256,256]{1,0:T(8,128)}, f32[48,48]{1,0:T(8,128)}, f32[48,48]{1,0:T(8,128)}, f32[8,48,256]{2,1,0:T(8,128)}) custom-call(f32[8,8]{1,0:T(8,128)} %basis_ref.3, f32[1,8]{1,0:T(1,128)} %bitcast.1, f32[1,8]{1,0:T(1,128)} %bitcast.2, f32[1,6,32]{2,1,0:T(8,128)} %copy.8.coef_ref), custom_call_target="tpu_custom_call" | custom-call | tf_op jit(solution)/shard_map/operators/pallas_call | solution.py:382
  24.1 0.0 collective-permute-done.4.refs_3_
  24.1 0.0 copy-start.6
  24.1 0.0 collective-permute-done.5.refs_4_
  24.1 0.0 copy-start.7
  24.1 0.6 %copy-done.6 = f32[64,128]{1,0:T(8,128)} copy-done((f32[64,128]{1,0:T(8,128)}, f32[64,128]{1,0:T(8,128)S(1)}, u32[]{:S(2)}) %copy-start.6) | copy-done | bytes 32792
  24.7 0.0 copy-done.7
  24.7 4.8 %solve.1 = (f32[8,48,256]{2,1,0:T(8,128)}, f32[2,8,256]{2,1,0:T(8,128)}, f32[2,48,128]{2,1,0:T(8,128)}, f32[56,256]{1,0:T(8,128)}, f32[8,256]{1,0:T(8,128)}) custom-call(f32[8,48,256]{2,1,0:T(8,128)} %get-tuple-element.32.t_ref, f32[8,8]{1,0:T(8,128)} %basis_ref.3, f32[256,256]{1,0:T(8,128)} %get-tuple-element.33.pz_ref, ...), custom_call_target="tpu_custom_call" | custom-call | tf_op jit(solution)/shard_map/solve/pallas_call | solution.py:382
  29.6 0.5 %collective-permute-start.6 = (f32[56,256]{1,0:T(8,128)}, f32[56,256]{1,0:T(8,128)S(1)}, u32[]{:S(2)}, u32[]{:S(2)}) collective-permute-start(f32[56,256]{1,0:T(8,128)} %get-tuple-element.52), channel_id=1, source_target_pairs={{0,16},{1,17},{2,18},{3,19},{4,20},{5,21},{6,22},{7,23},{8,24},{9,... | collective-permute-start | bytes 172040 | tf_op jit(solution)/shard_map/ppermute | solution.py:449
  30.1 3.9 %collective-permute-done.6.refs_0_ = f32[56,256]{1,0:T(8,128)S(1)} collective-permute-done((f32[56,256]{1,0:T(8,128)}, f32[56,256]{1,0:T(8,128)S(1)}, u32[]{:S(2)}, u32[]{:S(2)}) %collective-permute-start.6) | collective-permute-done | bytes 57376 | tf_op jit(solution)/shard_map/ppermute | solution.py:449
  33.9 0.6 %copy-done.1 = f32[56,256]{1,0:T(8,128)} copy-done((f32[56,256]{1,0:T(8,128)}, f32[56,256]{1,0:T(8,128)S(1)}, u32[]{:S(2)}) %copy-start.1) | copy-done | bytes 57368
  34.6 1.5 %y_faces.3 = (f32[16,256]{1,0:T(8,128)}, f32[16,256]{1,0:T(8,128)}, f32[8,256]{1,0:T(8,128)}) custom-call(f32[2,8,256]{2,1,0:T(8,128)} %get-tuple-element.50.yf_ref, f32[8,256]{1,0:T(8,128)} %get-tuple-element.51.tab_ref, f32[56,256]{1,0:T(8,128)} %copy-done.1), custom_call_target="tpu_custom_call" | custom-call | tf_op jit(solution)/shard_map/y_faces/pallas_call | solution.py:382
  36.0 0.0 collective-permute-start.7
  36.0 1.6 %collective-permute-start.8 = (f32[16,256]{1,0:T(8,128)}, f32[16,256]{1,0:T(8,128)S(1)}, u32[]{:S(2)}, u32[]{:S(2)}) collective-permute-start(f32[16,256]{1,0:T(8,128)} %get-tuple-element.55), channel_id=1, source_target_pairs={{0,12},{1,13},{2,14},{3,15},{4,8},{5,9},{6,10},{7,11},{8,4},{9,5},... | collective-permute-start | bytes 49160 | tf_op jit(solution)/shard_map/ppermute | solution.py:449
  37.7 0.0 collective-permute-done.7.refs_1_
  37.7 1.7 %collective-permute-done.8.refs_2_ = f32[16,256]{1,0:T(8,128)S(1)} collective-permute-done((f32[16,256]{1,0:T(8,128)}, f32[16,256]{1,0:T(8,128)S(1)}, u32[]{:S(2)}, u32[]{:S(2)}) %collective-permute-start.8) | collective-permute-done | bytes 16416 | tf_op jit(solution)/shard_map/ppermute | solution.py:449
  39.4 0.0 copy-done.4
  39.4 0.6 %copy-done.5 = f32[16,256]{1,0:T(8,128)} copy-done((f32[16,256]{1,0:T(8,128)}, f32[16,256]{1,0:T(8,128)S(1)}, u32[]{:S(2)}) %copy-start.5) | copy-done | bytes 16408
  40.0 1.6 %z_faces.3 = (f32[64,128]{1,0:T(8,128)}, f32[64,128]{1,0:T(8,128)}, f32[8,256]{1,0:T(8,128)}) custom-call(f32[2,48,128]{2,1,0:T(8,128)} %get-tuple-element.49.zf_ref, f32[8,256]{1,0:T(8,128)} %get-tuple-element.53.tab_ref, f32[56,256]{1,0:T(8,128)} %copy-done.1, f32[16,256]{1,0:T(8,128)} %copy-done.4, f32[16,256]{1,0:T(8,128)} %copy-done.5), custom_call_target="tpu_custom_call" | custom-call | tf_op jit(solution)/shard_map/z_faces/pallas_call | solution.py:382
  41.6 2.9 %collective-permute-start.9 = (f32[64,128]{1,0:T(8,128)}, f32[64,128]{1,0:T(8,128)S(1)}, u32[]{:S(2)}, u32[]{:S(2)}) collective-permute-start(f32[64,128]{1,0:T(8,128)} %get-tuple-element.57), channel_id=1, source_target_pairs={{0,1},{1,0},{2,3},{3,2},{4,5},{5,4},{6,7},{7,6},{8,9},{9,8},{10,11... | collective-permute-start | bytes 98312 | tf_op jit(solution)/shard_map/ppermute | solution.py:449
  44.5 0.2 collective-permute-start.10
  44.8 2.0 %collective-permute-done.9.refs_3_ = f32[64,128]{1,0:T(8,128)S(1)} collective-permute-done((f32[64,128]{1,0:T(8,128)}, f32[64,128]{1,0:T(8,128)S(1)}, u32[]{:S(2)}, u32[]{:S(2)}) %collective-permute-start.9) | collective-permute-done | bytes 32800 | tf_op jit(solution)/shard_map/ppermute | solution.py:449
  46.8 0.0 collective-permute-done.10.refs_4_
  46.8 0.6 %copy-done.8 = f32[64,128]{1,0:T(8,128)} copy-done((f32[64,128]{1,0:T(8,128)}, f32[64,128]{1,0:T(8,128)S(1)}, u32[]{:S(2)}) %copy-start.8) | copy-done | bytes 32792
  47.4 0.0 copy-done.9
  47.4 2.5 %final.1 = f32[8,48,256]{2,1,0:T(8,128)} custom-call(f32[8,48,256]{2,1,0:T(8,128)} %get-tuple-element.48.s_ref, f32[8,256]{1,0:T(8,128)} %get-tuple-element.56.tab_ref, f32[56,256]{1,0:T(8,128)} %copy-done.1, f32[16,256]{1,0:T(8,128)} %copy-done.4, f32[16,256]{1,0:T(8,128)} %copy-done.5, f32[64,128]{1,0:T(8,128)} %copy-done.8, f32[64,128]{1,0:T(8,128)} %copy-done.9), custom_call_target="tpu_custom_call" | custom-call | tf_op jit(solution)/shard_map/final/pallas_call | solution.py:382
  (5 shorter events, 0.0 us)
Async XLA Ops:
  4.6 6.8 %collective-permute-start = (f32[56,256]{1,0:T(8,128)}, f32[56,256]{1,0:T(8,128)S(1)}, u32[]{:S(2)}, u32[]{:S(2)}) collective-permute-start(f32[56,256]{1,0:T(8,128)} %get-tuple-element.41), channel_id=1, source_target_pairs={{0,16},{1,17},{2,18},{3,19},{4,20},{5,21},{6,22},{7,23},{8,24},{9,... | collective-permute-start | bytes 172040 | tf_op jit(solution)/shard_map/ppermute | solution.py:449
  7.6 3.9 %collective-permute-start.1 = (f32[8,256]{1,0:T(8,128)}, f32[8,256]{1,0:T(8,128)S(1)}, u32[]{:S(2)}, u32[]{:S(2)}) collective-permute-start(f32[8,256]{1,0:T(8,128)} %get-tuple-element.40.tab_ref), channel_id=1, source_target_pairs={{0,1},{1,0},{2,3},{3,2},{4,5},{5,4},{6,7},{7,6},{8,9},{9,8},{10,11... | collective-permute-start | bytes 24584 | tf_op jit(solution)/shard_map/ppermute | solution.py:449
  11.4 0.6 %copy-start.10 = (f32[8,256]{1,0:T(8,128)}, f32[8,256]{1,0:T(8,128)S(1)}, u32[]{:S(2)}) copy-start(f32[8,256]{1,0:T(8,128)S(1)} %collective-permute-done.1.refs_1_) | copy-start | bytes 24580
  11.5 0.6 %copy-start = (f32[56,256]{1,0:T(8,128)}, f32[56,256]{1,0:T(8,128)S(1)}, u32[]{:S(2)}) copy-start(f32[56,256]{1,0:T(8,128)S(1)} %collective-permute-done.refs_0_) | copy-start | bytes 172036
  13.6 1.6 %collective-permute-start.2 = (f32[16,256]{1,0:T(8,128)}, f32[16,256]{1,0:T(8,128)S(1)}, u32[]{:S(2)}, u32[]{:S(2)}) collective-permute-start(f32[16,256]{1,0:T(8,128)} %get-tuple-element.43), channel_id=1, source_target_pairs={{0,4},{1,5},{2,6},{3,7},{4,0},{5,1},{6,2},{7,3},{8,12},{9,13},{10,... | collective-permute-start | bytes 49160 | tf_op jit(solution)/shard_map/ppermute | solution.py:449
  13.6 3.4 %collective-permute-start.3 = (f32[16,256]{1,0:T(8,128)}, f32[16,256]{1,0:T(8,128)S(1)}, u32[]{:S(2)}, u32[]{:S(2)}) collective-permute-start(f32[16,256]{1,0:T(8,128)} %get-tuple-element.44), channel_id=1, source_target_pairs={{0,12},{1,13},{2,14},{3,15},{4,8},{5,9},{6,10},{7,11},{8,4},{9,5},... | collective-permute-start | bytes 49160 | tf_op jit(solution)/shard_map/ppermute | solution.py:449
  15.2 1.7 %copy-start.2 = (f32[16,256]{1,0:T(8,128)}, f32[16,256]{1,0:T(8,128)S(1)}, u32[]{:S(2)}) copy-start(f32[16,256]{1,0:T(8,128)S(1)} %collective-permute-done.2.refs_1_) | copy-start | bytes 49156
  16.9 0.6 %copy-start.3 = (f32[16,256]{1,0:T(8,128)}, f32[16,256]{1,0:T(8,128)S(1)}, u32[]{:S(2)}) copy-start(f32[16,256]{1,0:T(8,128)S(1)} %collective-permute-done.3.refs_2_) | copy-start | bytes 49156
  19.1 5.0 %collective-permute-start.4 = (f32[64,128]{1,0:T(8,128)}, f32[64,128]{1,0:T(8,128)S(1)}, u32[]{:S(2)}, u32[]{:S(2)}) collective-permute-start(f32[64,128]{1,0:T(8,128)} %get-tuple-element.46), channel_id=1, source_target_pairs={{0,1},{1,0},{2,3},{3,2},{4,5},{5,4},{6,7},{7,6},{8,9},{9,8},{10,11... | collective-permute-start | bytes 98312 | tf_op jit(solution)/shard_map/ppermute | solution.py:449
  20.7 3.4 %collective-permute-start.5 = (f32[64,128]{1,0:T(8,128)}, f32[64,128]{1,0:T(8,128)S(1)}, u32[]{:S(2)}, u32[]{:S(2)}) collective-permute-start(f32[64,128]{1,0:T(8,128)} %get-tuple-element.47), channel_id=1, source_target_pairs={{0,4},{1,2},{2,1},{3,7},{4,0},{5,6},{6,5},{7,3},{8,12},{9,10},{10,... | collective-permute-start | bytes 98312 | tf_op jit(solution)/shard_map/ppermute | solution.py:449
  24.1 0.6 %copy-start.6 = (f32[64,128]{1,0:T(8,128)}, f32[64,128]{1,0:T(8,128)S(1)}, u32[]{:S(2)}) copy-start(f32[64,128]{1,0:T(8,128)S(1)} %collective-permute-done.4.refs_3_) | copy-start | bytes 98308
  24.1 0.6 %copy-start.7 = (f32[64,128]{1,0:T(8,128)}, f32[64,128]{1,0:T(8,128)S(1)}, u32[]{:S(2)}) copy-start(f32[64,128]{1,0:T(8,128)S(1)} %collective-permute-done.5.refs_4_) | copy-start | bytes 98308
  29.6 4.4 %collective-permute-start.6 = (f32[56,256]{1,0:T(8,128)}, f32[56,256]{1,0:T(8,128)S(1)}, u32[]{:S(2)}, u32[]{:S(2)}) collective-permute-start(f32[56,256]{1,0:T(8,128)} %get-tuple-element.52), channel_id=1, source_target_pairs={{0,16},{1,17},{2,18},{3,19},{4,20},{5,21},{6,22},{7,23},{8,24},{9,... | collective-permute-start | bytes 172040 | tf_op jit(solution)/shard_map/ppermute | solution.py:449
  33.9 0.6 %copy-start.1 = (f32[56,256]{1,0:T(8,128)}, f32[56,256]{1,0:T(8,128)S(1)}, u32[]{:S(2)}) copy-start(f32[56,256]{1,0:T(8,128)S(1)} %collective-permute-done.6.refs_0_) | copy-start | bytes 172036
  36.0 1.6 %collective-permute-start.7 = (f32[16,256]{1,0:T(8,128)}, f32[16,256]{1,0:T(8,128)S(1)}, u32[]{:S(2)}, u32[]{:S(2)}) collective-permute-start(f32[16,256]{1,0:T(8,128)} %get-tuple-element.54), channel_id=1, source_target_pairs={{0,4},{1,5},{2,6},{3,7},{4,0},{5,1},{6,2},{7,3},{8,12},{9,13},{10,... | collective-permute-start | bytes 49160 | tf_op jit(solution)/shard_map/ppermute | solution.py:449
  36.0 3.4 %collective-permute-start.8 = (f32[16,256]{1,0:T(8,128)}, f32[16,256]{1,0:T(8,128)S(1)}, u32[]{:S(2)}, u32[]{:S(2)}) collective-permute-start(f32[16,256]{1,0:T(8,128)} %get-tuple-element.55), channel_id=1, source_target_pairs={{0,12},{1,13},{2,14},{3,15},{4,8},{5,9},{6,10},{7,11},{8,4},{9,5},... | collective-permute-start | bytes 49160 | tf_op jit(solution)/shard_map/ppermute | solution.py:449
  37.7 1.8 %copy-start.4 = (f32[16,256]{1,0:T(8,128)}, f32[16,256]{1,0:T(8,128)S(1)}, u32[]{:S(2)}) copy-start(f32[16,256]{1,0:T(8,128)S(1)} %collective-permute-done.7.refs_1_) | copy-start | bytes 49156
  39.4 0.6 %copy-start.5 = (f32[16,256]{1,0:T(8,128)}, f32[16,256]{1,0:T(8,128)S(1)}, u32[]{:S(2)}) copy-start(f32[16,256]{1,0:T(8,128)S(1)} %collective-permute-done.8.refs_2_) | copy-start | bytes 49156
  41.6 5.2 %collective-permute-start.9 = (f32[64,128]{1,0:T(8,128)}, f32[64,128]{1,0:T(8,128)S(1)}, u32[]{:S(2)}, u32[]{:S(2)}) collective-permute-start(f32[64,128]{1,0:T(8,128)} %get-tuple-element.57), channel_id=1, source_target_pairs={{0,1},{1,0},{2,3},{3,2},{4,5},{5,4},{6,7},{7,6},{8,9},{9,8},{10,11... | collective-permute-start | bytes 98312 | tf_op jit(solution)/shard_map/ppermute | solution.py:449
  44.5 2.3 %collective-permute-start.10 = (f32[64,128]{1,0:T(8,128)}, f32[64,128]{1,0:T(8,128)S(1)}, u32[]{:S(2)}, u32[]{:S(2)}) collective-permute-start(f32[64,128]{1,0:T(8,128)} %get-tuple-element.58), channel_id=1, source_target_pairs={{0,4},{1,2},{2,1},{3,7},{4,0},{5,6},{6,5},{7,3},{8,12},{9,10},{10,... | collective-permute-start | bytes 98312 | tf_op jit(solution)/shard_map/ppermute | solution.py:449
  46.8 0.6 %copy-start.8 = (f32[64,128]{1,0:T(8,128)}, f32[64,128]{1,0:T(8,128)S(1)}, u32[]{:S(2)}) copy-start(f32[64,128]{1,0:T(8,128)S(1)} %collective-permute-done.9.refs_3_) | copy-start | bytes 98308
  46.8 0.6 %copy-start.9 = (f32[64,128]{1,0:T(8,128)}, f32[64,128]{1,0:T(8,128)S(1)}, u32[]{:S(2)}) copy-start(f32[64,128]{1,0:T(8,128)S(1)} %collective-permute-done.10.refs_4_) | copy-start | bytes 98308

commit v2 on v1

--- a/solution.py
+++ b/solution.py
@@ -386,6 +386,7 @@
         in_specs=[SMEM if n in smem else VMEM for n in range(len(inputs))],
         out_specs=[VMEM] * len(shapes),
         scratch_shapes=[pltpu.VMEM(s, jnp.float32) for s in scratch],
+        compiler_params=pltpu.CompilerParams(vmem_limit_bytes=8 << 20),
     )(*inputs)
 
 

time: 50.4 us -> 37 us (0.73)
  Pallas kernels: 20 us -> 8.61 us
  waiting for transfers between devices: 11.7 us -> 10.7 us
  local copies, waits for them, and re-layouts: 4.95 us -> 4.15 us
    pallas_call x8, Pallas kernels: 20 us -> 8.61 us  [call(): pl.pallas_call(kernel, name=name, out_shape=[jax.ShapeDtypeStruct(s, jnp....]
    ppermute x11, waiting for transfers between devices: 11.7 us -> 10.7 us  [send(): return [lax.ppermute(p, AXES, q) for p, q in zip(payloads, pairs)]]
    unnamed x23 -> x13, local copies, waits for them, and re-layouts: 4.95 us -> 4.15 us
where the time goes in v2:
time: 37 us; the launch traced here: 36.7 us
  starting transfers between devices  13.1 us (35%)
  waiting for transfers between devices  10.7 us (29%)
  Pallas kernels  8.61 us (23%)
  local copies, waits for them, and re-layouts  4.15 us (11%)
    ppermute x11, starting transfers between devices, send(): return [lax.ppermute(p, AXES, q) for p, q in zip(payloads, pairs)]  13.1 us
    ppermute x11, waiting for transfers between devices, send(): return [lax.ppermute(p, AXES, q) for p, q in zip(payloads, pairs)]  10.7 us
    pallas_call x8, Pallas kernels, call(): pl.pallas_call(kernel, name=name, out_shape=[jax.ShapeDtypeStruct(s, jnp....  8.61 us
    unnamed x13, local copies, waits for them, and re-layouts  4.15 us
  transfers between devices with their start and end apart: 11, of which 5 were waited for; matrix products, arithmetic and copies ran while one was open for 0% of the time, Pallas kernels for 6%

profile of v2, /device:TPU:0, one launch (start us, length us, event | category | flops | bytes accessed | tf_op | source)
XLA Modules:
  0.0 36.7 jit_solution(9256967357624962955)
XLA Ops:
  0.0 0.0 copy-start.5
  0.0 0.7 %copy.8.coef_ref = f32[1,6,32]{2,1,0:T(8,128)S(1)} copy(f32[1,6,32]{2,0,1:T(1,128)} %param.9) | data formatting | bytes 1536 | tf_op args[2]
  0.7 0.0 copy-done.5
  0.7 0.0 copy-start
  0.7 1.0 %copy-done = f32[8,48,256]{2,1,0:T(8,128)S(1)} copy-done((f32[8,48,256]{2,1,0:T(8,128)S(1)}, f32[8,48,256]{2,1,0:T(8,128)}, u32[]{:S(2)}) %copy-start) | copy-done | bytes 393240
  1.7 0.0 copy-start.1
  1.7 1.0 %copy-done.1 = f32[8,48,256]{2,1,0:T(8,128)S(1)} copy-done((f32[8,48,256]{2,1,0:T(8,128)S(1)}, f32[8,48,256]{2,1,0:T(8,128)}, u32[]{:S(2)}) %copy-start.1) | copy-done | bytes 393240
  2.7 0.0 copy-start.2
  2.7 1.0 %copy-done.2 = f32[312,256]{1,0:T(8,128)S(1)} copy-done((f32[312,256]{1,0:T(8,128)S(1)}, f32[312,256]{1,0:T(8,128)}, u32[]{:S(2)}) %copy-start.2) | copy-done | bytes 319512
  3.7 1.5 %terms.1 = (f32[8,48,256]{2,1,0:T(8,128)S(1)}, f32[2,8,256]{2,1,0:T(8,128)S(1)}, f32[2,48,128]{2,1,0:T(8,128)S(1)}, f32[56,256]{1,0:T(8,128)S(1)}, f32[8,256]{1,0:T(8,128)S(1)}) custom-call(f32[8,48,256]{2,1,0:T(8,128)S(1)} %copy-done, f32[8,48,256]{2,1,0:T(8,128)S(1)} %copy-done.1, f32[1,6,32]{2,1,0:T(8,128)S(1)} %copy.8.coef_ref, f32[1,32]{1,0:T(1,128)S(1)} %copy-done.5, ...), custom_call_target="tpu_custom_call" | custom-call | tf_op jit(solution)/shard_map/terms/pallas_call | solution.py:382
  5.2 3.0 %collective-permute-start = (f32[56,256]{1,0:T(8,128)S(1)}, f32[56,256]{1,0:T(8,128)S(1)}, u32[]{:S(2)}, u32[]{:S(2)}) collective-permute-start(f32[56,256]{1,0:T(8,128)S(1)} %get-tuple-element.41), channel_id=1, source_target_pairs={{0,16},{1,17},{2,18},{3,19},{4,20},{5,21},{6,22},{7,23},{8,24},{9,... | collective-permute-start | bytes 172040 | tf_op jit(solution)/shard_map/ppermute | solution.py:450
  8.2 1.6 %collective-permute-start.1 = (f32[8,256]{1,0:T(8,128)S(1)}, f32[8,256]{1,0:T(8,128)S(1)}, u32[]{:S(2)}, u32[]{:S(2)}) collective-permute-start(f32[8,256]{1,0:T(8,128)S(1)} %get-tuple-element.40.tab_ref), channel_id=1, source_target_pairs={{0,1},{1,0},{2,3},{3,2},{4,5},{5,4},{6,7},{7,6},{8,9},{9,8},{10,11... | collective-permute-start | bytes 24584 | tf_op jit(solution)/shard_map/ppermute | solution.py:450
  9.8 2.1 %collective-permute-done.1.refs_1_ = f32[8,256]{1,0:T(8,128)S(1)} collective-permute-done((f32[8,256]{1,0:T(8,128)S(1)}, f32[8,256]{1,0:T(8,128)S(1)}, u32[]{:S(2)}, u32[]{:S(2)}) %collective-permute-start.1) | collective-permute-done | bytes 8224 | tf_op jit(solution)/shard_map/ppermute | solution.py:450
  11.8 0.0 collective-permute-done.refs_0_
  11.9 0.1 collective-permute-start.2
  11.9 1.6 %collective-permute-start.3 = (f32[16,256]{1,0:T(8,128)S(1)}, f32[16,256]{1,0:T(8,128)S(1)}, u32[]{:S(2)}, u32[]{:S(2)}) collective-permute-start(f32[16,256]{1,0:T(8,128)S(1)} %get-tuple-element.44), channel_id=1, source_target_pairs={{0,12},{1,13},{2,14},{3,15},{4,8},{5,9},{6,10},{7,11},{8,4},{9,5},... | collective-permute-start | bytes 49160 | tf_op jit(solution)/shard_map/ppermute | solution.py:450
  13.6 0.0 collective-permute-done.2.refs_1_
  13.6 1.6 %collective-permute-done.3.refs_2_ = f32[16,256]{1,0:T(8,128)S(1)} collective-permute-done((f32[16,256]{1,0:T(8,128)S(1)}, f32[16,256]{1,0:T(8,128)S(1)}, u32[]{:S(2)}, u32[]{:S(2)}) %collective-permute-start.3) | collective-permute-done | bytes 16416 | tf_op jit(solution)/shard_map/ppermute | solution.py:450
  15.2 0.1 z_faces.2
  15.3 0.0 copy-start.3
  15.3 1.6 %collective-permute-start.4 = (f32[64,128]{1,0:T(8,128)S(1)}, f32[64,128]{1,0:T(8,128)S(1)}, u32[]{:S(2)}, u32[]{:S(2)}) collective-permute-start(f32[64,128]{1,0:T(8,128)S(1)} %get-tuple-element.46), channel_id=1, source_target_pairs={{0,1},{1,0},{2,3},{3,2},{4,5},{5,4},{6,7},{7,6},{8,9},{9,8},{10,11... | collective-permute-start | bytes 98312 | tf_op jit(solution)/shard_map/ppermute | solution.py:450
  16.9 0.0 copy-start.4
  16.9 0.2 collective-permute-start.5
  17.1 0.0 copy-done.3
  17.1 0.5 %copy-done.4 = f32[8]{0:T(128)S(1)} copy-done((f32[8]{0:T(128)S(1)}, f32[8]{0:T(128)}, u32[]{:S(2)}) %copy-start.4) | copy-done | bytes 56
  17.6 2.1 %operators.1 = (f32[256,256]{1,0:T(8,128)S(1)}, f32[256,256]{1,0:T(8,128)S(1)}, f32[48,48]{1,0:T(8,128)S(1)}, f32[48,48]{1,0:T(8,128)S(1)}, f32[8,48,256]{2,1,0:T(8,128)S(1)}) custom-call(f32[8,8]{1,0:T(8,128)S(1)} %copy-done.3, f32[1,8]{1,0:T(1,128)S(1)} %bitcast.1, f32[1,8]{1,0:T(1,128)S(1)} %bitcast.2, f32[1,6,32]{2,1,0:T(8,128)S(1)} %copy.8.coef_ref), custom_call_target="tpu_custom_call" | custom-call | tf_op jit(solution)/shard_map/operators/pallas_call | solution.py:382
  19.7 0.0 collective-permute-done.4.refs_3_
  19.7 0.0 collective-permute-done.5.refs_4_
  19.7 3.4 %solve.1 = (f32[8,48,256]{2,1,0:T(8,128)S(1)}, f32[2,8,256]{2,1,0:T(8,128)S(1)}, f32[2,48,128]{2,1,0:T(8,128)S(1)}, f32[56,256]{1,0:T(8,128)S(1)}, f32[8,256]{1,0:T(8,128)S(1)}) custom-call(f32[8,48,256]{2,1,0:T(8,128)S(1)} %get-tuple-element.32.t_ref, f32[8,8]{1,0:T(8,128)S(1)} %copy-done.3, f32[256,256]{1,0:T(8,128)S(1)} %get-tuple-element.33.pz_ref, ...), custom_call_target="tpu_custom_call" | custom-call | tf_op jit(solution)/shard_map/solve/pallas_call | solution.py:382
  23.0 0.6 %collective-permute-start.6 = (f32[56,256]{1,0:T(8,128)S(1)}, f32[56,256]{1,0:T(8,128)S(1)}, u32[]{:S(2)}, u32[]{:S(2)}) collective-permute-start(f32[56,256]{1,0:T(8,128)S(1)} %get-tuple-element.52), channel_id=1, source_target_pairs={{0,16},{1,17},{2,18},{3,19},{4,20},{5,21},{6,22},{7,23},{8,24},{9,... | collective-permute-start | bytes 172040 | tf_op jit(solution)/shard_map/ppermute | solution.py:450
  23.6 3.6 %collective-permute-done.6.refs_0_ = f32[56,256]{1,0:T(8,128)S(1)} collective-permute-done((f32[56,256]{1,0:T(8,128)S(1)}, f32[56,256]{1,0:T(8,128)S(1)}, u32[]{:S(2)}, u32[]{:S(2)}) %collective-permute-start.6) | collective-permute-done | bytes 57376 | tf_op jit(solution)/shard_map/ppermute | solution.py:450
  27.3 0.1 collective-permute-start.7
  27.4 1.6 %collective-permute-start.8 = (f32[16,256]{1,0:T(8,128)S(1)}, f32[16,256]{1,0:T(8,128)S(1)}, u32[]{:S(2)}, u32[]{:S(2)}) collective-permute-start(f32[16,256]{1,0:T(8,128)S(1)} %get-tuple-element.55), channel_id=1, source_target_pairs={{0,12},{1,13},{2,14},{3,15},{4,8},{5,9},{6,10},{7,11},{8,4},{9,5},... | collective-permute-start | bytes 49160 | tf_op jit(solution)/shard_map/ppermute | solution.py:450
  29.0 0.0 collective-permute-done.7.refs_1_
  29.0 1.6 %collective-permute-done.8.refs_2_ = f32[16,256]{1,0:T(8,128)S(1)} collective-permute-done((f32[16,256]{1,0:T(8,128)S(1)}, f32[16,256]{1,0:T(8,128)S(1)}, u32[]{:S(2)}, u32[]{:S(2)}) %collective-permute-start.8) | collective-permute-done | bytes 16416 | tf_op jit(solution)/shard_map/ppermute | solution.py:450
  30.6 0.1 z_faces.3
  30.7 2.6 %collective-permute-start.9 = (f32[64,128]{1,0:T(8,128)S(1)}, f32[64,128]{1,0:T(8,128)S(1)}, u32[]{:S(2)}, u32[]{:S(2)}) collective-permute-start(f32[64,128]{1,0:T(8,128)S(1)} %get-tuple-element.57), channel_id=1, source_target_pairs={{0,1},{1,0},{2,3},{3,2},{4,5},{5,4},{6,7},{7,6},{8,9},{9,8},{10,11... | collective-permute-start | bytes 98312 | tf_op jit(solution)/shard_map/ppermute | solution.py:450
  33.3 0.2 collective-permute-start.10
  33.4 1.8 %collective-permute-done.9.refs_3_ = f32[64,128]{1,0:T(8,128)S(1)} collective-permute-done((f32[64,128]{1,0:T(8,128)S(1)}, f32[64,128]{1,0:T(8,128)S(1)}, u32[]{:S(2)}, u32[]{:S(2)}) %collective-permute-start.9) | collective-permute-done | bytes 32800 | tf_op jit(solution)/shard_map/ppermute | solution.py:450
  35.3 0.0 collective-permute-done.10.refs_4_
  35.3 1.4 %final.1 = f32[8,48,256]{2,1,0:T(8,128)} custom-call(f32[8,48,256]{2,1,0:T(8,128)S(1)} %get-tuple-element.48.s_ref, f32[8,256]{1,0:T(8,128)S(1)} %get-tuple-element.56.tab_ref, f32[56,256]{1,0:T(8,128)S(1)} %collective-permute-done.6.refs_0_, f32[16,256]{1,0:T(8,128)S(1)} %collective-permute-done.7.refs_1_, f32[16,256]{1,0:T(8,128)S(1)} %collective-permute-done.8.refs_2_, ...), custom_call_target="tpu_custom_call" | custom-call | tf_op jit(solution)/shard_map/final/pallas_call | solution.py:382
  (2 shorter events, 0.0 us)
Async XLA Ops:
  0.0 0.7 %copy-start.5 = (f32[1,32]{1,0:T(1,128)S(1)}, f32[1,32]{1,0:T(1,128)}, u32[]{:S(2)}) copy-start(f32[1,32]{1,0:T(1,128)} %cinv_ref.1) | copy-start | bytes 388
  0.7 1.0 %copy-start = (f32[8,48,256]{2,1,0:T(8,128)S(1)}, f32[8,48,256]{2,1,0:T(8,128)}, u32[]{:S(2)}) copy-start(f32[8,48,256]{2,1,0:T(8,128)} %u_ref.1) | copy-start | bytes 1179652
  1.7 1.0 %copy-start.1 = (f32[8,48,256]{2,1,0:T(8,128)S(1)}, f32[8,48,256]{2,1,0:T(8,128)}, u32[]{:S(2)}) copy-start(f32[8,48,256]{2,1,0:T(8,128)} %l_ref.1) | copy-start | bytes 1179652
  2.7 1.0 %copy-start.2 = (f32[312,256]{1,0:T(8,128)S(1)}, f32[312,256]{1,0:T(8,128)}, u32[]{:S(2)}) copy-start(f32[312,256]{1,0:T(8,128)} %constant.2.clone.const_ref) | copy-start | bytes 958468
  5.2 6.6 %collective-permute-start = (f32[56,256]{1,0:T(8,128)S(1)}, f32[56,256]{1,0:T(8,128)S(1)}, u32[]{:S(2)}, u32[]{:S(2)}) collective-permute-start(f32[56,256]{1,0:T(8,128)S(1)} %get-tuple-element.41), channel_id=1, source_target_pairs={{0,16},{1,17},{2,18},{3,19},{4,20},{5,21},{6,22},{7,23},{8,24},{9,... | collective-permute-start | bytes 172040 | tf_op jit(solution)/shard_map/ppermute | solution.py:450
  8.2 3.7 %collective-permute-start.1 = (f32[8,256]{1,0:T(8,128)S(1)}, f32[8,256]{1,0:T(8,128)S(1)}, u32[]{:S(2)}, u32[]{:S(2)}) collective-permute-start(f32[8,256]{1,0:T(8,128)S(1)} %get-tuple-element.40.tab_ref), channel_id=1, source_target_pairs={{0,1},{1,0},{2,3},{3,2},{4,5},{5,4},{6,7},{7,6},{8,9},{9,8},{10,11... | collective-permute-start | bytes 24584 | tf_op jit(solution)/shard_map/ppermute | solution.py:450
  11.9 1.7 %collective-permute-start.2 = (f32[16,256]{1,0:T(8,128)S(1)}, f32[16,256]{1,0:T(8,128)S(1)}, u32[]{:S(2)}, u32[]{:S(2)}) collective-permute-start(f32[16,256]{1,0:T(8,128)S(1)} %get-tuple-element.43), channel_id=1, source_target_pairs={{0,4},{1,5},{2,6},{3,7},{4,0},{5,1},{6,2},{7,3},{8,12},{9,13},{10,... | collective-permute-start | bytes 49160 | tf_op jit(solution)/shard_map/ppermute | solution.py:450
  11.9 3.2 %collective-permute-start.3 = (f32[16,256]{1,0:T(8,128)S(1)}, f32[16,256]{1,0:T(8,128)S(1)}, u32[]{:S(2)}, u32[]{:S(2)}) collective-permute-start(f32[16,256]{1,0:T(8,128)S(1)} %get-tuple-element.44), channel_id=1, source_target_pairs={{0,12},{1,13},{2,14},{3,15},{4,8},{5,9},{6,10},{7,11},{8,4},{9,5},... | collective-permute-start | bytes 49160 | tf_op jit(solution)/shard_map/ppermute | solution.py:450
  15.3 1.8 %copy-start.3 = (f32[8,8]{1,0:T(8,128)S(1)}, f32[8,8]{1,0:T(8,128)}, u32[]{:S(2)}) copy-start(f32[8,8]{1,0:T(8,128)} %basis_ref.3) | copy-start | bytes 772
  15.3 4.4 %collective-permute-start.4 = (f32[64,128]{1,0:T(8,128)S(1)}, f32[64,128]{1,0:T(8,128)S(1)}, u32[]{:S(2)}, u32[]{:S(2)}) collective-permute-start(f32[64,128]{1,0:T(8,128)S(1)} %get-tuple-element.46), channel_id=1, source_target_pairs={{0,1},{1,0},{2,3},{3,2},{4,5},{5,4},{6,7},{7,6},{8,9},{9,8},{10,11... | collective-permute-start | bytes 98312 | tf_op jit(solution)/shard_map/ppermute | solution.py:450
  16.9 0.7 %copy-start.4 = (f32[8]{0:T(128)S(1)}, f32[8]{0:T(128)}, u32[]{:S(2)}) copy-start(f32[8]{0:T(128)} %param.11) | copy-start | bytes 100
  16.9 2.8 %collective-permute-start.5 = (f32[64,128]{1,0:T(8,128)S(1)}, f32[64,128]{1,0:T(8,128)S(1)}, u32[]{:S(2)}, u32[]{:S(2)}) collective-permute-start(f32[64,128]{1,0:T(8,128)S(1)} %get-tuple-element.47), channel_id=1, source_target_pairs={{0,4},{1,2},{2,1},{3,7},{4,0},{5,6},{6,5},{7,3},{8,12},{9,10},{10,... | collective-permute-start | bytes 98312 | tf_op jit(solution)/shard_map/ppermute | solution.py:450
  23.0 4.2 %collective-permute-start.6 = (f32[56,256]{1,0:T(8,128)S(1)}, f32[56,256]{1,0:T(8,128)S(1)}, u32[]{:S(2)}, u32[]{:S(2)}) collective-permute-start(f32[56,256]{1,0:T(8,128)S(1)} %get-tuple-element.52), channel_id=1, source_target_pairs={{0,16},{1,17},{2,18},{3,19},{4,20},{5,21},{6,22},{7,23},{8,24},{9,... | collective-permute-start | bytes 172040 | tf_op jit(solution)/shard_map/ppermute | solution.py:450
  27.3 1.7 %collective-permute-start.7 = (f32[16,256]{1,0:T(8,128)S(1)}, f32[16,256]{1,0:T(8,128)S(1)}, u32[]{:S(2)}, u32[]{:S(2)}) collective-permute-start(f32[16,256]{1,0:T(8,128)S(1)} %get-tuple-element.54), channel_id=1, source_target_pairs={{0,4},{1,5},{2,6},{3,7},{4,0},{5,1},{6,2},{7,3},{8,12},{9,13},{10,... | collective-permute-start | bytes 49160 | tf_op jit(solution)/shard_map/ppermute | solution.py:450
  27.4 3.2 %collective-permute-start.8 = (f32[16,256]{1,0:T(8,128)S(1)}, f32[16,256]{1,0:T(8,128)S(1)}, u32[]{:S(2)}, u32[]{:S(2)}) collective-permute-start(f32[16,256]{1,0:T(8,128)S(1)} %get-tuple-element.55), channel_id=1, source_target_pairs={{0,12},{1,13},{2,14},{3,15},{4,8},{5,9},{6,10},{7,11},{8,4},{9,5},... | collective-permute-start | bytes 49160 | tf_op jit(solution)/shard_map/ppermute | solution.py:450
  30.7 4.6 %collective-permute-start.9 = (f32[64,128]{1,0:T(8,128)S(1)}, f32[64,128]{1,0:T(8,128)S(1)}, u32[]{:S(2)}, u32[]{:S(2)}) collective-permute-start(f32[64,128]{1,0:T(8,128)S(1)} %get-tuple-element.57), channel_id=1, source_target_pairs={{0,1},{1,0},{2,3},{3,2},{4,5},{5,4},{6,7},{7,6},{8,9},{9,8},{10,11... | collective-permute-start | bytes 98312 | tf_op jit(solution)/shard_map/ppermute | solution.py:450
  33.3 2.0 %collective-permute-start.10 = (f32[64,128]{1,0:T(8,128)S(1)}, f32[64,128]{1,0:T(8,128)S(1)}, u32[]{:S(2)}, u32[]{:S(2)}) collective-permute-start(f32[64,128]{1,0:T(8,128)S(1)} %get-tuple-element.58), channel_id=1, source_target_pairs={{0,4},{1,2},{2,1},{3,7},{4,0},{5,6},{6,5},{7,3},{8,12},{9,10},{10,... | collective-permute-start | bytes 98312 | tf_op jit(solution)/shard_map/ppermute | solution.py:450

commit v3 on v1

--- a/solution.py
+++ b/solution.py
@@ -95,10 +95,6 @@
     return jnp.where(offset == 0, own, jnp.where(offset < 0, low, high))
 
 
-def never():
-    return jnp.bool_(False)
-
-
 def z_weights(length, block, shape, position_dim):
     k = lax.axis_index("gz")
     offset = block - k
@@ -132,14 +128,34 @@
     zf_ref[1] = high
 
 
-def terms_kernel(gossip, pairs_x, u_ref, l_ref, coef_ref, cinv_ref, const_ref, t_ref, yf_ref, zf_ref, *outs):
+def diagonal_blocks(tile, length):
+    wide = jnp.concatenate([tile[:, :length]] * (length // NP), axis=0)
+    same = iota((length, length), 0) // NP == iota((length, length), 1) // NP
+    return jnp.where(same, wide, 0.0)
+
+
+def const_parts(const_ref, size_y, size_z):
+    stiff_z = diagonal_blocks(const_ref[0:NP, :], size_z)
+    stiff_y = diagonal_blocks(const_ref[NP : 2 * NP, :], size_y)
+    return stiff_z, stiff_y, const_ref[2 * NP : 3 * NP, :]
+
+
+def pair_planes(axis, size, count):
+    even = is_even(axis)
+    planes = [jnp.where(even, size - 1, 0), jnp.where(even, 0, size - 1)]
+    return planes[:count]
+
+
+def spread_coef(coef_ref, size_z):
+    elements, _, count = coef_ref.shape
+    coef = jnp.concatenate([coef_ref[e] for e in range(elements)], axis=0)
+    return dot(coef, (iota((count, size_z), 0) == iota((count, size_z), 1) // NP).astype(jnp.float32))
+
+
+def terms_kernel(gossip, pairs_x, u_ref, l_ref, const_ref, coef_ref, cinv_ref, _, t_ref, yf_ref, zf_ref, *outs):
     size_x, size_y, size_z = u_ref.shape
-    x_refs = outs[:pairs_x]
-    stiff_z = const_ref[0:size_z, :]
-    stiff_y = const_ref[size_z : size_z + size_y, 0:size_y]
-    mass = const_ref[size_z + size_y : size_z + size_y + NP, :]
-    spread = (iota((size_z // NP, size_z), 0) == iota((size_z // NP, size_z), 1) // NP).astype(jnp.float32)
-    coef = dot(coef_ref[0], spread) * HALF_WIDTH
+    stiff_z, stiff_y, mass = const_parts(const_ref, size_y, size_z)
+    coef = spread_coef(coef_ref, size_z) * HALF_WIDTH
     t_ref[...] = dot(u_ref[...].reshape(size_x * size_y, size_z), stiff_z).reshape(u_ref.shape)
     for x in range(size_x):
         t_ref[x] += dot(stiff_y, u_ref[x])
@@ -154,13 +170,10 @@
             source = HALF_WIDTH**3 * (l_ref[a, rows, :] - u[a])
             t_ref[a, rows, :] = (float(WEIGHTS[a]) * mass) * (source - scale * total)
     store_faces(t_ref, yf_ref, zf_ref)
-    faces = pair_payloads(t_ref[0], t_ref[size_x - 1], "gx", pairs_x)
-    for ref, face in zip(x_refs, faces):
-        ref[0:size_y, :] = face
+    for ref, face in zip(outs, pair_payloads(t_ref[0], t_ref[size_x - 1], "gx", pairs_x)):
+        ref[...] = face
     if gossip:
-        tab = coarse_tables(t_ref, cinv_ref)
-        outs[pairs_x][...] = tab
-        x_refs[0][size_y:, :] = tab
+        outs[pairs_x][...] = coarse_tables(t_ref, cinv_ref)
 
 
 def coarse_tables(t_ref, cinv_ref):
@@ -188,28 +201,32 @@
     return jnp.concatenate([part, inverse], axis=1)
 
 
-def coarse_planes(tab, size_x, size_y, size_z):
+def coarse_weights(size_x, size_z, line_ref, plane_ref, same_ref):
+    count_z = lax.axis_size("gz")
+    shape = line_ref.shape
+    line_ref[...] = z_weights(size_z, (iota(shape, 0) // count_z) % count_z, shape, 1)
+    square = same_ref.shape
+    same_ref[...] = (iota(square, 0) % count_z == iota(square, 1) % count_z).astype(jnp.float32)
+    _, size_y, rows = plane_ref.shape
+    for n, at_x in enumerate((0, 1, size_x - 1)):
+        plane_ref[n] = xy_weights(size_y, (size_y, rows), 0, iota((size_y, rows), 1), at_x, size_x)
+
+
+def coarse_planes(tab, line_ref, plane_ref, same_ref):
     count_z = lax.axis_size("gz")
     rows = tab.shape[0]
-    same = (iota((LANES, LANES), 0) % count_z == iota((LANES, LANES), 1) % count_z).astype(jnp.float32)
-    rhs = dot(tab[:, :LANES], same)
+    rhs = dot(tab[:, :LANES], same_ref[...])
     value = jnp.sum(rhs * tab[:, LANES:], axis=0, keepdims=True)
     value = jnp.broadcast_to(value, (rows, LANES))
     value = jnp.where(iota((rows, LANES), 1) // (count_z * count_z) == iota((rows, LANES), 0), value, 0.0)
-    shape = (LANES, size_z)
-    line = dot(value, z_weights(size_z, (iota(shape, 0) // count_z) % count_z, shape, 1))
-    planes = []
-    for at_x in (0, 1, size_x - 1):
-        w = xy_weights(size_y, (size_y, rows), 0, iota((size_y, rows), 1), at_x, size_x)
-        planes.append(dot(w, line))
-    return planes
-
-
-def y_kernel(gossip, pairs_x, extra, yf_ref, tab_ref, *refs):
+    line = dot(value, line_ref[...])
+    return [dot(plane_ref[n], line) for n in range(3)]
+
+
+def y_kernel(gossip, pairs_x, table_in_x, yf_ref, tab_ref, *refs):
     size_x, size_z = yf_ref.shape[1:]
     x_refs, refs = refs[:pairs_x], refs[pairs_x:]
-    extra_refs, refs = refs[:extra], refs[extra:]
-    size_y = x_refs[0].shape[0] - (NP if gossip else 0)
+    size_y = x_refs[0].shape[0] - (NP if table_in_x else 0)
     row = iota((size_x, size_z), 0)
     faces = []
     for side, at in ((0, 0), (1, size_y - 1)):
@@ -219,12 +236,16 @@
     for ref, face in zip(refs, pair_payloads(faces[0], faces[1], "gy", 2)):
         ref[0:size_x, :] = face
     if gossip:
-        tab = merge(tab_ref[...], x_refs[0][size_y:, :])
-        for r in extra_refs:
-            tab = merge(tab, r[...])
+        tab = tab_ref[...]
+        if table_in_x:
+            tab = merge(tab, x_refs[0][size_y:, :])
         refs[0][size_x:, :] = tab
         refs[1][size_x:, :] = tab
         refs[2][...] = tab
+
+
+def merge_kernel(tab_ref, far_ref, _, out_ref):
+    out_ref[...] = merge(tab_ref[...], far_ref[...])
 
 
 def z_kernel(gossip, pairs_x, zf_ref, tab_ref, *refs):
@@ -257,7 +278,23 @@
         refs[2][...] = tab
 
 
-def with_halo(plane, x, size_x, x_halo, y_halo, z_halo):
+def x_keep(x, size_x):
+    if x == 0:
+        return lax.axis_index("gx") != 0
+    if x == size_x - 1:
+        return jnp.logical_not(is_last("gx"))
+    return None
+
+
+def kept(plane, keep):
+    return plane if keep is None else jnp.where(keep, plane, 0.0)
+
+
+def z_keep(lane, size_z):
+    return jnp.logical_not(((lane == 0) & (lax.axis_index("gz") == 0)) | ((lane == size_z - 1) & is_last("gz")))
+
+
+def with_xy_halo(plane, x, size_x, x_halo, y_halo):
     size_y, size_z = plane.shape
     if x == 0:
         plane = plane + x_halo[0]
@@ -266,22 +303,25 @@
     row, lane = iota(plane.shape, 0), iota(plane.shape, 1)
     plane = plane + jnp.where(row == 0, y_halo[0][x : x + 1, :], 0.0)
     plane = plane + jnp.where(row == size_y - 1, y_halo[1][x : x + 1, :], 0.0)
-    plane = plane + jnp.where(lane == 0, z_halo[0][:, x : x + 1], 0.0)
-    plane = plane + jnp.where(lane == size_z - 1, z_halo[1][:, x : x + 1], 0.0)
-    keep = jnp.logical_not(((lane == 0) & (lax.axis_index("gz") == 0)) | ((lane == size_z - 1) & is_last("gz")))
-    if x == 0:
-        keep = keep & (lax.axis_index("gx") != 0)
-    if x == size_x - 1:
-        keep = keep & jnp.logical_not(is_last("gx"))
-    return jnp.where(keep, plane, 0.0)
-
-
-def halos(shape, x_refs, y_refs, z_refs):
+    return kept(jnp.where(z_keep(lane, size_z), plane, 0.0), x_keep(x, size_x))
+
+
+def xy_halos(shape, x_refs, y_refs):
     size_x, size_y, _ = shape
     x_halo = low_high([r[0:size_y, :] for r in x_refs], "gx")
     y_halo = low_high([r[0:size_x, :] for r in y_refs], "gy")
-    z_halo = low_high([r[0:size_y, :] for r in z_refs], "gz")
-    return x_halo, y_halo, z_halo
+    return x_halo, y_halo
+
+
+def z_halos(shape, z_refs):
+    size_x, size_y, _ = shape
+    low, high = low_high([r[0:size_y, :] for r in z_refs], "gz")
+    lane = iota((size_y, LANES), 1)
+    keep = (lane > 0) | (lax.axis_index("gx") != 0)
+    keep = keep & ((lane < size_x - 1) | jnp.logical_not(is_last("gx")))
+    low = jnp.where(keep & (lax.axis_index("gz") != 0), low, 0.0)
+    high = jnp.where(keep & jnp.logical_not(is_last("gz")), high, 0.0)
+    return low, high
 
 
 def merged_table(tab_ref, z_refs, size_y):
@@ -291,101 +331,186 @@
     return tab
 
 
-def prepare_kernel(basis_ref, values_ref, scalar_ref, coef_ref, pz_ref, pzt_ref, py_ref, pyt_ref, inv_ref):
+def prepare_kernel(basis_ref, values_ref, coef_ref, _, pz_ref, pzt_ref, py_ref, pyt_ref, px_ref, entry_ref, inv_ref, tile_ref):
     size_x, size_y, size_z = inv_ref.shape
-
-    def folded(length, transposed):
-        pick = (iota((length, NP), 0) % NP == iota((length, NP), 1)).astype(jnp.float32)
-        basis = basis_ref[...]
-        left = dot(pick, basis, ((1,), (1 if transposed else 0,)))
-        wide = dot(left, pick, ((1,), (1,)))
+    square = (NP, NP)
+    diagonal = iota(square, 0) == iota(square, 1)
+    basis = basis_ref[...]
+    turned = dot(diagonal.astype(jnp.float32), basis, ((1,), (1,)))
+    along_y = jnp.sum(jnp.where(diagonal, values_ref[...], 0.0), axis=1, keepdims=True)
+
+    def repeated(matrix):
+        tile_ref[...] = jnp.zeros_like(tile_ref)
+        tile_ref[:, 0:NP] = matrix
+        tile = tile_ref[...]
+        for step in (8, 16, 32, 64):
+            tile = tile + pltpu.roll(tile, step, 1)
+        return jnp.concatenate([tile] * (size_z // LANES), axis=1)
+
+    plain, flipped = repeated(basis), repeated(turned)
+    along_z = repeated(jnp.broadcast_to(values_ref[...], square))
+
+    def folded(length):
         row, col = iota((length, length), 0), iota((length, length), 1)
-        wide = jnp.where(row // NP == col // NP, wide, 0.0)
-        dim, at = (1, col) if transposed else (0, row)
-        after = pltpu.roll(wide, length - 1, dim)
-        before = pltpu.roll(wide, 1, dim)
-        wide = wide + jnp.where((at % NP == NP - 1) & (at != length - 1), after, 0.0)
-        return wide + jnp.where((at % NP == 0) & (at != 0), before, 0.0)
-
-    pz_ref[...] = folded(size_z, False)
-    pzt_ref[...] = folded(size_z, True)
-    py_ref[...] = folded(size_y, False)
-    pyt_ref[...] = folded(size_y, True)
-    spread = (iota((size_z // NP, size_z), 0) == iota((size_z // NP, size_z), 1) // NP).astype(jnp.float32)
-    coef = dot(coef_ref[0], spread)
-    pick = (iota((NP, size_z), 0) == iota((NP, size_z), 1) % NP).astype(jnp.float32)
-    along_z = dot(values_ref[...], pick)
-    diagonal = iota((NP, NP), 0) == iota((NP, NP), 1)
-    along_y = jnp.sum(jnp.where(diagonal, values_ref[...], 0.0), axis=1, keepdims=True)
+        wide = diagonal_blocks(plain, length)
+        up, down = row // NP + 1 == col // NP, row // NP == col // NP + 1
+        wide = wide + jnp.where(up & (row % NP == NP - 1), plain[0:1, :length], 0.0)
+        return wide + jnp.where(down & (row % NP == 0), plain[NP - 1 : NP, :length], 0.0)
+
+    def folded_turned(length):
+        row, col = iota((length, length), 0), iota((length, length), 1)
+        wide = diagonal_blocks(flipped, length)
+        up, down = col // NP + 1 == row // NP, col // NP == row // NP + 1
+        first = jnp.concatenate([turned[:, 0:1]] * (length // NP), axis=0)
+        last = jnp.concatenate([turned[:, NP - 1 : NP]] * (length // NP), axis=0)
+        wide = wide + jnp.where(up & (col % NP == NP - 1), first, 0.0)
+        return wide + jnp.where(down & (col % NP == 0), last, 0.0)
+
+    pz_ref[...] = folded(size_z)
+    pzt_ref[...] = folded_turned(size_z)
+    py_ref[...] = folded(size_y)
+    pyt_ref[...] = folded_turned(size_y)
+    px_ref[...] = diagonal_blocks(plain, LANES)
+    for a in range(NP):
+        for b in range(NP):
+            entry_ref[a * NP + b : a * NP + b + 1, :] = jnp.broadcast_to(basis[a : a + 1, b : b + 1], (1, size_z))
     along = along_y + along_z
-    for e in range(size_y // NP):
-        for a in range(NP):
-            inv_ref[a, e * NP : (e + 1) * NP, :] = 1.0 / (coef[e : e + 1, :] * (along + scalar_ref[0, a]) + 1.0)
-
-
-def solve_kernel(gossip, pairs_x, t_ref, basis_ref, pz_ref, pzt_ref, py_ref, pyt_ref, inv_ref, tab_ref, *refs):
+    coef = spread_coef(coef_ref, size_z)
+    for a in range(NP):
+        along_x = values_ref[:, a : a + 1]
+        for e in range(size_y // NP):
+            inv_ref[a, e * NP : (e + 1) * NP, :] = 1.0 / (coef[e : e + 1, :] * (along + along_x) + 1.0)
+
+
+def forward_kernel(pairs_x, t_ref, pz_ref, pyt_ref, entry_ref, *refs):
     shape = size_x, size_y, size_z = t_ref.shape
-    x_refs, y_refs, z_refs = refs[:pairs_x], refs[pairs_x : pairs_x + 2], refs[pairs_x + 2 : pairs_x + 4]
-    y_ref, yf_ref, zf_ref, *outs = refs[pairs_x + 4 :]
-    scratch = outs[-1]
-    x_halo, y_halo, z_halo = halos(shape, x_refs, y_refs, z_refs)
+    x_refs, y_refs, (s_ref, scratch) = refs[:pairs_x], refs[pairs_x : pairs_x + 2], refs[pairs_x + 2 :]
+    x_halo, y_halo = xy_halos(shape, x_refs, y_refs)
     for x in range(size_x):
-        plane = with_halo(t_ref[x], x, size_x, x_halo, y_halo, z_halo)
-        y_ref[x] = dot(pyt_ref[...], plane)
-    flat = (size_x * size_y, size_z)
-    scratch[...] = dot(y_ref[...].reshape(flat), pz_ref[...]).reshape(shape)
+        s_ref[x] = dot(pyt_ref[...], with_xy_halo(t_ref[x], x, size_x, x_halo, y_halo))
+    scratch[...] = dot(s_ref[...].reshape(size_x * size_y, size_z), pz_ref[...]).reshape(shape)
     for e in range(size_y // NP):
         rows = slice(e * NP, (e + 1) * NP)
         r = [scratch[b, rows, :] for b in range(NP)]
+        for a in range(NP):
+            total = entry_ref[a : a + 1, :] * r[0]
+            for b in range(1, NP):
+                total = total + entry_ref[b * NP + a : b * NP + a + 1, :] * r[b]
+            s_ref[a, rows, :] = total
+
+
+def middle_kernel(gossip, pairs_x, s_ref, pz_ref, pzt_ref, py_ref, pyt_ref, px_ref, entry_ref, inv_ref, tab_ref, *refs):
+    shape = size_x, size_y, size_z = s_ref.shape
+    z_refs, half_ref, outs = refs[:2], refs[2], refs[3:]
+    low, high = z_halos(shape, z_refs)
+    both = jnp.where(iota((size_y, LANES), 1) < NP, low, pltpu.roll(high, NP, 1))
+    both = jnp.where(iota((size_y, LANES), 1) < 2 * NP, both, 0.0)
+    both = dot(dot(pyt_ref[...], both), px_ref[...])
+    last = (size_x - 1) * NP
+    weights = []
+    for plane in pair_planes("gx", size_x, pairs_x):
+        weights.append([jnp.where(plane == 0, entry_ref[b : b + 1, :], entry_ref[last + b : last + b + 1, :]) for b in range(NP)])
+    low_row = pz_ref[0:1, 0:LANES]
+    high_row = pz_ref[size_z - 1 : size_z, size_z - LANES :]
+    for e in range(size_y // NP):
+        rows = slice(e * NP, (e + 1) * NP)
         s = []
         for a in range(NP):
-            total = basis_ref[0, a] * r[0]
+            add_low = both[rows, a : a + 1] * low_row
+            add_high = both[rows, NP + a : NP + a + 1] * high_row
+            if size_z == 2 * LANES:
+                add = jnp.concatenate([add_low, add_high], axis=1)
+            else:
+                gap = jnp.zeros((NP, size_z - 2 * LANES), jnp.float32)
+                add = jnp.concatenate([add_low, gap, add_high], axis=1)
+            s.append((s_ref[a, rows, :] + add) * inv_ref[a, rows, :])
+            half_ref[a, rows, :] = s[a]
+        for ref, row in zip(outs[:pairs_x], weights):
+            total = row[0] * s[0]
             for b in range(1, NP):
-                total = total + basis_ref[b, a] * r[b]
-            s.append(total * inv_ref[a, rows, :])
-        for a in range(NP):
-            total = basis_ref[a, 0] * s[0]
-            for b in range(1, NP):
-                total = total + basis_ref[a, b] * s[b]
-            scratch[a, rows, :] = total
-    scratch[...] = dot(scratch[...].reshape(flat), pzt_ref[...]).reshape(shape)
-    for x in range(size_x):
-        y_ref[x] = dot(py_ref[...], scratch[x])
-    store_faces(y_ref, yf_ref, zf_ref)
-    for ref, face in zip(outs[:pairs_x], pair_payloads(y_ref[0], y_ref[size_x - 1], "gx", pairs_x)):
-        ref[0:size_y, :] = face
+                total = total + row[b] * s[b]
+            ref[rows, :] = total
+    for ref in outs[:pairs_x]:
+        ref[0:size_y, :] = dot(py_ref[...], dot(ref[0:size_y, :], pzt_ref[...]))
     if gossip:
         tab = merged_table(tab_ref, z_refs, size_y)
         outs[pairs_x][...] = tab
         outs[0][size_y:, :] = tab
 
 
-def final_kernel(gossip, pairs_x, s_ref, tab_ref, *refs):
+def inverse_kernel(half_ref, pzt_ref, py_ref, entry_ref, y_ref, yf_ref, zf_ref, scratch):
+    shape = size_x, size_y, size_z = half_ref.shape
+    for e in range(size_y // NP):
+        rows = slice(e * NP, (e + 1) * NP)
+        s = [half_ref[b, rows, :] for b in range(NP)]
+        for a in range(NP):
+            total = entry_ref[a * NP : a * NP + 1, :] * s[0]
+            for b in range(1, NP):
+                total = total + entry_ref[a * NP + b : a * NP + b + 1, :] * s[b]
+            y_ref[a, rows, :] = total
+    scratch[...] = dot(y_ref[...].reshape(size_x * size_y, size_z), pzt_ref[...]).reshape(shape)
+    for x in range(size_x):
+        y_ref[x] = dot(py_ref[...], scratch[x])
+    store_faces(y_ref, yf_ref, zf_ref)
+
+
+def assemble_kernel(pairs_x, s_ref, *refs):
+    shape = s_ref.shape
+    x_refs, y_refs, out_ref = refs[:pairs_x], refs[pairs_x : pairs_x + 2], refs[-1]
+    x_halo, y_halo = xy_halos(shape, x_refs, y_refs)
+    for x in range(shape[0]):
+        out_ref[x] = with_xy_halo(s_ref[x], x, shape[0], x_halo, y_halo)
+
+
+def final_kernel(gossip, s_ref, tab_ref, z_low_ref, z_high_ref, *refs):
     shape = size_x, size_y, size_z = s_ref.shape
-    x_refs, y_refs, z_refs = refs[:pairs_x], refs[pairs_x : pairs_x + 2], refs[pairs_x + 2 : pairs_x + 4]
-    out_ref = refs[-1]
+    z_refs = (z_low_ref, z_high_ref)
+    out_ref, buffer, sems = refs[-3:]
     if gossip:
-        coarse = coarse_planes(merged_table(tab_ref, z_refs, size_y), *shape)
+        coarse = coarse_planes(merged_table(tab_ref, z_refs, size_y), *refs[:3])
     else:
         coarse = [tab_ref[c] for c in range(3)]
-    x_halo, y_halo, z_halo = halos(shape, x_refs, y_refs, z_refs)
+    lane = iota((size_y, size_z), 1)
+    coarse = [jnp.where(z_keep(lane, size_z), plane, 0.0) for plane in coarse]
+    low, high = z_halos(shape, z_refs)
+    copies = []
     for x in range(size_x):
-        plane = s_ref[x] + coarse[0 if x == 0 else 2 if x == size_x - 1 else 1]
-        out_ref[x] = with_halo(plane, x, size_x, x_halo, y_halo, z_halo)
+        plane = kept(coarse[0 if x == 0 else 2 if x == size_x - 1 else 1], x_keep(x, size_x)) + s_ref[x]
+        plane = plane + jnp.where(lane == 0, low[:, x : x + 1], 0.0)
+        buffer[x] = plane + jnp.where(lane == size_z - 1, high[:, x : x + 1], 0.0)
+        copies.append(pltpu.make_async_copy(buffer.at[x], out_ref.at[x], sems.at[x]))
+        copies[-1].start()
+    for copy in copies:
+        copy.wait()
 
 
 VMEM = pl.BlockSpec(memory_space=pltpu.VMEM)
-SMEM = pl.BlockSpec(memory_space=pltpu.SMEM)
-
-
-def call(kernel, name, inputs, shapes, scratch=(), smem=()):
+FLOPS = {
+    "weights": 1_500_000_000,
+    "operators": 10_000_000,
+    "terms": 1_700_000_000,
+    "y_faces": 10_000_000,
+    "merge": 100_000_000,
+    "z_faces": 100_000_000,
+    "forward": 1_100_000_000,
+    "middle": 1_200_000_000,
+    "inverse": 1_800_000_000,
+    "assemble": 100_000_000,
+    "final": 1_400_000_000,
+}
+HBM = pl.BlockSpec(memory_space=pltpu.MemorySpace.HBM)
+
+
+def call(kernel, name, inputs, shapes, scratch=(), in_spec=VMEM, out_spec=VMEM, grant=8 << 20):
     return pl.pallas_call(
         kernel,
         name=name,
         out_shape=[jax.ShapeDtypeStruct(s, jnp.float32) for s in shapes],
-        in_specs=[SMEM if n in smem else VMEM for n in range(len(inputs))],
-        out_specs=[VMEM] * len(shapes),
-        scratch_shapes=[pltpu.VMEM(s, jnp.float32) for s in scratch],
+        in_specs=[in_spec] * len(inputs),
+        out_specs=[out_spec] * len(shapes),
+        scratch_shapes=[pltpu.VMEM(s, jnp.float32) if isinstance(s, tuple) else s for s in scratch],
+        compiler_params=pltpu.CompilerParams(vmem_limit_bytes=grant),
+        cost_estimate=pl.CostEstimate(flops=FLOPS[name], bytes_accessed=0, transcendentals=0),
     )(*inputs)
 
 
@@ -405,6 +530,12 @@
             pairs.append((int(np.ravel_multi_index(place, sizes)), int(np.ravel_multi_index(other, sizes))))
         result.append(pairs)
     return result
+
+
+def far_pairs(sizes):
+    places = list(np.ndindex(*sizes))
+    others = [(i, j, k ^ 2) for i, j, k in places]
+    return [(int(np.ravel_multi_index(a, sizes)), int(np.ravel_multi_index(b, sizes))) for a, b in zip(places, others)]
 
 
 def coarse_by_sums(terms, coarse_inverse):
@@ -432,72 +563,97 @@
 def on_device(sizes, fluidity, local_fluidity, element_coef, fdm_basis, fdm_values, coarse_inverse):
     shape = size_x, size_y, size_z = fluidity.shape
     gossip = sizes == (2, 4, 4)
-    extra_rows = NP if gossip else 0
-    perms = [pair_permutations(sizes, dim) for dim in range(3)]
-    pairs_x = len(perms[0])
-
-    const = np.zeros((size_z + size_y + NP, size_z), np.float32)
-    const[:size_z] = np.kron(np.eye(size_z // NP), STIFF.T)
-    const[size_z : size_z + size_y, :size_y] = np.kron(np.eye(size_y // NP), STIFF)
-    const[size_z + size_y :] = WEIGHTS[:, None] * np.tile(WEIGHTS, size_z // NP)[None, :]
-
+    table_rows = NP if gossip else 0
+    perms_x, perms_y, perms_z = [pair_permutations(sizes, dim) for dim in range(3)]
+    pairs_x = len(perms_x)
+
+    tiles = [np.tile(m, size_z // NP) for m in (STIFF.T, STIFF, WEIGHTS[:, None] * WEIGHTS)]
+    const = np.concatenate(tiles).astype(np.float32)
+
+    square_z, square_y = (size_z, size_z), (size_y, size_y)
     face_shapes = [(2, size_x, size_z), (2, size_y, LANES)]
-    x_shapes = [(size_y + extra_rows, size_z)] * pairs_x
     tab_shapes = [(NP, size_z)] if gossip else []
 
     def send(payloads, pairs):
         return [lax.ppermute(p, AXES, q) for p, q in zip(payloads, pairs)]
 
-    def exchange(y_faces, z_faces, x_payloads, tab, extra):
-        x_got = send(x_payloads, perms[0])
-        extra_got = send([tab] * len(extra), extra)
-        y_out = call(
-            functools.partial(y_kernel, gossip, pairs_x, len(extra)),
+    def y_round(y_faces, x_got, tab, table_in_x):
+        out = call(
+            functools.partial(y_kernel, gossip, pairs_x, table_in_x),
             "y_faces",
-            [y_faces, tab, *x_got, *extra_got],
-            [(size_x + extra_rows, size_z)] * 2 + tab_shapes,
+            [y_faces, tab, *x_got],
+            [(size_x + table_rows, size_z)] * 2 + tab_shapes,
         )
-        y_got = send(y_out[:2], perms[1])
-        tab = y_out[-1] if gossip else tab
-        z_out = call(
+        return send(out[:2], perms_y), out[-1] if gossip else tab, out[0]
+
+    def z_round(z_faces, x_got, y_got, tab):
+        out = call(
             functools.partial(z_kernel, gossip, pairs_x),
             "z_faces",
             [z_faces, tab, *x_got, *y_got],
-            [(size_y + 2 * extra_rows, LANES)] * 2 + tab_shapes,
+            [(size_y + 2 * table_rows, LANES)] * 2 + tab_shapes,
         )
-        z_got = send(z_out[:2], perms[2])
-        tab = z_out[-1] if gossip else tab
-        return [*x_got, *y_got, *z_got], tab
-
+        return send(out[:2], perms_z), out[-1] if gossip else tab
+
+    coef = element_coef.reshape(size_y // NP, 1, size_z // NP)
+    weights = []
+    if gossip:
+        weights = call(
+            functools.partial(coarse_weights, size_x, size_z),
+            "weights",
+            [],
+            [(LANES, size_z), (3, size_y, sizes[0] * sizes[1]), (LANES, LANES)],
+        )
     terms, y_faces, z_faces, *rest = call(
         functools.partial(terms_kernel, gossip, pairs_x),
         "terms",
-        [fluidity, local_fluidity, element_coef, coarse_inverse, const],
-        [shape] + face_shapes + x_shapes + tab_shapes,
+        [fluidity, local_fluidity, const, coef, coarse_inverse, weights[0] if gossip else coef],
+        [shape] + face_shapes + [(size_y, size_z)] * pairs_x + tab_shapes,
     )
-    tab = rest[-1]
-    extra = [perms[2][0]] if gossip else []
-    got, tab = exchange(y_faces, z_faces, rest[:pairs_x], tab, extra)
-    values = fdm_values.reshape(1, NP)
-    operators = call(
+    x_got = send(rest[:pairs_x], perms_x)
+    tab = rest[-1] if gossip else coef
+    far = send([tab], [far_pairs(sizes)]) if gossip else []
+    y_got, tab, sent = y_round(y_faces, x_got, tab, False)
+    pz, pzt, py, pyt, px, entries, inverse = call(
         prepare_kernel,
         "operators",
-        [fdm_basis, values, values, element_coef],
-        [(size_z, size_z)] * 2 + [(size_y, size_y)] * 2 + [shape],
-        smem=(2,),
+        [fdm_basis, fdm_values.reshape(1, NP), coef, sent],
+        [square_z, square_z, square_y, square_y, (LANES, LANES), (NP * NP, size_z), shape],
+        scratch=[(NP, LANES)],
     )
-    solved, y_faces, z_faces, *rest = call(
-        functools.partial(solve_kernel, gossip, pairs_x),
-        "solve",
-        [terms, fdm_basis, *operators, tab, *got],
-        [shape] + face_shapes + x_shapes + tab_shapes,
+    if gossip:
+        tab = call(merge_kernel, "merge", [tab, far[0], px], tab_shapes)[0]
+    z_got, tab = z_round(z_faces, x_got, y_got, tab)
+    spectrum = call(
+        functools.partial(forward_kernel, pairs_x),
+        "forward",
+        [terms, pz, pyt, entries, *x_got, *y_got],
+        [shape],
         scratch=[shape],
-        smem=(1,),
+    )[0]
+    half, *rest = call(
+        functools.partial(middle_kernel, gossip, pairs_x),
+        "middle",
+        [spectrum, pz, pzt, py, pyt, px, entries, inverse, tab, *z_got],
+        [shape] + [(size_y + table_rows, size_z)] * pairs_x + tab_shapes,
     )
-    got, tab = exchange(y_faces, z_faces, rest[:pairs_x], rest[-1], [])
+    x_got = send(rest[:pairs_x], perms_x)
+    solved, y_faces, z_faces = call(
+        inverse_kernel, "inverse", [half, pzt, py, entries], [shape] + face_shapes, scratch=[shape]
+    )
+    y_got, tab, _ = y_round(y_faces, x_got, rest[-1] if gossip else coef, gossip)
+    z_got, tab = z_round(z_faces, x_got, y_got, tab)
+    solved = call(
+        functools.partial(assemble_kernel, pairs_x), "assemble", [solved, *x_got, *y_got], [shape]
+    )[0]
     coarse = tab if gossip else coarse_by_sums(terms, coarse_inverse)
     return call(
-        functools.partial(final_kernel, gossip, pairs_x), "final", [solved, coarse, *got], [shape]
+        functools.partial(final_kernel, gossip),
+        "final",
+        [solved, coarse, *z_got, *weights],
+        [shape],
+        scratch=[shape, pltpu.SemaphoreType.DMA((size_x,))],
+        out_spec=HBM,
     )[0]
 
 

time: 50.4 us -> 30.8 us (0.61)
  Pallas kernels: 20 us -> 7.84 us
  waiting for transfers between devices: 11.7 us -> 6.69 us
  local copies, waits for them, and re-layouts: 4.95 us -> 1.06 us
  starting transfers between devices: 13.3 us -> 15 us
    pallas_call x8 -> x13, Pallas kernels: 20 us -> 7.84 us  [call(): pl.pallas_call(kernel, name=name, out_shape=[jax.ShapeDtypeStruct(s, jnp....]
    ppermute x11, waiting for transfers between devices: 11.7 us -> 6.69 us  [send(): return [lax.ppermute(p, AXES, q) for p, q in zip(payloads, pairs)]]
    unnamed x23 -> x14, local copies, waits for them, and re-layouts: 4.95 us -> 1.06 us
    ppermute x11, starting transfers between devices: 13.3 us -> 15 us  [send(): return [lax.ppermute(p, AXES, q) for p, q in zip(payloads, pairs)]]
  transfers between devices with their start and end apart: 11 -> 11, of which waited for: 5 -> 5; matrix products, arithmetic and copies ran while one was open for 0% -> 0% of each run, Pallas kernels for 6% -> 11%
where the time goes in v3:
time: 30.8 us; the launch traced here: 30.7 us
  starting transfers between devices  15 us (49%)
  Pallas kernels  7.84 us (25%)
  waiting for transfers between devices  6.69 us (22%)
  local copies, waits for them, and re-layouts  1.06 us (3%)
    ppermute x11, starting transfers between devices, send(): return [lax.ppermute(p, AXES, q) for p, q in zip(payloads, pairs)]  15 us
    pallas_call x13, Pallas kernels, call(): pl.pallas_call(kernel, name=name, out_shape=[jax.ShapeDtypeStruct(s, jnp....  7.84 us
    ppermute x11, waiting for transfers between devices, send(): return [lax.ppermute(p, AXES, q) for p, q in zip(payloads, pairs)]  6.69 us
    unnamed x14, local copies, waits for them, and re-layouts  1.06 us
  transfers between devices with their start and end apart: 11, of which 5 were waited for; matrix products, arithmetic and copies ran while one was open for 0% of the time, Pallas kernels for 11%

profile of v3, /device:TPU:0, one launch (start us, length us, event | category | flops | bytes accessed | tf_op | source)
XLA Modules:
  0.0 30.7 jit_solution(4683542709189563520)
XLA Ops:
  0.0 0.0 copy-start.6
  0.0 0.0 copy-start.1
  0.0 0.0 copy-start
  0.0 0.1 weights.1
  0.1 0.0 copy-start.3
  0.1 0.0 copy-start.4
  0.1 0.6 %copy-done.6 = f32[24,256]{1,0:T(8,128)S(1)} copy-done((f32[24,256]{1,0:T(8,128)S(1)}, f32[24,256]{1,0:T(8,128)}, u32[]{:S(2)}) %copy-start.6) | copy-done | bytes 24600
  0.7 0.3 copy-done.1
  1.0 0.1 copy-done
  1.1 0.0 copy-done.3
  1.1 0.0 copy-done.4
  1.1 1.6 %terms.1 = (f32[8,48,256]{2,1,0:T(8,128)S(1)}, f32[2,8,256]{2,1,0:T(8,128)S(1)}, f32[2,48,128]{2,1,0:T(8,128)S(1)}, f32[48,256]{1,0:T(8,128)S(1)}, f32[8,256]{1,0:T(8,128)S(1)}) custom-call(f32[8,48,256]{2,1,0:T(8,128)S(1)} %copy-done, f32[8,48,256]{2,1,0:T(8,128)S(1)} %copy-done.1, f32[24,256]{1,0:T(8,128)S(1)} %copy-done.6, f32[6,1,32]{2,1,0:T(1,128)S(1)} %bitcast.2, ...), custom_call_target="tpu_custom_call" | custom-call | flops 1700000000 | tf_op jit(solution)/shard_map/terms/pallas_call | solution.py:505
  2.7 3.0 %collective-permute-start = (f32[48,256]{1,0:T(8,128)S(1)}, f32[48,256]{1,0:T(8,128)S(1)}, u32[]{:S(2)}, u32[]{:S(2)}) collective-permute-start(f32[48,256]{1,0:T(8,128)S(1)} %get-tuple-element.42), channel_id=1, source_target_pairs={{0,16},{1,17},{2,18},{3,19},{4,20},{5,21},{6,22},{7,23},{8,24},{9,... | collective-permute-start | bytes 147464 | tf_op jit(solution)/shard_map/ppermute | solution.py:578
  5.7 2.6 %collective-permute-start.3 = (f32[8,256]{1,0:T(8,128)S(1)}, f32[8,256]{1,0:T(8,128)S(1)}, u32[]{:S(2)}, u32[]{:S(2)}) collective-permute-start(f32[8,256]{1,0:T(8,128)S(1)} %get-tuple-element.41.tab_ref), channel_id=1, source_target_pairs={{0,2},{1,3},{2,0},{3,1},{4,6},{5,7},{6,4},{7,5},{8,10},{9,11},{10,... | collective-permute-start | bytes 24584 | tf_op jit(solution)/shard_map/ppermute | solution.py:578
  8.3 0.0 collective-permute-done.refs_0_
  8.3 0.0 copy-start.2
  8.3 0.5 %collective-permute-start.2 = (f32[16,256]{1,0:T(8,128)S(1)}, f32[16,256]{1,0:T(8,128)S(1)}, u32[]{:S(2)}, u32[]{:S(2)}) collective-permute-start(f32[16,256]{1,0:T(8,128)S(1)} %get-tuple-element.47), channel_id=1, source_target_pairs={{0,12},{1,13},{2,14},{3,15},{4,8},{5,9},{6,10},{7,11},{8,4},{9,5},... | collective-permute-start | bytes 49160 | tf_op jit(solution)/shard_map/ppermute | solution.py:578
  8.8 0.0 copy-start.5
  8.8 1.2 %collective-permute-start.1 = (f32[16,256]{1,0:T(8,128)S(1)}, f32[16,256]{1,0:T(8,128)S(1)}, u32[]{:S(2)}, u32[]{:S(2)}) collective-permute-start(f32[16,256]{1,0:T(8,128)S(1)} %get-tuple-element.43._), channel_id=1, source_target_pairs={{0,4},{1,5},{2,6},{3,7},{4,0},{5,1},{6,2},{7,3},{8,12},{9,13},{10,... | collective-permute-start | bytes 49160 | tf_op jit(solution)/shard_map/ppermute | solution.py:578
  10.0 0.0 copy-done.2
  10.0 0.0 copy-done.5
  10.0 0.7 %operators.1 = (f32[256,256]{1,0:T(8,128)S(1)}, f32[256,256]{1,0:T(8,128)S(1)}, f32[48,48]{1,0:T(8,128)S(1)}, f32[48,48]{1,0:T(8,128)S(1)}, f32[128,128]{1,0:T(8...) custom-call(f32[8,8]{1,0:T(8,128)S(1)} %copy-done.2, f32[1,8]{1,0:T(1,128)S(1)} %bitcast.4, ...), custom_call_target="tpu_custom_call" | custom-call | flops 10000000 | tf_op jit(solution)/shard_map/operators/pallas_call | solution.py:505
  10.7 0.0 collective-permute-done.3.far_ref
  10.7 0.9 %collective-permute-done.2.refs_2_ = f32[16,256]{1,0:T(8,128)S(1)} collective-permute-done((f32[16,256]{1,0:T(8,128)S(1)}, f32[16,256]{1,0:T(8,128)S(1)}, u32[]{:S(2)}, u32[]{:S(2)}) %collective-permute-start.2) | collective-permute-done | bytes 16416 | tf_op jit(solution)/shard_map/ppermute | solution.py:578
  11.6 0.0 collective-permute-done.1.refs_1_
  11.6 0.1 z_faces.2
  11.7 1.6 %collective-permute-start.4 = (f32[64,128]{1,0:T(8,128)S(1)}, f32[64,128]{1,0:T(8,128)S(1)}, u32[]{:S(2)}, u32[]{:S(2)}) collective-permute-start(f32[64,128]{1,0:T(8,128)S(1)} %get-tuple-element.55), channel_id=1, source_target_pairs={{0,1},{1,0},{2,3},{3,2},{4,5},{5,4},{6,7},{7,6},{8,9},{9,8},{10,11... | collective-permute-start | bytes 98312 | tf_op jit(solution)/shard_map/ppermute | solution.py:578
  13.4 0.0 collective-permute-start.5
  13.4 1.0 %forward.1.s_ref = f32[8,48,256]{2,1,0:T(8,128)S(1)} custom-call(f32[8,48,256]{2,1,0:T(8,128)S(1)} %get-tuple-element.39.t_ref, f32[256,256]{1,0:T(8,128)S(1)} %get-tuple-element.44.pz_ref, f32[48,48]{1,0:T(8,128)S(1)} %get-tuple-element.45.pyt_ref, f32[64,256]{1,0:T(8,128)S(1)} %get-tuple-element.46.entry_ref, f32[48,256]{1,0:T(8,128)S(1)} %collective-permute-done.refs_0_, ...), custom_call_target="tpu_custom_call" | custom-call | flops 1100000000 | tf_op jit(solution)/shard_map/forward/pallas_call | solution.py:505
  14.4 1.3 %collective-permute-done.4.refs_0_ = f32[64,128]{1,0:T(8,128)S(1)} collective-permute-done((f32[64,128]{1,0:T(8,128)S(1)}, f32[64,128]{1,0:T(8,128)S(1)}, u32[]{:S(2)}, u32[]{:S(2)}) %collective-permute-start.4) | collective-permute-done | bytes 32800 | tf_op jit(solution)/shard_map/ppermute | solution.py:578
  15.7 0.0 collective-permute-done.5.refs_1_
  15.7 1.1 %middle.1 = (f32[8,48,256]{2,1,0:T(8,128)S(1)}, f32[56,256]{1,0:T(8,128)S(1)}, f32[8,256]{1,0:T(8,128)S(1)}) custom-call(f32[8,48,256]{2,1,0:T(8,128)S(1)} %forward.1.s_ref, f32[256,256]{1,0:T(8,128)S(1)} %get-tuple-element.44.pz_ref, f32[256,256]{1,0:T(8,128)S(1)} %get-tuple-element.48.pzt_ref, f32[48,48]{1,0:T(8,128)S(1)} %get-tuple-element.49.py_ref, ...), custom_call_target="tpu_custom_call" | custom-call | flops 1200000000 | tf_op jit(solution)/shard_map/middle/pallas_call | solution.py:505
  16.9 1.6 %collective-permute-start.6 = (f32[56,256]{1,0:T(8,128)S(1)}, f32[56,256]{1,0:T(8,128)S(1)}, u32[]{:S(2)}, u32[]{:S(2)}) collective-permute-start(f32[56,256]{1,0:T(8,128)S(1)} %get-tuple-element.59), channel_id=1, source_target_pairs={{0,16},{1,17},{2,18},{3,19},{4,20},{5,21},{6,22},{7,23},{8,24},{9,... | collective-permute-start | bytes 172040 | tf_op jit(solution)/shard_map/ppermute | solution.py:578
  18.4 1.7 %inverse.1 = (f32[8,48,256]{2,1,0:T(8,128)S(1)}, f32[2,8,256]{2,1,0:T(8,128)S(1)}, f32[2,48,128]{2,1,0:T(8,128)S(1)}) custom-call(f32[8,48,256]{2,1,0:T(8,128)S(1)} %get-tuple-element.57.half_ref, f32[256,256]{1,0:T(8,128)S(1)} %get-tuple-element.48.pzt_ref, f32[48,48]{1,0:T(8,128)S(1)} %get-tuple-element.49.py_ref, f32[64,256]{1,0:T(8,128)S(1)} %get-tuple-element.46.entry_ref), custom_call_target="tpu_custom_call" | custom-call | flops 1800000000 | tf_op jit(solution)/shard_map/inverse/pallas_call | solution.py:505
  20.1 1.0 %collective-permute-done.6.refs_0_ = f32[56,256]{1,0:T(8,128)S(1)} collective-permute-done((f32[56,256]{1,0:T(8,128)S(1)}, f32[56,256]{1,0:T(8,128)S(1)}, u32[]{:S(2)}, u32[]{:S(2)}) %collective-permute-start.6) | collective-permute-done | bytes 57376 | tf_op jit(solution)/shard_map/ppermute | solution.py:578
  21.1 0.1 collective-permute-start.7
  21.2 1.5 %collective-permute-start.8 = (f32[16,256]{1,0:T(8,128)S(1)}, f32[16,256]{1,0:T(8,128)S(1)}, u32[]{:S(2)}, u32[]{:S(2)}) collective-permute-start(f32[16,256]{1,0:T(8,128)S(1)} %get-tuple-element.63), channel_id=1, source_target_pairs={{0,12},{1,13},{2,14},{3,15},{4,8},{5,9},{6,10},{7,11},{8,4},{9,5},... | collective-permute-start | bytes 49160 | tf_op jit(solution)/shard_map/ppermute | solution.py:578
  22.7 0.0 collective-permute-done.7.refs_1_
  22.7 1.7 %collective-permute-done.8.refs_2_ = f32[16,256]{1,0:T(8,128)S(1)} collective-permute-done((f32[16,256]{1,0:T(8,128)S(1)}, f32[16,256]{1,0:T(8,128)S(1)}, u32[]{:S(2)}, u32[]{:S(2)}) %collective-permute-start.8) | collective-permute-done | bytes 16416 | tf_op jit(solution)/shard_map/ppermute | solution.py:578
  24.4 0.1 z_faces.3
  24.5 2.8 %collective-permute-start.9 = (f32[64,128]{1,0:T(8,128)S(1)}, f32[64,128]{1,0:T(8,128)S(1)}, u32[]{:S(2)}, u32[]{:S(2)}) collective-permute-start(f32[64,128]{1,0:T(8,128)S(1)} %get-tuple-element.67), channel_id=1, source_target_pairs={{0,1},{1,0},{2,3},{3,2},{4,5},{5,4},{6,7},{7,6},{8,9},{9,8},{10,11... | collective-permute-start | bytes 98312 | tf_op jit(solution)/shard_map/ppermute | solution.py:578
  27.3 0.2 collective-permute-start.10
  27.4 0.1 assemble.1.s_ref
  27.5 1.8 %collective-permute-done.9.z_low_ref = f32[64,128]{1,0:T(8,128)S(1)} collective-permute-done((f32[64,128]{1,0:T(8,128)S(1)}, f32[64,128]{1,0:T(8,128)S(1)}, u32[]{:S(2)}, u32[]{:S(2)}) %collective-permute-start.9) | collective-permute-done | bytes 32800 | tf_op jit(solution)/shard_map/ppermute | solution.py:578
  29.3 0.0 collective-permute-done.10.z_high_ref
  29.3 1.4 %final.1 = f32[8,48,256]{2,1,0:T(8,128)} custom-call(f32[8,48,256]{2,1,0:T(8,128)S(1)} %assemble.1.s_ref, f32[8,256]{1,0:T(8,128)S(1)} %get-tuple-element.66.tab_ref, f32[64,128]{1,0:T(8,128)S(1)} %collective-permute-done.9.z_low_ref, f32[64,128]{1,0:T(8,128)S(1)} %collective-permute-done.10.z_high_ref, f32[128,256]{1,0:T(8,128)S(1)} %get-tuple-element.38._.refs_0_, ...), custom_call_target="tpu_custom_call" | custom-call | flops 1400000000 | tf_op jit(solution)/shard_map/final/pallas_call | solution.py:505
  (3 shorter events, 0.0 us)
Async XLA Ops:
  0.0 0.7 %copy-start.6 = (f32[24,256]{1,0:T(8,128)S(1)}, f32[24,256]{1,0:T(8,128)}, u32[]{:S(2)}) copy-start(f32[24,256]{1,0:T(8,128)} %constant.2.clone.const_ref) | copy-start | bytes 73732
  0.0 1.0 %copy-start.1 = (f32[8,48,256]{2,1,0:T(8,128)S(1)}, f32[8,48,256]{2,1,0:T(8,128)}, u32[]{:S(2)}) copy-start(f32[8,48,256]{2,1,0:T(8,128)} %l_ref.1) | copy-start | bytes 1179652
  0.0 1.1 %copy-start = (f32[8,48,256]{2,1,0:T(8,128)S(1)}, f32[8,48,256]{2,1,0:T(8,128)}, u32[]{:S(2)}) copy-start(f32[8,48,256]{2,1,0:T(8,128)} %u_ref.1) | copy-start | bytes 1179652
  0.1 1.1 %copy-start.3 = (f32[1,6,32]{2,0,1:T(1,128)S(1)}, f32[1,6,32]{2,0,1:T(1,128)}, u32[]{:S(2)}) copy-start(f32[1,6,32]{2,0,1:T(1,128)} %param.9) | copy-start | bytes 2308
  0.1 1.1 %copy-start.4 = (f32[1,32]{1,0:T(1,128)S(1)}, f32[1,32]{1,0:T(1,128)}, u32[]{:S(2)}) copy-start(f32[1,32]{1,0:T(1,128)} %cinv_ref.1) | copy-start | bytes 388
  2.7 5.6 %collective-permute-start = (f32[48,256]{1,0:T(8,128)S(1)}, f32[48,256]{1,0:T(8,128)S(1)}, u32[]{:S(2)}, u32[]{:S(2)}) collective-permute-start(f32[48,256]{1,0:T(8,128)S(1)} %get-tuple-element.42), channel_id=1, source_target_pairs={{0,16},{1,17},{2,18},{3,19},{4,20},{5,21},{6,22},{7,23},{8,24},{9,... | collective-permute-start | bytes 147464 | tf_op jit(solution)/shard_map/ppermute | solution.py:578
  5.7 5.0 %collective-permute-start.3 = (f32[8,256]{1,0:T(8,128)S(1)}, f32[8,256]{1,0:T(8,128)S(1)}, u32[]{:S(2)}, u32[]{:S(2)}) collective-permute-start(f32[8,256]{1,0:T(8,128)S(1)} %get-tuple-element.41.tab_ref), channel_id=1, source_target_pairs={{0,2},{1,3},{2,0},{3,1},{4,6},{5,7},{6,4},{7,5},{8,10},{9,11},{10,... | collective-permute-start | bytes 24584 | tf_op jit(solution)/shard_map/ppermute | solution.py:578
  8.3 1.7 %copy-start.2 = (f32[8,8]{1,0:T(8,128)S(1)}, f32[8,8]{1,0:T(8,128)}, u32[]{:S(2)}) copy-start(f32[8,8]{1,0:T(8,128)} %basis_ref.1) | copy-start | bytes 772
  8.3 3.3 %collective-permute-start.2 = (f32[16,256]{1,0:T(8,128)S(1)}, f32[16,256]{1,0:T(8,128)S(1)}, u32[]{:S(2)}, u32[]{:S(2)}) collective-permute-start(f32[16,256]{1,0:T(8,128)S(1)} %get-tuple-element.47), channel_id=1, source_target_pairs={{0,12},{1,13},{2,14},{3,15},{4,8},{5,9},{6,10},{7,11},{8,4},{9,5},... | collective-permute-start | bytes 49160 | tf_op jit(solution)/shard_map/ppermute | solution.py:578
  8.8 1.2 %copy-start.5 = (f32[8]{0:T(128)S(1)}, f32[8]{0:T(128)}, u32[]{:S(2)}) copy-start(f32[8]{0:T(128)} %param.11) | copy-start | bytes 100
  8.8 2.9 %collective-permute-start.1 = (f32[16,256]{1,0:T(8,128)S(1)}, f32[16,256]{1,0:T(8,128)S(1)}, u32[]{:S(2)}, u32[]{:S(2)}) collective-permute-start(f32[16,256]{1,0:T(8,128)S(1)} %get-tuple-element.43._), channel_id=1, source_target_pairs={{0,4},{1,5},{2,6},{3,7},{4,0},{5,1},{6,2},{7,3},{8,12},{9,13},{10,... | collective-permute-start | bytes 49160 | tf_op jit(solution)/shard_map/ppermute | solution.py:578
  11.7 4.0 %collective-permute-start.4 = (f32[64,128]{1,0:T(8,128)S(1)}, f32[64,128]{1,0:T(8,128)S(1)}, u32[]{:S(2)}, u32[]{:S(2)}) collective-permute-start(f32[64,128]{1,0:T(8,128)S(1)} %get-tuple-element.55), channel_id=1, source_target_pairs={{0,1},{1,0},{2,3},{3,2},{4,5},{5,4},{6,7},{7,6},{8,9},{9,8},{10,11... | collective-permute-start | bytes 98312 | tf_op jit(solution)/shard_map/ppermute | solution.py:578
  13.4 2.3 %collective-permute-start.5 = (f32[64,128]{1,0:T(8,128)S(1)}, f32[64,128]{1,0:T(8,128)S(1)}, u32[]{:S(2)}, u32[]{:S(2)}) collective-permute-start(f32[64,128]{1,0:T(8,128)S(1)} %get-tuple-element.56), channel_id=1, source_target_pairs={{0,4},{1,2},{2,1},{3,7},{4,0},{5,6},{6,5},{7,3},{8,12},{9,10},{10,... | collective-permute-start | bytes 98312 | tf_op jit(solution)/shard_map/ppermute | solution.py:578
  16.9 4.2 %collective-permute-start.6 = (f32[56,256]{1,0:T(8,128)S(1)}, f32[56,256]{1,0:T(8,128)S(1)}, u32[]{:S(2)}, u32[]{:S(2)}) collective-permute-start(f32[56,256]{1,0:T(8,128)S(1)} %get-tuple-element.59), channel_id=1, source_target_pairs={{0,16},{1,17},{2,18},{3,19},{4,20},{5,21},{6,22},{7,23},{8,24},{9,... | collective-permute-start | bytes 172040 | tf_op jit(solution)/shard_map/ppermute | solution.py:578
  21.1 1.6 %collective-permute-start.7 = (f32[16,256]{1,0:T(8,128)S(1)}, f32[16,256]{1,0:T(8,128)S(1)}, u32[]{:S(2)}, u32[]{:S(2)}) collective-permute-start(f32[16,256]{1,0:T(8,128)S(1)} %get-tuple-element.62), channel_id=1, source_target_pairs={{0,4},{1,5},{2,6},{3,7},{4,0},{5,1},{6,2},{7,3},{8,12},{9,13},{10,... | collective-permute-start | bytes 49160 | tf_op jit(solution)/shard_map/ppermute | solution.py:578
  21.2 3.2 %collective-permute-start.8 = (f32[16,256]{1,0:T(8,128)S(1)}, f32[16,256]{1,0:T(8,128)S(1)}, u32[]{:S(2)}, u32[]{:S(2)}) collective-permute-start(f32[16,256]{1,0:T(8,128)S(1)} %get-tuple-element.63), channel_id=1, source_target_pairs={{0,12},{1,13},{2,14},{3,15},{4,8},{5,9},{6,10},{7,11},{8,4},{9,5},... | collective-permute-start | bytes 49160 | tf_op jit(solution)/shard_map/ppermute | solution.py:578
  24.5 4.8 %collective-permute-start.9 = (f32[64,128]{1,0:T(8,128)S(1)}, f32[64,128]{1,0:T(8,128)S(1)}, u32[]{:S(2)}, u32[]{:S(2)}) collective-permute-start(f32[64,128]{1,0:T(8,128)S(1)} %get-tuple-element.67), channel_id=1, source_target_pairs={{0,1},{1,0},{2,3},{3,2},{4,5},{5,4},{6,7},{7,6},{8,9},{9,8},{10,11... | collective-permute-start | bytes 98312 | tf_op jit(solution)/shard_map/ppermute | solution.py:578
  27.3 2.0 %collective-permute-start.10 = (f32[64,128]{1,0:T(8,128)S(1)}, f32[64,128]{1,0:T(8,128)S(1)}, u32[]{:S(2)}, u32[]{:S(2)}) collective-permute-start(f32[64,128]{1,0:T(8,128)S(1)} %get-tuple-element.68), channel_id=1, source_target_pairs={{0,4},{1,2},{2,1},{3,7},{4,0},{5,6},{6,5},{7,3},{8,12},{9,10},{10,... | collective-permute-start | bytes 98312 | tf_op jit(solution)/shard_map/ppermute | solution.py:578

commit v4 on v3

--- a/solution.py
+++ b/solution.py
@@ -53,6 +53,23 @@
     )
 
 
+def parts(a):
+    high = a.astype(jnp.bfloat16).astype(jnp.float32)
+    rest = a - high
+    middle = rest.astype(jnp.bfloat16).astype(jnp.float32)
+    return jnp.concatenate([high, middle, rest - middle], axis=0)
+
+
+def dot_weights(a, weights):
+    out = jnp.dot(parts(a).astype(jnp.bfloat16), weights.astype(jnp.bfloat16), preferred_element_type=jnp.float32)
+    rows = a.shape[0]
+    return out[:rows] + out[rows : 2 * rows] + out[2 * rows :]
+
+
+def weights_dot(weights, a):
+    return jnp.dot(weights.astype(jnp.bfloat16), parts(a).astype(jnp.bfloat16), preferred_element_type=jnp.float32)
+
+
 def iota(shape, dim):
     return lax.broadcasted_iota(jnp.int32, shape, dim)
 
@@ -102,15 +119,15 @@
     return jnp.where(jnp.abs(offset) <= 1, value, 0.0)
 
 
-def xy_weights(length_y, shape, y_dim, place, at_x, size_x):
+def xy_weights(size_x, size_y, point, place):
     count = lax.axis_size("gy")
     i, j = lax.axis_index("gx"), lax.axis_index("gy")
     off_x = place // count - i
     off_y = lax.rem(place % count - j + count + 1, count) - 1
-    y = coarse_weight(iota(shape, y_dim), length_y, False, False, off_y)
-    x = coarse_weight(
-        jnp.full(shape, at_x, jnp.int32), size_x, i == 0, is_last("gx"), off_x
-    )
+    kind = (point // size_y) % 3
+    at_x = jnp.where(kind == 0, 0, jnp.where(kind == 1, 1, size_x - 1))
+    y = coarse_weight(point % size_y, size_y, False, False, off_y)
+    x = coarse_weight(at_x, size_x, i == 0, is_last("gx"), off_x)
     return jnp.where((jnp.abs(off_x) <= 1) & (jnp.abs(off_y) <= 1), x * y, 0.0)
 
 
@@ -152,7 +169,8 @@
     return dot(coef, (iota((count, size_z), 0) == iota((count, size_z), 1) // NP).astype(jnp.float32))
 
 
-def terms_kernel(gossip, pairs_x, u_ref, l_ref, const_ref, coef_ref, cinv_ref, _, t_ref, yf_ref, zf_ref, *outs):
+def terms_kernel(gossip, pairs_x, u_ref, l_ref, const_ref, coef_ref, cinv_ref, *refs):
+    weights, (t_ref, yf_ref, zf_ref, *outs) = (refs[:3], refs[3:]) if gossip else ((), refs)
     size_x, size_y, size_z = u_ref.shape
     stiff_z, stiff_y, mass = const_parts(const_ref, size_y, size_z)
     coef = spread_coef(coef_ref, size_z) * HALF_WIDTH
@@ -173,54 +191,55 @@
     for ref, face in zip(outs, pair_payloads(t_ref[0], t_ref[size_x - 1], "gx", pairs_x)):
         ref[...] = face
     if gossip:
-        outs[pairs_x][...] = coarse_tables(t_ref, cinv_ref)
-
-
-def coarse_tables(t_ref, cinv_ref):
+        outs[pairs_x][...] = coarse_tables(t_ref, cinv_ref, *weights)
+
+
+def coarse_tables(t_ref, cinv_ref, sum_y_ref, sum_z_ref, place_ref):
     size_x, size_y, size_z = t_ref.shape
-    count_z = lax.axis_size("gz")
-    rows = lax.axis_size("gx") * lax.axis_size("gy")
-    device = (lax.axis_index("gx") * lax.axis_size("gy") + lax.axis_index("gy")) * count_z + lax.axis_index("gz")
+    rows, width = sum_y_ref.shape[0], cinv_ref.shape[1]
     middle = t_ref[1]
     for x in range(2, size_x - 1):
         middle = middle + t_ref[x]
-    total = jnp.zeros((rows, size_z), jnp.float32)
-    for at_x, plane in ((0, t_ref[0]), (1, middle), (size_x - 1, t_ref[size_x - 1])):
-        w = xy_weights(size_y, (rows, size_y), 1, iota((rows, size_y), 0), at_x, size_x)
-        total = total + dot(w, plane)
-    lane = iota((size_z, LANES), 1)
-    w = z_weights(size_z, lane % count_z, (size_z, LANES), 0)
-    points = size_x * size_y * size_z
-    part = dot(total, jnp.where(lane // count_z == device, w, 0.0)) / points
-    width = rows * count_z
+    planes = jnp.concatenate([t_ref[0], middle, t_ref[size_x - 1]], axis=0)
+    total = weights_dot(sum_y_ref[...], planes)
+    part = dot_weights(total, sum_z_ref[...]) / (size_x * size_y * size_z)
     row = jnp.broadcast_to(cinv_ref[...], (rows, width))
-    row = jnp.where(iota((rows, width), 1) // count_z == iota((rows, width), 0), row, 0.0)
-    lane = iota((width, LANES), 1)
-    place = (lane // count_z == device) & (lane % count_z == iota((width, LANES), 0) % count_z)
-    inverse = dot(row, place.astype(jnp.float32))
-    return jnp.concatenate([part, inverse], axis=1)
-
-
-def coarse_weights(size_x, size_z, line_ref, plane_ref, same_ref):
+    row = jnp.where(iota((rows, width), 1) // (width // rows) == iota((rows, width), 0), row, 0.0)
+    return jnp.concatenate([part, dot_weights(row, place_ref[...])], axis=1)
+
+
+def coarse_weights(size_x, size_z, line_ref, plane_ref, same_ref, sum_y_ref, sum_z_ref, place_ref):
     count_z = lax.axis_size("gz")
     shape = line_ref.shape
     line_ref[...] = z_weights(size_z, (iota(shape, 0) // count_z) % count_z, shape, 1)
     square = same_ref.shape
     same_ref[...] = (iota(square, 0) % count_z == iota(square, 1) % count_z).astype(jnp.float32)
-    _, size_y, rows = plane_ref.shape
-    for n, at_x in enumerate((0, 1, size_x - 1)):
-        plane_ref[n] = xy_weights(size_y, (size_y, rows), 0, iota((size_y, rows), 1), at_x, size_x)
+    size_y = plane_ref.shape[0] // 3
+    rows = sum_y_ref.shape[0]
+    shape = plane_ref.shape
+    plane_ref[...] = xy_weights(size_x, size_y, iota(shape, 0), iota(shape, 1) % rows)
+    shape = sum_y_ref.shape
+    sum_y_ref[...] = xy_weights(size_x, size_y, iota(shape, 1), iota(shape, 0))
+    device = (lax.axis_index("gx") * lax.axis_size("gy") + lax.axis_index("gy")) * count_z + lax.axis_index("gz")
+    lane = iota((size_z, LANES), 1)
+    w = z_weights(size_z, lane % count_z, (size_z, LANES), 0)
+    sum_z_ref[...] = jnp.where(lane // count_z == device, w, 0.0)
+    shape = place_ref.shape
+    lane = iota(shape, 1)
+    place = (lane // count_z == device) & (lane % count_z == iota(shape, 0) % count_z)
+    place_ref[...] = place.astype(jnp.float32)
 
 
 def coarse_planes(tab, line_ref, plane_ref, same_ref):
     count_z = lax.axis_size("gz")
     rows = tab.shape[0]
-    rhs = dot(tab[:, :LANES], same_ref[...])
+    rhs = dot_weights(tab[:, :LANES], same_ref[...])
     value = jnp.sum(rhs * tab[:, LANES:], axis=0, keepdims=True)
     value = jnp.broadcast_to(value, (rows, LANES))
     value = jnp.where(iota((rows, LANES), 1) // (count_z * count_z) == iota((rows, LANES), 0), value, 0.0)
-    line = dot(value, line_ref[...])
-    return [dot(plane_ref[n], line) for n in range(3)]
+    planes = weights_dot(plane_ref[...], dot_weights(value, line_ref[...]))
+    size_y = plane_ref.shape[0] // 3
+    return [planes[n * size_y : (n + 1) * size_y] for n in range(3)]
 
 
 def y_kernel(gossip, pairs_x, table_in_x, yf_ref, tab_ref, *refs):
@@ -596,18 +615,18 @@
         return send(out[:2], perms_z), out[-1] if gossip else tab
 
     coef = element_coef.reshape(size_y // NP, 1, size_z // NP)
-    weights = []
+    weights, rows = [], sizes[0] * sizes[1]
     if gossip:
         weights = call(
             functools.partial(coarse_weights, size_x, size_z),
             "weights",
             [],
-            [(LANES, size_z), (3, size_y, sizes[0] * sizes[1]), (LANES, LANES)],
+            [(LANES, size_z), (3 * size_y, 3 * rows), (LANES, LANES), (rows, 9 * size_y), (size_z, LANES), (rows * sizes[2], LANES)],
         )
     terms, y_faces, z_faces, *rest = call(
         functools.partial(terms_kernel, gossip, pairs_x),
         "terms",
-        [fluidity, local_fluidity, const, coef, coarse_inverse, weights[0] if gossip else coef],
+        [fluidity, local_fluidity, const, coef, coarse_inverse, *weights[3:]],
         [shape] + face_shapes + [(size_y, size_z)] * pairs_x + tab_shapes,
     )
     x_got = send(rest[:pairs_x], perms_x)
@@ -650,7 +669,7 @@
     return call(
         functools.partial(final_kernel, gossip),
         "final",
-        [solved, coarse, *z_got, *weights],
+        [solved, coarse, *z_got, *weights[:3]],
         [shape],
         scratch=[shape, pltpu.SemaphoreType.DMA((size_x,))],
         out_spec=HBM,

time: 30.8 us -> 30.5 us (level)
  no operation moved by 1% of the time
where the time goes in v4:
time: 30.5 us; the launch traced here: 30.4 us
  starting transfers between devices  15 us (49%)
  Pallas kernels  7.71 us (25%)
  waiting for transfers between devices  6.69 us (22%)
  local copies, waits for them, and re-layouts  0.79 us (3%)
    ppermute x11, starting transfers between devices, send(): return [lax.ppermute(p, AXES, q) for p, q in zip(payloads, pairs)]  15 us
    pallas_call x13, Pallas kernels, call(): pl.pallas_call(kernel, name=name, out_shape=[jax.ShapeDtypeStruct(s, jnp....  7.71 us
    ppermute x11, waiting for transfers between devices, send(): return [lax.ppermute(p, AXES, q) for p, q in zip(payloads, pairs)]  6.69 us
    unnamed x14, local copies, waits for them, and re-layouts  0.79 us
  transfers between devices with their start and end apart: 11, of which 5 were waited for; matrix products, arithmetic and copies ran while one was open for 0% of the time, Pallas kernels for 11%

profile of v4, /device:TPU:0, one launch (start us, length us, event | category | flops | bytes accessed | tf_op | source)
XLA Modules:
  0.0 30.4 jit_solution(637094239417440844)
XLA Ops:
  0.0 0.0 copy-start.6
  0.0 0.0 copy-start.1
  0.0 0.0 copy-start
  0.0 0.3 %weights.1 = (f32[128,256]{1,0:T(8,128)S(1)}, f32[144,24]{1,0:T(8,128)S(1)}, f32[128,128]{1,0:T(8,128)S(1)}, f32[8,432]{1,0:T(8,128)S(1)}, f32[256,128]{1,0:T(8,128)S(1)}, /*index=5*/f32[32,128]{1,0:T(8,128)S(1)}) custom-call(), custom_call_target="tpu_custom_call" | custom-call | flops 1500000000 | tf_op jit(solution)/shard_map/weights/pallas_call | solution.py:524
  0.3 0.0 copy-start.3
  0.4 0.0 copy-start.4
  0.4 0.4 %copy-done.6 = f32[24,256]{1,0:T(8,128)S(1)} copy-done((f32[24,256]{1,0:T(8,128)S(1)}, f32[24,256]{1,0:T(8,128)}, u32[]{:S(2)}) %copy-start.6) | copy-done | bytes 24600
  0.7 0.3 copy-done.1
  1.0 0.1 copy-done
  1.1 0.0 copy-done.3
  1.1 0.0 copy-done.4
  1.1 1.4 %terms.1 = (f32[8,48,256]{2,1,0:T(8,128)S(1)}, f32[2,8,256]{2,1,0:T(8,128)S(1)}, f32[2,48,128]{2,1,0:T(8,128)S(1)}, f32[48,256]{1,0:T(8,128)S(1)}, f32[8,256]{1,0:T(8,128)S(1)}) custom-call(f32[8,48,256]{2,1,0:T(8,128)S(1)} %copy-done, f32[8,48,256]{2,1,0:T(8,128)S(1)} %copy-done.1, f32[24,256]{1,0:T(8,128)S(1)} %copy-done.6, f32[6,1,32]{2,1,0:T(1,128)S(1)} %bitcast.2, ...), custom_call_target="tpu_custom_call" | custom-call | flops 1700000000 | tf_op jit(solution)/shard_map/terms/pallas_call | solution.py:524
  2.5 3.0 %collective-permute-start = (f32[48,256]{1,0:T(8,128)S(1)}, f32[48,256]{1,0:T(8,128)S(1)}, u32[]{:S(2)}, u32[]{:S(2)}) collective-permute-start(f32[48,256]{1,0:T(8,128)S(1)} %get-tuple-element.47), channel_id=1, source_target_pairs={{0,16},{1,17},{2,18},{3,19},{4,20},{5,21},{6,22},{7,23},{8,24},{9,... | collective-permute-start | bytes 147464 | tf_op jit(solution)/shard_map/ppermute | solution.py:597
  5.5 2.6 %collective-permute-start.3 = (f32[8,256]{1,0:T(8,128)S(1)}, f32[8,256]{1,0:T(8,128)S(1)}, u32[]{:S(2)}, u32[]{:S(2)}) collective-permute-start(f32[8,256]{1,0:T(8,128)S(1)} %get-tuple-element.46.tab_ref), channel_id=1, source_target_pairs={{0,2},{1,3},{2,0},{3,1},{4,6},{5,7},{6,4},{7,5},{8,10},{9,11},{10,... | collective-permute-start | bytes 24584 | tf_op jit(solution)/shard_map/ppermute | solution.py:597
  8.1 0.0 collective-permute-done.refs_0_
  8.1 0.0 copy-start.2
  8.2 0.5 %collective-permute-start.2 = (f32[16,256]{1,0:T(8,128)S(1)}, f32[16,256]{1,0:T(8,128)S(1)}, u32[]{:S(2)}, u32[]{:S(2)}) collective-permute-start(f32[16,256]{1,0:T(8,128)S(1)} %get-tuple-element.52), channel_id=1, source_target_pairs={{0,12},{1,13},{2,14},{3,15},{4,8},{5,9},{6,10},{7,11},{8,4},{9,5},... | collective-permute-start | bytes 49160 | tf_op jit(solution)/shard_map/ppermute | solution.py:597
  8.6 0.0 copy-start.5
  8.6 1.2 %collective-permute-start.1 = (f32[16,256]{1,0:T(8,128)S(1)}, f32[16,256]{1,0:T(8,128)S(1)}, u32[]{:S(2)}, u32[]{:S(2)}) collective-permute-start(f32[16,256]{1,0:T(8,128)S(1)} %get-tuple-element.48._), channel_id=1, source_target_pairs={{0,4},{1,5},{2,6},{3,7},{4,0},{5,1},{6,2},{7,3},{8,12},{9,13},{10,... | collective-permute-start | bytes 49160 | tf_op jit(solution)/shard_map/ppermute | solution.py:597
  9.9 0.0 copy-done.2
  9.9 0.0 copy-done.5
  9.9 0.7 %operators.1 = (f32[256,256]{1,0:T(8,128)S(1)}, f32[256,256]{1,0:T(8,128)S(1)}, f32[48,48]{1,0:T(8,128)S(1)}, f32[48,48]{1,0:T(8,128)S(1)}, f32[128,128]{1,0:T(8...) custom-call(f32[8,8]{1,0:T(8,128)S(1)} %copy-done.2, f32[1,8]{1,0:T(1,128)S(1)} %bitcast.4, ...), custom_call_target="tpu_custom_call" | custom-call | flops 10000000 | tf_op jit(solution)/shard_map/operators/pallas_call | solution.py:524
  10.6 0.0 collective-permute-done.3.far_ref
  10.6 0.9 %collective-permute-done.2.refs_2_ = f32[16,256]{1,0:T(8,128)S(1)} collective-permute-done((f32[16,256]{1,0:T(8,128)S(1)}, f32[16,256]{1,0:T(8,128)S(1)}, u32[]{:S(2)}, u32[]{:S(2)}) %collective-permute-start.2) | collective-permute-done | bytes 16416 | tf_op jit(solution)/shard_map/ppermute | solution.py:597
  11.5 0.0 collective-permute-done.1.refs_1_
  11.5 0.1 z_faces.2
  11.6 1.6 %collective-permute-start.4 = (f32[64,128]{1,0:T(8,128)S(1)}, f32[64,128]{1,0:T(8,128)S(1)}, u32[]{:S(2)}, u32[]{:S(2)}) collective-permute-start(f32[64,128]{1,0:T(8,128)S(1)} %get-tuple-element.60), channel_id=1, source_target_pairs={{0,1},{1,0},{2,3},{3,2},{4,5},{5,4},{6,7},{7,6},{8,9},{9,8},{10,11... | collective-permute-start | bytes 98312 | tf_op jit(solution)/shard_map/ppermute | solution.py:597
  13.2 0.0 collective-permute-start.5
  13.2 1.0 %forward.1.s_ref = f32[8,48,256]{2,1,0:T(8,128)S(1)} custom-call(f32[8,48,256]{2,1,0:T(8,128)S(1)} %get-tuple-element.44.t_ref, f32[256,256]{1,0:T(8,128)S(1)} %get-tuple-element.49.pz_ref, f32[48,48]{1,0:T(8,128)S(1)} %get-tuple-element.50.pyt_ref, f32[64,256]{1,0:T(8,128)S(1)} %get-tuple-element.51.entry_ref, f32[48,256]{1,0:T(8,128)S(1)} %collective-permute-done.refs_0_, ...), custom_call_target="tpu_custom_call" | custom-call | flops 1100000000 | tf_op jit(solution)/shard_map/forward/pallas_call | solution.py:524
  14.3 1.3 %collective-permute-done.4.refs_0_ = f32[64,128]{1,0:T(8,128)S(1)} collective-permute-done((f32[64,128]{1,0:T(8,128)S(1)}, f32[64,128]{1,0:T(8,128)S(1)}, u32[]{:S(2)}, u32[]{:S(2)}) %collective-permute-start.4) | collective-permute-done | bytes 32800 | tf_op jit(solution)/shard_map/ppermute | solution.py:597
  15.6 0.0 collective-permute-done.5.refs_1_
  15.6 1.1 %middle.1 = (f32[8,48,256]{2,1,0:T(8,128)S(1)}, f32[56,256]{1,0:T(8,128)S(1)}, f32[8,256]{1,0:T(8,128)S(1)}) custom-call(f32[8,48,256]{2,1,0:T(8,128)S(1)} %forward.1.s_ref, f32[256,256]{1,0:T(8,128)S(1)} %get-tuple-element.49.pz_ref, f32[256,256]{1,0:T(8,128)S(1)} %get-tuple-element.53.pzt_ref, f32[48,48]{1,0:T(8,128)S(1)} %get-tuple-element.54.py_ref, ...), custom_call_target="tpu_custom_call" | custom-call | flops 1200000000 | tf_op jit(solution)/shard_map/middle/pallas_call | solution.py:524
  16.7 1.6 %collective-permute-start.6 = (f32[56,256]{1,0:T(8,128)S(1)}, f32[56,256]{1,0:T(8,128)S(1)}, u32[]{:S(2)}, u32[]{:S(2)}) collective-permute-start(f32[56,256]{1,0:T(8,128)S(1)} %get-tuple-element.64), channel_id=1, source_target_pairs={{0,16},{1,17},{2,18},{3,19},{4,20},{5,21},{6,22},{7,23},{8,24},{9,... | collective-permute-start | bytes 172040 | tf_op jit(solution)/shard_map/ppermute | solution.py:597
  18.3 1.7 %inverse.1 = (f32[8,48,256]{2,1,0:T(8,128)S(1)}, f32[2,8,256]{2,1,0:T(8,128)S(1)}, f32[2,48,128]{2,1,0:T(8,128)S(1)}) custom-call(f32[8,48,256]{2,1,0:T(8,128)S(1)} %get-tuple-element.62.half_ref, f32[256,256]{1,0:T(8,128)S(1)} %get-tuple-element.53.pzt_ref, f32[48,48]{1,0:T(8,128)S(1)} %get-tuple-element.54.py_ref, f32[64,256]{1,0:T(8,128)S(1)} %get-tuple-element.51.entry_ref), custom_call_target="tpu_custom_call" | custom-call | flops 1800000000 | tf_op jit(solution)/shard_map/inverse/pallas_call | solution.py:524
  19.9 1.0 %collective-permute-done.6.refs_0_ = f32[56,256]{1,0:T(8,128)S(1)} collective-permute-done((f32[56,256]{1,0:T(8,128)S(1)}, f32[56,256]{1,0:T(8,128)S(1)}, u32[]{:S(2)}, u32[]{:S(2)}) %collective-permute-start.6) | collective-permute-done | bytes 57376 | tf_op jit(solution)/shard_map/ppermute | solution.py:597
  21.0 0.1 collective-permute-start.7
  21.0 1.5 %collective-permute-start.8 = (f32[16,256]{1,0:T(8,128)S(1)}, f32[16,256]{1,0:T(8,128)S(1)}, u32[]{:S(2)}, u32[]{:S(2)}) collective-permute-start(f32[16,256]{1,0:T(8,128)S(1)} %get-tuple-element.68), channel_id=1, source_target_pairs={{0,12},{1,13},{2,14},{3,15},{4,8},{5,9},{6,10},{7,11},{8,4},{9,5},... | collective-permute-start | bytes 49160 | tf_op jit(solution)/shard_map/ppermute | solution.py:597
  22.6 0.0 collective-permute-done.7.refs_1_
  22.6 1.7 %collective-permute-done.8.refs_2_ = f32[16,256]{1,0:T(8,128)S(1)} collective-permute-done((f32[16,256]{1,0:T(8,128)S(1)}, f32[16,256]{1,0:T(8,128)S(1)}, u32[]{:S(2)}, u32[]{:S(2)}) %collective-permute-start.8) | collective-permute-done | bytes 16416 | tf_op jit(solution)/shard_map/ppermute | solution.py:597
  24.3 0.1 z_faces.3
  24.4 2.8 %collective-permute-start.9 = (f32[64,128]{1,0:T(8,128)S(1)}, f32[64,128]{1,0:T(8,128)S(1)}, u32[]{:S(2)}, u32[]{:S(2)}) collective-permute-start(f32[64,128]{1,0:T(8,128)S(1)} %get-tuple-element.72), channel_id=1, source_target_pairs={{0,1},{1,0},{2,3},{3,2},{4,5},{5,4},{6,7},{7,6},{8,9},{9,8},{10,11... | collective-permute-start | bytes 98312 | tf_op jit(solution)/shard_map/ppermute | solution.py:597
  27.1 0.2 collective-permute-start.10
  27.3 0.1 assemble.1.s_ref
  27.4 1.8 %collective-permute-done.9.z_low_ref = f32[64,128]{1,0:T(8,128)S(1)} collective-permute-done((f32[64,128]{1,0:T(8,128)S(1)}, f32[64,128]{1,0:T(8,128)S(1)}, u32[]{:S(2)}, u32[]{:S(2)}) %collective-permute-start.9) | collective-permute-done | bytes 32800 | tf_op jit(solution)/shard_map/ppermute | solution.py:597
  29.1 0.0 collective-permute-done.10.z_high_ref
  29.1 1.2 %final.1 = f32[8,48,256]{2,1,0:T(8,128)} custom-call(f32[8,48,256]{2,1,0:T(8,128)S(1)} %assemble.1.s_ref, f32[8,256]{1,0:T(8,128)S(1)} %get-tuple-element.71.tab_ref, f32[64,128]{1,0:T(8,128)S(1)} %collective-permute-done.9.z_low_ref, f32[64,128]{1,0:T(8,128)S(1)} %collective-permute-done.10.z_high_ref, f32[128,256]{1,0:T(8,128)S(1)} %get-tuple-element.74.refs_0_, ...), custom_call_target="tpu_custom_call" | custom-call | flops 1400000000 | tf_op jit(solution)/shard_map/final/pallas_call | solution.py:524
  (3 shorter events, 0.0 us)
Async XLA Ops:
  0.0 0.7 %copy-start.6 = (f32[24,256]{1,0:T(8,128)S(1)}, f32[24,256]{1,0:T(8,128)}, u32[]{:S(2)}) copy-start(f32[24,256]{1,0:T(8,128)} %constant.2.clone.const_ref) | copy-start | bytes 73732
  0.0 1.0 %copy-start.1 = (f32[8,48,256]{2,1,0:T(8,128)S(1)}, f32[8,48,256]{2,1,0:T(8,128)}, u32[]{:S(2)}) copy-start(f32[8,48,256]{2,1,0:T(8,128)} %l_ref.1) | copy-start | bytes 1179652
  0.0 1.1 %copy-start = (f32[8,48,256]{2,1,0:T(8,128)S(1)}, f32[8,48,256]{2,1,0:T(8,128)}, u32[]{:S(2)}) copy-start(f32[8,48,256]{2,1,0:T(8,128)} %u_ref.1) | copy-start | bytes 1179652
  0.3 0.8 %copy-start.3 = (f32[1,6,32]{2,0,1:T(1,128)S(1)}, f32[1,6,32]{2,0,1:T(1,128)}, u32[]{:S(2)}) copy-start(f32[1,6,32]{2,0,1:T(1,128)} %param.9) | copy-start | bytes 2308
  0.4 0.8 %copy-start.4 = (f32[1,32]{1,0:T(1,128)S(1)}, f32[1,32]{1,0:T(1,128)}, u32[]{:S(2)}) copy-start(f32[1,32]{1,0:T(1,128)} %cinv_ref.1) | copy-start | bytes 388
  2.5 5.6 %collective-permute-start = (f32[48,256]{1,0:T(8,128)S(1)}, f32[48,256]{1,0:T(8,128)S(1)}, u32[]{:S(2)}, u32[]{:S(2)}) collective-permute-start(f32[48,256]{1,0:T(8,128)S(1)} %get-tuple-element.47), channel_id=1, source_target_pairs={{0,16},{1,17},{2,18},{3,19},{4,20},{5,21},{6,22},{7,23},{8,24},{9,... | collective-permute-start | bytes 147464 | tf_op jit(solution)/shard_map/ppermute | solution.py:597
  5.5 5.0 %collective-permute-start.3 = (f32[8,256]{1,0:T(8,128)S(1)}, f32[8,256]{1,0:T(8,128)S(1)}, u32[]{:S(2)}, u32[]{:S(2)}) collective-permute-start(f32[8,256]{1,0:T(8,128)S(1)} %get-tuple-element.46.tab_ref), channel_id=1, source_target_pairs={{0,2},{1,3},{2,0},{3,1},{4,6},{5,7},{6,4},{7,5},{8,10},{9,11},{10,... | collective-permute-start | bytes 24584 | tf_op jit(solution)/shard_map/ppermute | solution.py:597
  8.1 1.7 %copy-start.2 = (f32[8,8]{1,0:T(8,128)S(1)}, f32[8,8]{1,0:T(8,128)}, u32[]{:S(2)}) copy-start(f32[8,8]{1,0:T(8,128)} %basis_ref.1) | copy-start | bytes 772
  8.2 3.3 %collective-permute-start.2 = (f32[16,256]{1,0:T(8,128)S(1)}, f32[16,256]{1,0:T(8,128)S(1)}, u32[]{:S(2)}, u32[]{:S(2)}) collective-permute-start(f32[16,256]{1,0:T(8,128)S(1)} %get-tuple-element.52), channel_id=1, source_target_pairs={{0,12},{1,13},{2,14},{3,15},{4,8},{5,9},{6,10},{7,11},{8,4},{9,5},... | collective-permute-start | bytes 49160 | tf_op jit(solution)/shard_map/ppermute | solution.py:597
  8.6 1.2 %copy-start.5 = (f32[8]{0:T(128)S(1)}, f32[8]{0:T(128)}, u32[]{:S(2)}) copy-start(f32[8]{0:T(128)} %param.11) | copy-start | bytes 100
  8.6 2.9 %collective-permute-start.1 = (f32[16,256]{1,0:T(8,128)S(1)}, f32[16,256]{1,0:T(8,128)S(1)}, u32[]{:S(2)}, u32[]{:S(2)}) collective-permute-start(f32[16,256]{1,0:T(8,128)S(1)} %get-tuple-element.48._), channel_id=1, source_target_pairs={{0,4},{1,5},{2,6},{3,7},{4,0},{5,1},{6,2},{7,3},{8,12},{9,13},{10,... | collective-permute-start | bytes 49160 | tf_op jit(solution)/shard_map/ppermute | solution.py:597
  11.6 4.0 %collective-permute-start.4 = (f32[64,128]{1,0:T(8,128)S(1)}, f32[64,128]{1,0:T(8,128)S(1)}, u32[]{:S(2)}, u32[]{:S(2)}) collective-permute-start(f32[64,128]{1,0:T(8,128)S(1)} %get-tuple-element.60), channel_id=1, source_target_pairs={{0,1},{1,0},{2,3},{3,2},{4,5},{5,4},{6,7},{7,6},{8,9},{9,8},{10,11... | collective-permute-start | bytes 98312 | tf_op jit(solution)/shard_map/ppermute | solution.py:597
  13.2 2.3 %collective-permute-start.5 = (f32[64,128]{1,0:T(8,128)S(1)}, f32[64,128]{1,0:T(8,128)S(1)}, u32[]{:S(2)}, u32[]{:S(2)}) collective-permute-start(f32[64,128]{1,0:T(8,128)S(1)} %get-tuple-element.61), channel_id=1, source_target_pairs={{0,4},{1,2},{2,1},{3,7},{4,0},{5,6},{6,5},{7,3},{8,12},{9,10},{10,... | collective-permute-start | bytes 98312 | tf_op jit(solution)/shard_map/ppermute | solution.py:597
  16.7 4.2 %collective-permute-start.6 = (f32[56,256]{1,0:T(8,128)S(1)}, f32[56,256]{1,0:T(8,128)S(1)}, u32[]{:S(2)}, u32[]{:S(2)}) collective-permute-start(f32[56,256]{1,0:T(8,128)S(1)} %get-tuple-element.64), channel_id=1, source_target_pairs={{0,16},{1,17},{2,18},{3,19},{4,20},{5,21},{6,22},{7,23},{8,24},{9,... | collective-permute-start | bytes 172040 | tf_op jit(solution)/shard_map/ppermute | solution.py:597
  21.0 1.6 %collective-permute-start.7 = (f32[16,256]{1,0:T(8,128)S(1)}, f32[16,256]{1,0:T(8,128)S(1)}, u32[]{:S(2)}, u32[]{:S(2)}) collective-permute-start(f32[16,256]{1,0:T(8,128)S(1)} %get-tuple-element.67), channel_id=1, source_target_pairs={{0,4},{1,5},{2,6},{3,7},{4,0},{5,1},{6,2},{7,3},{8,12},{9,13},{10,... | collective-permute-start | bytes 49160 | tf_op jit(solution)/shard_map/ppermute | solution.py:597
  21.0 3.2 %collective-permute-start.8 = (f32[16,256]{1,0:T(8,128)S(1)}, f32[16,256]{1,0:T(8,128)S(1)}, u32[]{:S(2)}, u32[]{:S(2)}) collective-permute-start(f32[16,256]{1,0:T(8,128)S(1)} %get-tuple-element.68), channel_id=1, source_target_pairs={{0,12},{1,13},{2,14},{3,15},{4,8},{5,9},{6,10},{7,11},{8,4},{9,5},... | collective-permute-start | bytes 49160 | tf_op jit(solution)/shard_map/ppermute | solution.py:597
  24.4 4.8 %collective-permute-start.9 = (f32[64,128]{1,0:T(8,128)S(1)}, f32[64,128]{1,0:T(8,128)S(1)}, u32[]{:S(2)}, u32[]{:S(2)}) collective-permute-start(f32[64,128]{1,0:T(8,128)S(1)} %get-tuple-element.72), channel_id=1, source_target_pairs={{0,1},{1,0},{2,3},{3,2},{4,5},{5,4},{6,7},{7,6},{8,9},{9,8},{10,11... | collective-permute-start | bytes 98312 | tf_op jit(solution)/shard_map/ppermute | solution.py:597
  27.1 2.0 %collective-permute-start.10 = (f32[64,128]{1,0:T(8,128)S(1)}, f32[64,128]{1,0:T(8,128)S(1)}, u32[]{:S(2)}, u32[]{:S(2)}) collective-permute-start(f32[64,128]{1,0:T(8,128)S(1)} %get-tuple-element.73), channel_id=1, source_target_pairs={{0,4},{1,2},{2,1},{3,7},{4,0},{5,6},{6,5},{7,3},{8,12},{9,10},{10,... | collective-permute-start | bytes 98312 | tf_op jit(solution)/shard_map/ppermute | solution.py:597

commit v5 on v4

--- a/solution.py
+++ b/solution.py
@@ -267,24 +267,66 @@
     out_ref[...] = merge(tab_ref[...], far_ref[...])
 
 
-def z_kernel(gossip, pairs_x, zf_ref, tab_ref, *refs):
-    size_y = zf_ref.shape[1]
+def x_lanes_kept(lane, size_x):
+    keep = (lane % NP != 0) | (lax.axis_index("gx") != 0)
+    return keep & ((lane % NP != size_x - 1) | jnp.logical_not(is_last("gx"))) & (lane < 2 * NP)
+
+
+def ahead_kernel(pairs_x, zf_ref, pyt_ref, px_ref, *refs):
+    x_refs, out_ref = refs[:pairs_x], refs[-1]
+    _, size_y, _ = zf_ref.shape
+    size_x, size_z = NP, x_refs[0].shape[1]
+    lane = iota((size_y, LANES), 1)
+    faces = []
+    for side, at in ((0, 0), (1, size_z - 1)):
+        x_low, x_high = low_high([r[0:size_y, at : at + 1] for r in x_refs], "gx")
+        face = zf_ref[side]
+        faces.append(face + jnp.where(lane == 0, x_low, 0.0) + jnp.where(lane == size_x - 1, x_high, 0.0))
+    both = jnp.where(lane < NP, faces[0], pltpu.roll(faces[1], NP, 1))
+    both = jnp.where(x_lanes_kept(lane, size_x), both, 0.0)
+    out_ref[...] = dot(dot(pyt_ref[...], both), px_ref[...])
+
+
+def transformed_faces(ahead_ref, pyt_ref, px_ref, y_refs, size_x):
+    size_y, size_z = ahead_ref.shape[0], y_refs[0].shape[1]
+    at_lane = iota((size_x, LANES), 1)
+    lines = []
+    for side in range(2):
+        lines.append(jnp.zeros((1, LANES), jnp.float32))
+        for half, at in ((0, 0), (1, size_z - 1)):
+            column = low_high([r[0:size_x, at : at + 1] for r in y_refs], "gy")[side]
+            here = at_lane == iota((size_x, LANES), 0) + half * NP
+            lines[side] = lines[side] + jnp.sum(jnp.where(here, column, 0.0), axis=0, keepdims=True)
+    row = iota((NP, LANES), 0)
+    pair = jnp.where(row == 0, lines[0], jnp.where(row == 1, lines[1], 0.0))
+    pair = jnp.where(x_lanes_kept(iota((NP, LANES), 1), size_x), pair, 0.0)
+    pair = dot(pair, px_ref[...])
+    both = ahead_ref[...] + pyt_ref[:, 0:1] * pair[0:1, :] + pyt_ref[:, size_y - 1 : size_y] * pair[1:2, :]
+    return both, pltpu.roll(both, LANES - NP, 1)
+
+
+def z_kernel(gossip, pairs_x, transformed, zf_ref, tab_ref, *refs):
+    operators, refs = refs[:transformed], refs[transformed:]
     x_refs, y_refs, refs = refs[:pairs_x], refs[pairs_x : pairs_x + 2], refs[pairs_x + 2 :]
     size_x = y_refs[0].shape[0] - (NP if gossip else 0)
     size_z = y_refs[0].shape[1]
-    lane = iota((size_y, LANES), 1)
-    row = iota((size_y, LANES), 0)
-    diagonal = iota((size_x, LANES), 0) == iota((size_x, LANES), 1)
-    faces = []
-    for side, at in ((0, 0), (1, size_z - 1)):
-        x_low, x_high = low_high([r[0:size_y, at : at + 1] for r in x_refs], "gx")
-        y_low, y_high = low_high([r[0:size_x, at : at + 1] for r in y_refs], "gy")
-        face = zf_ref[side]
-        face = face + jnp.where(lane == 0, x_low, 0.0) + jnp.where(lane == size_x - 1, x_high, 0.0)
-        for at_y, column in ((0, y_low), (size_y - 1, y_high)):
-            line = jnp.sum(jnp.where(diagonal, column, 0.0), axis=0, keepdims=True)
-            face = face + jnp.where(row == at_y, line, 0.0)
-        faces.append(face)
+    size_y = refs[0].shape[0] - (2 * NP if gossip else 0)
+    if transformed:
+        faces = transformed_faces(zf_ref, *operators, y_refs, size_x)
+    else:
+        lane = iota((size_y, LANES), 1)
+        row = iota((size_y, LANES), 0)
+        diagonal = iota((size_x, LANES), 0) == iota((size_x, LANES), 1)
+        faces = []
+        for side, at in ((0, 0), (1, size_z - 1)):
+            x_low, x_high = low_high([r[0:size_y, at : at + 1] for r in x_refs], "gx")
+            y_low, y_high = low_high([r[0:size_x, at : at + 1] for r in y_refs], "gy")
+            face = zf_ref[side]
+            face = face + jnp.where(lane == 0, x_low, 0.0) + jnp.where(lane == size_x - 1, x_high, 0.0)
+            for at_y, column in ((0, y_low), (size_y - 1, y_high)):
+                line = jnp.sum(jnp.where(diagonal, column, 0.0), axis=0, keepdims=True)
+                face = face + jnp.where(row == at_y, line, 0.0)
+            faces.append(face)
     for ref, face in zip(refs, pair_payloads(faces[0], faces[1], "gz", 2)):
         ref[0:size_y, :] = face
     if gossip:
@@ -418,13 +460,13 @@
             s_ref[a, rows, :] = total
 
 
-def middle_kernel(gossip, pairs_x, s_ref, pz_ref, pzt_ref, py_ref, pyt_ref, px_ref, entry_ref, inv_ref, tab_ref, *refs):
+def middle_kernel(gossip, pairs_x, s_ref, pz_ref, pzt_ref, py_ref, entry_ref, inv_ref, tab_ref, *refs):
     shape = size_x, size_y, size_z = s_ref.shape
     z_refs, half_ref, outs = refs[:2], refs[2], refs[3:]
-    low, high = z_halos(shape, z_refs)
+    low, high = low_high([r[0:size_y, :] for r in z_refs], "gz")
+    low = jnp.where(lax.axis_index("gz") != 0, low, 0.0)
+    high = jnp.where(is_last("gz"), 0.0, high)
     both = jnp.where(iota((size_y, LANES), 1) < NP, low, pltpu.roll(high, NP, 1))
-    both = jnp.where(iota((size_y, LANES), 1) < 2 * NP, both, 0.0)
-    both = dot(dot(pyt_ref[...], both), px_ref[...])
     last = (size_x - 1) * NP
     weights = []
     for plane in pair_planes("gx", size_x, pairs_x):
@@ -481,7 +523,7 @@
         out_ref[x] = with_xy_halo(s_ref[x], x, shape[0], x_halo, y_halo)
 
 
-def final_kernel(gossip, s_ref, tab_ref, z_low_ref, z_high_ref, *refs):
+def final_kernel(gossip, s_ref, tab_ref, z_high_ref, z_low_ref, *refs):
     shape = size_x, size_y, size_z = s_ref.shape
     z_refs = (z_low_ref, z_high_ref)
     out_ref, buffer, sems = refs[-3:]
@@ -510,6 +552,7 @@
     "terms": 1_700_000_000,
     "y_faces": 10_000_000,
     "merge": 100_000_000,
+    "ahead": 10_000_000,
     "z_faces": 100_000_000,
     "forward": 1_100_000_000,
     "middle": 1_200_000_000,
@@ -605,11 +648,11 @@
         )
         return send(out[:2], perms_y), out[-1] if gossip else tab, out[0]
 
-    def z_round(z_faces, x_got, y_got, tab):
+    def z_round(z_faces, x_got, y_got, tab, operators=()):
         out = call(
-            functools.partial(z_kernel, gossip, pairs_x),
+            functools.partial(z_kernel, gossip, pairs_x, len(operators)),
             "z_faces",
-            [z_faces, tab, *x_got, *y_got],
+            [z_faces, tab, *operators, *x_got, *y_got],
             [(size_y + 2 * table_rows, LANES)] * 2 + tab_shapes,
         )
         return send(out[:2], perms_z), out[-1] if gossip else tab
@@ -642,7 +685,10 @@
     )
     if gossip:
         tab = call(merge_kernel, "merge", [tab, far[0], px], tab_shapes)[0]
-    z_got, tab = z_round(z_faces, x_got, y_got, tab)
+    ahead = call(
+        functools.partial(ahead_kernel, pairs_x), "ahead", [z_faces, pyt, px, *x_got], [(size_y, LANES)]
+    )[0]
+    z_got, tab = z_round(ahead, x_got, y_got, tab, (pyt, px))
     spectrum = call(
         functools.partial(forward_kernel, pairs_x),
         "forward",
@@ -653,7 +699,7 @@
     half, *rest = call(
         functools.partial(middle_kernel, gossip, pairs_x),
         "middle",
-        [spectrum, pz, pzt, py, pyt, px, entries, inverse, tab, *z_got],
+        [spectrum, pz, pzt, py, entries, inverse, tab, *z_got],
         [shape] + [(size_y + table_rows, size_z)] * pairs_x + tab_shapes,
     )
     x_got = send(rest[:pairs_x], perms_x)
@@ -669,7 +715,7 @@
     return call(
         functools.partial(final_kernel, gossip),
         "final",
-        [solved, coarse, *z_got, *weights[:3]],
+        [solved, coarse, *z_got[::-1], *weights[:3]],
         [shape],
         scratch=[shape, pltpu.SemaphoreType.DMA((size_x,))],
         out_spec=HBM,

time: 30.5 us -> 30.2 us (level)
  waiting for transfers between devices: 6.69 us -> 5.95 us
    ppermute x11, waiting for transfers between devices: 6.69 us -> 5.95 us  [send(): return [lax.ppermute(p, AXES, q) for p, q in zip(payloads, pairs)]]
    pallas_call x13 -> x14, Pallas kernels: 7.71 us -> 7.96 us  [call(): pl.pallas_call(kernel, name=name, out_shape=[jax.ShapeDtypeStruct(s, jnp....]
  transfers between devices with their start and end apart: 11 -> 11, of which waited for: 5 -> 5; matrix products, arithmetic and copies ran while one was open for 0% -> 0% of each run, Pallas kernels for 11% -> 13%
where the time goes in v5:
time: 30.2 us; the launch traced here: 30.1 us
  starting transfers between devices  15.2 us (50%)
  Pallas kernels  7.96 us (26%)
  waiting for transfers between devices  5.95 us (20%)
  local copies, waits for them, and re-layouts  0.79 us (3%)
    ppermute x11, starting transfers between devices, send(): return [lax.ppermute(p, AXES, q) for p, q in zip(payloads, pairs)]  15.2 us
    pallas_call x14, Pallas kernels, call(): pl.pallas_call(kernel, name=name, out_shape=[jax.ShapeDtypeStruct(s, jnp....  7.96 us
    ppermute x11, waiting for transfers between devices, send(): return [lax.ppermute(p, AXES, q) for p, q in zip(payloads, pairs)]  5.95 us
    unnamed x14, local copies, waits for them, and re-layouts  0.79 us
  transfers between devices with their start and end apart: 11, of which 5 were waited for; matrix products, arithmetic and copies ran while one was open for 0% of the time, Pallas kernels for 13%

profile of v5, /device:TPU:0, one launch (start us, length us, event | category | flops | bytes accessed | tf_op | source)
XLA Modules:
  0.0 30.1 jit_solution(7417684402697479835)
XLA Ops:
  0.0 0.0 copy-start.6
  0.0 0.0 copy-start
  0.0 0.0 copy-start.1
  0.0 0.3 %weights.1 = (f32[128,256]{1,0:T(8,128)S(1)}, f32[144,24]{1,0:T(8,128)S(1)}, f32[128,128]{1,0:T(8,128)S(1)}, f32[8,432]{1,0:T(8,128)S(1)}, f32[256,128]{1,0:T(8,128)S(1)}, /*index=5*/f32[32,128]{1,0:T(8,128)S(1)}) custom-call(), custom_call_target="tpu_custom_call" | custom-call | flops 1500000000 | tf_op jit(solution)/shard_map/weights/pallas_call | solution.py:567
  0.3 0.0 copy-start.3
  0.4 0.0 copy-start.4
  0.4 0.4 %copy-done.6 = f32[24,256]{1,0:T(8,128)S(1)} copy-done((f32[24,256]{1,0:T(8,128)S(1)}, f32[24,256]{1,0:T(8,128)}, u32[]{:S(2)}) %copy-start.6) | copy-done | bytes 24600
  0.7 0.3 copy-done
  1.0 0.1 copy-done.1
  1.1 0.0 copy-done.3
  1.1 0.0 copy-done.4
  1.1 1.4 %terms.1 = (f32[8,48,256]{2,1,0:T(8,128)S(1)}, f32[2,8,256]{2,1,0:T(8,128)S(1)}, f32[2,48,128]{2,1,0:T(8,128)S(1)}, f32[48,256]{1,0:T(8,128)S(1)}, f32[8,256]{1,0:T(8,128)S(1)}) custom-call(f32[8,48,256]{2,1,0:T(8,128)S(1)} %copy-done, f32[8,48,256]{2,1,0:T(8,128)S(1)} %copy-done.1, f32[24,256]{1,0:T(8,128)S(1)} %copy-done.6, f32[6,1,32]{2,1,0:T(1,128)S(1)} %bitcast.2, ...), custom_call_target="tpu_custom_call" | custom-call | flops 1700000000 | tf_op jit(solution)/shard_map/terms/pallas_call | solution.py:567
  2.5 3.0 %collective-permute-start = (f32[48,256]{1,0:T(8,128)S(1)}, f32[48,256]{1,0:T(8,128)S(1)}, u32[]{:S(2)}, u32[]{:S(2)}) collective-permute-start(f32[48,256]{1,0:T(8,128)S(1)} %get-tuple-element.47), channel_id=1, source_target_pairs={{0,16},{1,17},{2,18},{3,19},{4,20},{5,21},{6,22},{7,23},{8,24},{9,... | collective-permute-start | bytes 147464 | tf_op jit(solution)/shard_map/ppermute | solution.py:640
  5.5 2.6 %collective-permute-start.3 = (f32[8,256]{1,0:T(8,128)S(1)}, f32[8,256]{1,0:T(8,128)S(1)}, u32[]{:S(2)}, u32[]{:S(2)}) collective-permute-start(f32[8,256]{1,0:T(8,128)S(1)} %get-tuple-element.46.tab_ref), channel_id=1, source_target_pairs={{0,2},{1,3},{2,0},{3,1},{4,6},{5,7},{6,4},{7,5},{8,10},{9,11},{10,... | collective-permute-start | bytes 24584 | tf_op jit(solution)/shard_map/ppermute | solution.py:640
  8.1 0.0 collective-permute-done.refs_0_.refs_2_
  8.1 0.0 copy-start.2
  8.1 0.1 collective-permute-start.1
  8.2 0.0 copy-start.5
  8.2 1.6 %collective-permute-start.2 = (f32[16,256]{1,0:T(8,128)S(1)}, f32[16,256]{1,0:T(8,128)S(1)}, u32[]{:S(2)}, u32[]{:S(2)}) collective-permute-start(f32[16,256]{1,0:T(8,128)S(1)} %get-tuple-element.52), channel_id=1, source_target_pairs={{0,12},{1,13},{2,14},{3,15},{4,8},{5,9},{6,10},{7,11},{8,4},{9,5},... | collective-permute-start | bytes 49160 | tf_op jit(solution)/shard_map/ppermute | solution.py:640
  9.9 0.0 copy-done.2
  9.9 0.0 copy-done.5
  9.9 0.7 %operators.1 = (f32[256,256]{1,0:T(8,128)S(1)}, f32[256,256]{1,0:T(8,128)S(1)}, f32[48,48]{1,0:T(8,128)S(1)}, f32[48,48]{1,0:T(8,128)S(1)}, f32[128,128]{1,0:T(8...) custom-call(f32[8,8]{1,0:T(8,128)S(1)} %copy-done.2, f32[1,8]{1,0:T(1,128)S(1)} %bitcast.4, ...), custom_call_target="tpu_custom_call" | custom-call | flops 10000000 | tf_op jit(solution)/shard_map/operators/pallas_call | solution.py:567
  10.6 0.4 %ahead.1.zf_ref = f32[48,128]{1,0:T(8,128)S(1)} custom-call(f32[2,48,128]{2,1,0:T(8,128)S(1)} %get-tuple-element.56.zf_ref, f32[48,48]{1,0:T(8,128)S(1)} %get-tuple-element.50.pyt_ref.refs_0_, f32[128,128]{1,0:T(8,128)S(1)} %get-tuple-element.57.px_ref._.refs_1_, f32[48,256]{1,0:T(8,128)S(1)} %collective-permute-done.refs_0_.refs_2_), custom_call_target="tpu_custom_call" | custom-call | flops 10000000 | tf_op jit(solution)/shard_map/ahead/pallas_call | solution.py:567
  11.0 0.0 collective-permute-done.3.far_ref
  11.1 0.0 collective-permute-done.1.refs_1_.refs_3_
  11.1 0.4 %collective-permute-done.2.refs_2_.refs_4_ = f32[16,256]{1,0:T(8,128)S(1)} collective-permute-done((f32[16,256]{1,0:T(8,128)S(1)}, f32[16,256]{1,0:T(8,128)S(1)}, u32[]{:S(2)}, u32[]{:S(2)}) %collective-permute-start.2) | collective-permute-done | bytes 16416 | tf_op jit(solution)/shard_map/ppermute | solution.py:640
  11.5 0.3 %z_faces.2 = (f32[64,128]{1,0:T(8,128)S(1)}, f32[64,128]{1,0:T(8,128)S(1)}, f32[8,256]{1,0:T(8,128)S(1)}) custom-call(f32[48,128]{1,0:T(8,128)S(1)} %ahead.1.zf_ref, f32[8,256]{1,0:T(8,128)S(1)} %merge.1.tab_ref, f32[48,48]{1,0:T(8,128)S(1)} %get-tuple-element.50.pyt_ref.refs_0_, f32[128,128]{1,0:T(8,128)S(1)} %get-tuple-element.57.px_ref._.refs_1_, ...), custom_call_target="tpu_custom_call" | custom-call | flops 100000000 | tf_op jit(solution)/shard_map/z_faces/pallas_call | solution.py:567
  11.8 1.6 %collective-permute-start.4 = (f32[64,128]{1,0:T(8,128)S(1)}, f32[64,128]{1,0:T(8,128)S(1)}, u32[]{:S(2)}, u32[]{:S(2)}) collective-permute-start(f32[64,128]{1,0:T(8,128)S(1)} %get-tuple-element.60), channel_id=1, source_target_pairs={{0,1},{1,0},{2,3},{3,2},{4,5},{5,4},{6,7},{7,6},{8,9},{9,8},{10,11... | collective-permute-start | bytes 98312 | tf_op jit(solution)/shard_map/ppermute | solution.py:640
  13.4 0.2 collective-permute-start.5
  13.5 1.0 %forward.1.s_ref = f32[8,48,256]{2,1,0:T(8,128)S(1)} custom-call(f32[8,48,256]{2,1,0:T(8,128)S(1)} %get-tuple-element.44.t_ref, f32[256,256]{1,0:T(8,128)S(1)} %get-tuple-element.49.pz_ref, f32[48,48]{1,0:T(8,128)S(1)} %get-tuple-element.50.pyt_ref.refs_0_, f32[64,256]{1,0:T(8,128)S(1)} %get-tuple-element.51.entry_ref, ...), custom_call_target="tpu_custom_call" | custom-call | flops 1100000000 | tf_op jit(solution)/shard_map/forward/pallas_call | solution.py:567
  14.6 1.2 %collective-permute-done.4.refs_0_ = f32[64,128]{1,0:T(8,128)S(1)} collective-permute-done((f32[64,128]{1,0:T(8,128)S(1)}, f32[64,128]{1,0:T(8,128)S(1)}, u32[]{:S(2)}, u32[]{:S(2)}) %collective-permute-start.4) | collective-permute-done | bytes 32800 | tf_op jit(solution)/shard_map/ppermute | solution.py:640
  15.7 0.0 collective-permute-done.5.refs_1_
  15.7 0.7 %middle.1 = (f32[8,48,256]{2,1,0:T(8,128)S(1)}, f32[56,256]{1,0:T(8,128)S(1)}, f32[8,256]{1,0:T(8,128)S(1)}) custom-call(f32[8,48,256]{2,1,0:T(8,128)S(1)} %forward.1.s_ref, f32[256,256]{1,0:T(8,128)S(1)} %get-tuple-element.49.pz_ref, f32[256,256]{1,0:T(8,128)S(1)} %get-tuple-element.53.pzt_ref, f32[48,48]{1,0:T(8,128)S(1)} %get-tuple-element.54.py_ref, ...), custom_call_target="tpu_custom_call" | custom-call | flops 1200000000 | tf_op jit(solution)/shard_map/middle/pallas_call | solution.py:567
  16.4 1.6 %collective-permute-start.6 = (f32[56,256]{1,0:T(8,128)S(1)}, f32[56,256]{1,0:T(8,128)S(1)}, u32[]{:S(2)}, u32[]{:S(2)}) collective-permute-start(f32[56,256]{1,0:T(8,128)S(1)} %get-tuple-element.64), channel_id=1, source_target_pairs={{0,16},{1,17},{2,18},{3,19},{4,20},{5,21},{6,22},{7,23},{8,24},{9,... | collective-permute-start | bytes 172040 | tf_op jit(solution)/shard_map/ppermute | solution.py:640
  18.0 1.7 %inverse.1 = (f32[8,48,256]{2,1,0:T(8,128)S(1)}, f32[2,8,256]{2,1,0:T(8,128)S(1)}, f32[2,48,128]{2,1,0:T(8,128)S(1)}) custom-call(f32[8,48,256]{2,1,0:T(8,128)S(1)} %get-tuple-element.62.half_ref, f32[256,256]{1,0:T(8,128)S(1)} %get-tuple-element.53.pzt_ref, f32[48,48]{1,0:T(8,128)S(1)} %get-tuple-element.54.py_ref, f32[64,256]{1,0:T(8,128)S(1)} %get-tuple-element.51.entry_ref), custom_call_target="tpu_custom_call" | custom-call | flops 1800000000 | tf_op jit(solution)/shard_map/inverse/pallas_call | solution.py:567
  19.7 1.0 %collective-permute-done.6.refs_0_ = f32[56,256]{1,0:T(8,128)S(1)} collective-permute-done((f32[56,256]{1,0:T(8,128)S(1)}, f32[56,256]{1,0:T(8,128)S(1)}, u32[]{:S(2)}, u32[]{:S(2)}) %collective-permute-start.6) | collective-permute-done | bytes 57376 | tf_op jit(solution)/shard_map/ppermute | solution.py:640
  20.7 0.1 collective-permute-start.7
  20.8 1.6 %collective-permute-start.8 = (f32[16,256]{1,0:T(8,128)S(1)}, f32[16,256]{1,0:T(8,128)S(1)}, u32[]{:S(2)}, u32[]{:S(2)}) collective-permute-start(f32[16,256]{1,0:T(8,128)S(1)} %get-tuple-element.68), channel_id=1, source_target_pairs={{0,12},{1,13},{2,14},{3,15},{4,8},{5,9},{6,10},{7,11},{8,4},{9,5},... | collective-permute-start | bytes 49160 | tf_op jit(solution)/shard_map/ppermute | solution.py:640
  22.4 0.0 collective-permute-done.7.refs_1_
  22.4 1.6 %collective-permute-done.8.refs_2_ = f32[16,256]{1,0:T(8,128)S(1)} collective-permute-done((f32[16,256]{1,0:T(8,128)S(1)}, f32[16,256]{1,0:T(8,128)S(1)}, u32[]{:S(2)}, u32[]{:S(2)}) %collective-permute-start.8) | collective-permute-done | bytes 16416 | tf_op jit(solution)/shard_map/ppermute | solution.py:640
  24.0 0.1 z_faces.3
  24.1 2.8 %collective-permute-start.10 = (f32[64,128]{1,0:T(8,128)S(1)}, f32[64,128]{1,0:T(8,128)S(1)}, u32[]{:S(2)}, u32[]{:S(2)}) collective-permute-start(f32[64,128]{1,0:T(8,128)S(1)} %get-tuple-element.73), channel_id=1, source_target_pairs={{0,1},{1,0},{2,3},{3,2},{4,5},{5,4},{6,7},{7,6},{8,9},{9,8},{10,11... | collective-permute-start | bytes 98312 | tf_op jit(solution)/shard_map/ppermute | solution.py:640
  26.9 0.2 collective-permute-start.9
  27.0 0.1 assemble.1.s_ref
  27.1 1.8 %collective-permute-done.10.z_low_ref = f32[64,128]{1,0:T(8,128)S(1)} collective-permute-done((f32[64,128]{1,0:T(8,128)S(1)}, f32[64,128]{1,0:T(8,128)S(1)}, u32[]{:S(2)}, u32[]{:S(2)}) %collective-permute-start.10) | collective-permute-done | bytes 32800 | tf_op jit(solution)/shard_map/ppermute | solution.py:640
  28.9 0.0 collective-permute-done.9.z_high_ref
  28.9 1.2 %final.1 = f32[8,48,256]{2,1,0:T(8,128)} custom-call(f32[8,48,256]{2,1,0:T(8,128)S(1)} %assemble.1.s_ref, f32[8,256]{1,0:T(8,128)S(1)} %get-tuple-element.71.tab_ref, f32[64,128]{1,0:T(8,128)S(1)} %collective-permute-done.9.z_high_ref, f32[64,128]{1,0:T(8,128)S(1)} %collective-permute-done.10.z_low_ref, f32[128,256]{1,0:T(8,128)S(1)} %get-tuple-element.74.refs_0_, ...), custom_call_target="tpu_custom_call" | custom-call | flops 1400000000 | tf_op jit(solution)/shard_map/final/pallas_call | solution.py:567
  (3 shorter events, 0.0 us)
Async XLA Ops:
  0.0 0.7 %copy-start.6 = (f32[24,256]{1,0:T(8,128)S(1)}, f32[24,256]{1,0:T(8,128)}, u32[]{:S(2)}) copy-start(f32[24,256]{1,0:T(8,128)} %constant.2.clone.const_ref) | copy-start | bytes 73732
  0.0 1.0 %copy-start = (f32[8,48,256]{2,1,0:T(8,128)S(1)}, f32[8,48,256]{2,1,0:T(8,128)}, u32[]{:S(2)}) copy-start(f32[8,48,256]{2,1,0:T(8,128)} %u_ref.1) | copy-start | bytes 1179652
  0.0 1.1 %copy-start.1 = (f32[8,48,256]{2,1,0:T(8,128)S(1)}, f32[8,48,256]{2,1,0:T(8,128)}, u32[]{:S(2)}) copy-start(f32[8,48,256]{2,1,0:T(8,128)} %l_ref.1) | copy-start | bytes 1179652
  0.3 0.8 %copy-start.3 = (f32[1,6,32]{2,0,1:T(1,128)S(1)}, f32[1,6,32]{2,0,1:T(1,128)}, u32[]{:S(2)}) copy-start(f32[1,6,32]{2,0,1:T(1,128)} %param.9) | copy-start | bytes 2308
  0.4 0.8 %copy-start.4 = (f32[1,32]{1,0:T(1,128)S(1)}, f32[1,32]{1,0:T(1,128)}, u32[]{:S(2)}) copy-start(f32[1,32]{1,0:T(1,128)} %cinv_ref.1) | copy-start | bytes 388
  2.5 5.6 %collective-permute-start = (f32[48,256]{1,0:T(8,128)S(1)}, f32[48,256]{1,0:T(8,128)S(1)}, u32[]{:S(2)}, u32[]{:S(2)}) collective-permute-start(f32[48,256]{1,0:T(8,128)S(1)} %get-tuple-element.47), channel_id=1, source_target_pairs={{0,16},{1,17},{2,18},{3,19},{4,20},{5,21},{6,22},{7,23},{8,24},{9,... | collective-permute-start | bytes 147464 | tf_op jit(solution)/shard_map/ppermute | solution.py:640
  5.5 5.5 %collective-permute-start.3 = (f32[8,256]{1,0:T(8,128)S(1)}, f32[8,256]{1,0:T(8,128)S(1)}, u32[]{:S(2)}, u32[]{:S(2)}) collective-permute-start(f32[8,256]{1,0:T(8,128)S(1)} %get-tuple-element.46.tab_ref), channel_id=1, source_target_pairs={{0,2},{1,3},{2,0},{3,1},{4,6},{5,7},{6,4},{7,5},{8,10},{9,11},{10,... | collective-permute-start | bytes 24584 | tf_op jit(solution)/shard_map/ppermute | solution.py:640
  8.1 1.7 %copy-start.2 = (f32[8,8]{1,0:T(8,128)S(1)}, f32[8,8]{1,0:T(8,128)}, u32[]{:S(2)}) copy-start(f32[8,8]{1,0:T(8,128)} %basis_ref.1) | copy-start | bytes 772
  8.1 2.9 %collective-permute-start.1 = (f32[16,256]{1,0:T(8,128)S(1)}, f32[16,256]{1,0:T(8,128)S(1)}, u32[]{:S(2)}, u32[]{:S(2)}) collective-permute-start(f32[16,256]{1,0:T(8,128)S(1)} %get-tuple-element.48._), channel_id=1, source_target_pairs={{0,4},{1,5},{2,6},{3,7},{4,0},{5,1},{6,2},{7,3},{8,12},{9,13},{10,... | collective-permute-start | bytes 49160 | tf_op jit(solution)/shard_map/ppermute | solution.py:640
  8.2 1.6 %copy-start.5 = (f32[8]{0:T(128)S(1)}, f32[8]{0:T(128)}, u32[]{:S(2)}) copy-start(f32[8]{0:T(128)} %param.11) | copy-start | bytes 100
  8.2 3.2 %collective-permute-start.2 = (f32[16,256]{1,0:T(8,128)S(1)}, f32[16,256]{1,0:T(8,128)S(1)}, u32[]{:S(2)}, u32[]{:S(2)}) collective-permute-start(f32[16,256]{1,0:T(8,128)S(1)} %get-tuple-element.52), channel_id=1, source_target_pairs={{0,12},{1,13},{2,14},{3,15},{4,8},{5,9},{6,10},{7,11},{8,4},{9,5},... | collective-permute-start | bytes 49160 | tf_op jit(solution)/shard_map/ppermute | solution.py:640
  11.8 3.9 %collective-permute-start.4 = (f32[64,128]{1,0:T(8,128)S(1)}, f32[64,128]{1,0:T(8,128)S(1)}, u32[]{:S(2)}, u32[]{:S(2)}) collective-permute-start(f32[64,128]{1,0:T(8,128)S(1)} %get-tuple-element.60), channel_id=1, source_target_pairs={{0,1},{1,0},{2,3},{3,2},{4,5},{5,4},{6,7},{7,6},{8,9},{9,8},{10,11... | collective-permute-start | bytes 98312 | tf_op jit(solution)/shard_map/ppermute | solution.py:640
  13.4 2.3 %collective-permute-start.5 = (f32[64,128]{1,0:T(8,128)S(1)}, f32[64,128]{1,0:T(8,128)S(1)}, u32[]{:S(2)}, u32[]{:S(2)}) collective-permute-start(f32[64,128]{1,0:T(8,128)S(1)} %get-tuple-element.61), channel_id=1, source_target_pairs={{0,4},{1,2},{2,1},{3,7},{4,0},{5,6},{6,5},{7,3},{8,12},{9,10},{10,... | collective-permute-start | bytes 98312 | tf_op jit(solution)/shard_map/ppermute | solution.py:640
  16.4 4.2 %collective-permute-start.6 = (f32[56,256]{1,0:T(8,128)S(1)}, f32[56,256]{1,0:T(8,128)S(1)}, u32[]{:S(2)}, u32[]{:S(2)}) collective-permute-start(f32[56,256]{1,0:T(8,128)S(1)} %get-tuple-element.64), channel_id=1, source_target_pairs={{0,16},{1,17},{2,18},{3,19},{4,20},{5,21},{6,22},{7,23},{8,24},{9,... | collective-permute-start | bytes 172040 | tf_op jit(solution)/shard_map/ppermute | solution.py:640
  20.7 1.7 %collective-permute-start.7 = (f32[16,256]{1,0:T(8,128)S(1)}, f32[16,256]{1,0:T(8,128)S(1)}, u32[]{:S(2)}, u32[]{:S(2)}) collective-permute-start(f32[16,256]{1,0:T(8,128)S(1)} %get-tuple-element.67), channel_id=1, source_target_pairs={{0,4},{1,5},{2,6},{3,7},{4,0},{5,1},{6,2},{7,3},{8,12},{9,13},{10,... | collective-permute-start | bytes 49160 | tf_op jit(solution)/shard_map/ppermute | solution.py:640
  20.8 3.2 %collective-permute-start.8 = (f32[16,256]{1,0:T(8,128)S(1)}, f32[16,256]{1,0:T(8,128)S(1)}, u32[]{:S(2)}, u32[]{:S(2)}) collective-permute-start(f32[16,256]{1,0:T(8,128)S(1)} %get-tuple-element.68), channel_id=1, source_target_pairs={{0,12},{1,13},{2,14},{3,15},{4,8},{5,9},{6,10},{7,11},{8,4},{9,5},... | collective-permute-start | bytes 49160 | tf_op jit(solution)/shard_map/ppermute | solution.py:640
  24.1 4.8 %collective-permute-start.10 = (f32[64,128]{1,0:T(8,128)S(1)}, f32[64,128]{1,0:T(8,128)S(1)}, u32[]{:S(2)}, u32[]{:S(2)}) collective-permute-start(f32[64,128]{1,0:T(8,128)S(1)} %get-tuple-element.73), channel_id=1, source_target_pairs={{0,1},{1,0},{2,3},{3,2},{4,5},{5,4},{6,7},{7,6},{8,9},{9,8},{10,11... | collective-permute-start | bytes 98312 | tf_op jit(solution)/shard_map/ppermute | solution.py:640
  26.9 2.0 %collective-permute-start.9 = (f32[64,128]{1,0:T(8,128)S(1)}, f32[64,128]{1,0:T(8,128)S(1)}, u32[]{:S(2)}, u32[]{:S(2)}) collective-permute-start(f32[64,128]{1,0:T(8,128)S(1)} %get-tuple-element.72), channel_id=1, source_target_pairs={{0,4},{1,2},{2,1},{3,7},{4,0},{5,6},{6,5},{7,3},{8,12},{9,10},{10,... | collective-permute-start | bytes 98312 | tf_op jit(solution)/shard_map/ppermute | solution.py:640

commit v6 on v5

--- a/solution.py
+++ b/solution.py
@@ -527,18 +527,18 @@
     shape = size_x, size_y, size_z = s_ref.shape
     z_refs = (z_low_ref, z_high_ref)
     out_ref, buffer, sems = refs[-3:]
+    lane = iota((size_y, size_z), 1)
+    low, high = z_halos(shape, z_refs)
+    for x in range(size_x):
+        plane = s_ref[x] + jnp.where(lane == 0, low[:, x : x + 1], 0.0)
+        buffer[x] = plane + jnp.where(lane == size_z - 1, high[:, x : x + 1], 0.0)
     if gossip:
         coarse = coarse_planes(merged_table(tab_ref, z_refs, size_y), *refs[:3])
     else:
         coarse = [tab_ref[c] for c in range(3)]
-    lane = iota((size_y, size_z), 1)
-    coarse = [jnp.where(z_keep(lane, size_z), plane, 0.0) for plane in coarse]
-    low, high = z_halos(shape, z_refs)
     copies = []
     for x in range(size_x):
-        plane = kept(coarse[0 if x == 0 else 2 if x == size_x - 1 else 1], x_keep(x, size_x)) + s_ref[x]
-        plane = plane + jnp.where(lane == 0, low[:, x : x + 1], 0.0)
-        buffer[x] = plane + jnp.where(lane == size_z - 1, high[:, x : x + 1], 0.0)
+        buffer[x] += coarse[0 if x == 0 else 2 if x == size_x - 1 else 1]
         copies.append(pltpu.make_async_copy(buffer.at[x], out_ref.at[x], sems.at[x]))
         copies[-1].start()
     for copy in copies:

time: 30.2 us -> 30.2 us (level)
  no operation moved by 1% of the time
where the time goes in v6:
time: 30.2 us; the launch traced here: 30.1 us
  starting transfers between devices  15.2 us (50%)
  Pallas kernels  7.95 us (26%)
  waiting for transfers between devices  5.95 us (20%)
  local copies, waits for them, and re-layouts  0.79 us (3%)
    ppermute x11, starting transfers between devices, send(): return [lax.ppermute(p, AXES, q) for p, q in zip(payloads, pairs)]  15.2 us
    pallas_call x14, Pallas kernels, call(): pl.pallas_call(kernel, name=name, out_shape=[jax.ShapeDtypeStruct(s, jnp....  7.95 us
    ppermute x11, waiting for transfers between devices, send(): return [lax.ppermute(p, AXES, q) for p, q in zip(payloads, pairs)]  5.95 us
    unnamed x14, local copies, waits for them, and re-layouts  0.79 us
  transfers between devices with their start and end apart: 11, of which 5 were waited for; matrix products, arithmetic and copies ran while one was open for 0% of the time, Pallas kernels for 13%

profile of v6, /device:TPU:0, one launch (start us, length us, event | category | flops | bytes accessed | tf_op | source)
XLA Modules:
  0.0 30.1 jit_solution(11858646428635510917)
XLA Ops:
  0.0 0.0 copy-start.6
  0.0 0.0 copy-start
  0.0 0.0 copy-start.1
  0.0 0.3 %weights.1 = (f32[128,256]{1,0:T(8,128)S(1)}, f32[144,24]{1,0:T(8,128)S(1)}, f32[128,128]{1,0:T(8,128)S(1)}, f32[8,432]{1,0:T(8,128)S(1)}, f32[256,128]{1,0:T(8,128)S(1)}, /*index=5*/f32[32,128]{1,0:T(8,128)S(1)}) custom-call(), custom_call_target="tpu_custom_call" | custom-call | flops 1500000000 | tf_op jit(solution)/shard_map/weights/pallas_call | solution.py:567
  0.3 0.0 copy-start.3
  0.4 0.0 copy-start.4
  0.4 0.4 %copy-done.6 = f32[24,256]{1,0:T(8,128)S(1)} copy-done((f32[24,256]{1,0:T(8,128)S(1)}, f32[24,256]{1,0:T(8,128)}, u32[]{:S(2)}) %copy-start.6) | copy-done | bytes 24600
  0.7 0.3 copy-done
  1.0 0.1 copy-done.1
  1.1 0.0 copy-done.3
  1.1 0.0 copy-done.4
  1.1 1.4 %terms.1 = (f32[8,48,256]{2,1,0:T(8,128)S(1)}, f32[2,8,256]{2,1,0:T(8,128)S(1)}, f32[2,48,128]{2,1,0:T(8,128)S(1)}, f32[48,256]{1,0:T(8,128)S(1)}, f32[8,256]{1,0:T(8,128)S(1)}) custom-call(f32[8,48,256]{2,1,0:T(8,128)S(1)} %copy-done, f32[8,48,256]{2,1,0:T(8,128)S(1)} %copy-done.1, f32[24,256]{1,0:T(8,128)S(1)} %copy-done.6, f32[6,1,32]{2,1,0:T(1,128)S(1)} %bitcast.2, ...), custom_call_target="tpu_custom_call" | custom-call | flops 1700000000 | tf_op jit(solution)/shard_map/terms/pallas_call | solution.py:567
  2.5 3.0 %collective-permute-start = (f32[48,256]{1,0:T(8,128)S(1)}, f32[48,256]{1,0:T(8,128)S(1)}, u32[]{:S(2)}, u32[]{:S(2)}) collective-permute-start(f32[48,256]{1,0:T(8,128)S(1)} %get-tuple-element.47), channel_id=1, source_target_pairs={{0,16},{1,17},{2,18},{3,19},{4,20},{5,21},{6,22},{7,23},{8,24},{9,... | collective-permute-start | bytes 147464 | tf_op jit(solution)/shard_map/ppermute | solution.py:640
  5.5 2.6 %collective-permute-start.3 = (f32[8,256]{1,0:T(8,128)S(1)}, f32[8,256]{1,0:T(8,128)S(1)}, u32[]{:S(2)}, u32[]{:S(2)}) collective-permute-start(f32[8,256]{1,0:T(8,128)S(1)} %get-tuple-element.46.tab_ref), channel_id=1, source_target_pairs={{0,2},{1,3},{2,0},{3,1},{4,6},{5,7},{6,4},{7,5},{8,10},{9,11},{10,... | collective-permute-start | bytes 24584 | tf_op jit(solution)/shard_map/ppermute | solution.py:640
  8.1 0.0 collective-permute-done.refs_0_.refs_2_
  8.1 0.0 copy-start.2
  8.1 0.1 collective-permute-start.1
  8.2 0.0 copy-start.5
  8.2 1.6 %collective-permute-start.2 = (f32[16,256]{1,0:T(8,128)S(1)}, f32[16,256]{1,0:T(8,128)S(1)}, u32[]{:S(2)}, u32[]{:S(2)}) collective-permute-start(f32[16,256]{1,0:T(8,128)S(1)} %get-tuple-element.52), channel_id=1, source_target_pairs={{0,12},{1,13},{2,14},{3,15},{4,8},{5,9},{6,10},{7,11},{8,4},{9,5},... | collective-permute-start | bytes 49160 | tf_op jit(solution)/shard_map/ppermute | solution.py:640
  9.9 0.0 copy-done.2
  9.9 0.0 copy-done.5
  9.9 0.7 %operators.1 = (f32[256,256]{1,0:T(8,128)S(1)}, f32[256,256]{1,0:T(8,128)S(1)}, f32[48,48]{1,0:T(8,128)S(1)}, f32[48,48]{1,0:T(8,128)S(1)}, f32[128,128]{1,0:T(8...) custom-call(f32[8,8]{1,0:T(8,128)S(1)} %copy-done.2, f32[1,8]{1,0:T(1,128)S(1)} %bitcast.4, ...), custom_call_target="tpu_custom_call" | custom-call | flops 10000000 | tf_op jit(solution)/shard_map/operators/pallas_call | solution.py:567
  10.6 0.4 %ahead.1.zf_ref = f32[48,128]{1,0:T(8,128)S(1)} custom-call(f32[2,48,128]{2,1,0:T(8,128)S(1)} %get-tuple-element.56.zf_ref, f32[48,48]{1,0:T(8,128)S(1)} %get-tuple-element.50.pyt_ref.refs_0_, f32[128,128]{1,0:T(8,128)S(1)} %get-tuple-element.57.px_ref._.refs_1_, f32[48,256]{1,0:T(8,128)S(1)} %collective-permute-done.refs_0_.refs_2_), custom_call_target="tpu_custom_call" | custom-call | flops 10000000 | tf_op jit(solution)/shard_map/ahead/pallas_call | solution.py:567
  11.0 0.0 collective-permute-done.3.far_ref
  11.1 0.0 collective-permute-done.1.refs_1_.refs_3_
  11.1 0.4 %collective-permute-done.2.refs_2_.refs_4_ = f32[16,256]{1,0:T(8,128)S(1)} collective-permute-done((f32[16,256]{1,0:T(8,128)S(1)}, f32[16,256]{1,0:T(8,128)S(1)}, u32[]{:S(2)}, u32[]{:S(2)}) %collective-permute-start.2) | collective-permute-done | bytes 16416 | tf_op jit(solution)/shard_map/ppermute | solution.py:640
  11.5 0.3 %z_faces.2 = (f32[64,128]{1,0:T(8,128)S(1)}, f32[64,128]{1,0:T(8,128)S(1)}, f32[8,256]{1,0:T(8,128)S(1)}) custom-call(f32[48,128]{1,0:T(8,128)S(1)} %ahead.1.zf_ref, f32[8,256]{1,0:T(8,128)S(1)} %merge.1.tab_ref, f32[48,48]{1,0:T(8,128)S(1)} %get-tuple-element.50.pyt_ref.refs_0_, f32[128,128]{1,0:T(8,128)S(1)} %get-tuple-element.57.px_ref._.refs_1_, ...), custom_call_target="tpu_custom_call" | custom-call | flops 100000000 | tf_op jit(solution)/shard_map/z_faces/pallas_call | solution.py:567
  11.8 1.6 %collective-permute-start.4 = (f32[64,128]{1,0:T(8,128)S(1)}, f32[64,128]{1,0:T(8,128)S(1)}, u32[]{:S(2)}, u32[]{:S(2)}) collective-permute-start(f32[64,128]{1,0:T(8,128)S(1)} %get-tuple-element.60), channel_id=1, source_target_pairs={{0,1},{1,0},{2,3},{3,2},{4,5},{5,4},{6,7},{7,6},{8,9},{9,8},{10,11... | collective-permute-start | bytes 98312 | tf_op jit(solution)/shard_map/ppermute | solution.py:640
  13.4 0.2 collective-permute-start.5
  13.5 1.0 %forward.1.s_ref = f32[8,48,256]{2,1,0:T(8,128)S(1)} custom-call(f32[8,48,256]{2,1,0:T(8,128)S(1)} %get-tuple-element.44.t_ref, f32[256,256]{1,0:T(8,128)S(1)} %get-tuple-element.49.pz_ref, f32[48,48]{1,0:T(8,128)S(1)} %get-tuple-element.50.pyt_ref.refs_0_, f32[64,256]{1,0:T(8,128)S(1)} %get-tuple-element.51.entry_ref, ...), custom_call_target="tpu_custom_call" | custom-call | flops 1100000000 | tf_op jit(solution)/shard_map/forward/pallas_call | solution.py:567
  14.6 1.2 %collective-permute-done.4.refs_0_ = f32[64,128]{1,0:T(8,128)S(1)} collective-permute-done((f32[64,128]{1,0:T(8,128)S(1)}, f32[64,128]{1,0:T(8,128)S(1)}, u32[]{:S(2)}, u32[]{:S(2)}) %collective-permute-start.4) | collective-permute-done | bytes 32800 | tf_op jit(solution)/shard_map/ppermute | solution.py:640
  15.7 0.0 collective-permute-done.5.refs_1_
  15.7 0.7 %middle.1 = (f32[8,48,256]{2,1,0:T(8,128)S(1)}, f32[56,256]{1,0:T(8,128)S(1)}, f32[8,256]{1,0:T(8,128)S(1)}) custom-call(f32[8,48,256]{2,1,0:T(8,128)S(1)} %forward.1.s_ref, f32[256,256]{1,0:T(8,128)S(1)} %get-tuple-element.49.pz_ref, f32[256,256]{1,0:T(8,128)S(1)} %get-tuple-element.53.pzt_ref, f32[48,48]{1,0:T(8,128)S(1)} %get-tuple-element.54.py_ref, ...), custom_call_target="tpu_custom_call" | custom-call | flops 1200000000 | tf_op jit(solution)/shard_map/middle/pallas_call | solution.py:567
  16.4 1.6 %collective-permute-start.6 = (f32[56,256]{1,0:T(8,128)S(1)}, f32[56,256]{1,0:T(8,128)S(1)}, u32[]{:S(2)}, u32[]{:S(2)}) collective-permute-start(f32[56,256]{1,0:T(8,128)S(1)} %get-tuple-element.64), channel_id=1, source_target_pairs={{0,16},{1,17},{2,18},{3,19},{4,20},{5,21},{6,22},{7,23},{8,24},{9,... | collective-permute-start | bytes 172040 | tf_op jit(solution)/shard_map/ppermute | solution.py:640
  18.0 1.7 %inverse.1 = (f32[8,48,256]{2,1,0:T(8,128)S(1)}, f32[2,8,256]{2,1,0:T(8,128)S(1)}, f32[2,48,128]{2,1,0:T(8,128)S(1)}) custom-call(f32[8,48,256]{2,1,0:T(8,128)S(1)} %get-tuple-element.62.half_ref, f32[256,256]{1,0:T(8,128)S(1)} %get-tuple-element.53.pzt_ref, f32[48,48]{1,0:T(8,128)S(1)} %get-tuple-element.54.py_ref, f32[64,256]{1,0:T(8,128)S(1)} %get-tuple-element.51.entry_ref), custom_call_target="tpu_custom_call" | custom-call | flops 1800000000 | tf_op jit(solution)/shard_map/inverse/pallas_call | solution.py:567
  19.7 1.0 %collective-permute-done.6.refs_0_ = f32[56,256]{1,0:T(8,128)S(1)} collective-permute-done((f32[56,256]{1,0:T(8,128)S(1)}, f32[56,256]{1,0:T(8,128)S(1)}, u32[]{:S(2)}, u32[]{:S(2)}) %collective-permute-start.6) | collective-permute-done | bytes 57376 | tf_op jit(solution)/shard_map/ppermute | solution.py:640
  20.7 0.1 collective-permute-start.7
  20.8 1.6 %collective-permute-start.8 = (f32[16,256]{1,0:T(8,128)S(1)}, f32[16,256]{1,0:T(8,128)S(1)}, u32[]{:S(2)}, u32[]{:S(2)}) collective-permute-start(f32[16,256]{1,0:T(8,128)S(1)} %get-tuple-element.68), channel_id=1, source_target_pairs={{0,12},{1,13},{2,14},{3,15},{4,8},{5,9},{6,10},{7,11},{8,4},{9,5},... | collective-permute-start | bytes 49160 | tf_op jit(solution)/shard_map/ppermute | solution.py:640
  22.4 0.0 collective-permute-done.7.refs_1_
  22.4 1.6 %collective-permute-done.8.refs_2_ = f32[16,256]{1,0:T(8,128)S(1)} collective-permute-done((f32[16,256]{1,0:T(8,128)S(1)}, f32[16,256]{1,0:T(8,128)S(1)}, u32[]{:S(2)}, u32[]{:S(2)}) %collective-permute-start.8) | collective-permute-done | bytes 16416 | tf_op jit(solution)/shard_map/ppermute | solution.py:640
  24.0 0.1 z_faces.3
  24.1 2.8 %collective-permute-start.10 = (f32[64,128]{1,0:T(8,128)S(1)}, f32[64,128]{1,0:T(8,128)S(1)}, u32[]{:S(2)}, u32[]{:S(2)}) collective-permute-start(f32[64,128]{1,0:T(8,128)S(1)} %get-tuple-element.73), channel_id=1, source_target_pairs={{0,1},{1,0},{2,3},{3,2},{4,5},{5,4},{6,7},{7,6},{8,9},{9,8},{10,11... | collective-permute-start | bytes 98312 | tf_op jit(solution)/shard_map/ppermute | solution.py:640
  26.9 0.2 collective-permute-start.9
  27.0 0.1 assemble.1.s_ref
  27.1 1.8 %collective-permute-done.10.z_low_ref = f32[64,128]{1,0:T(8,128)S(1)} collective-permute-done((f32[64,128]{1,0:T(8,128)S(1)}, f32[64,128]{1,0:T(8,128)S(1)}, u32[]{:S(2)}, u32[]{:S(2)}) %collective-permute-start.10) | collective-permute-done | bytes 32800 | tf_op jit(solution)/shard_map/ppermute | solution.py:640
  28.9 0.0 collective-permute-done.9.z_high_ref
  28.9 1.2 %final.1 = f32[8,48,256]{2,1,0:T(8,128)} custom-call(f32[8,48,256]{2,1,0:T(8,128)S(1)} %assemble.1.s_ref, f32[8,256]{1,0:T(8,128)S(1)} %get-tuple-element.71.tab_ref, f32[64,128]{1,0:T(8,128)S(1)} %collective-permute-done.9.z_high_ref, f32[64,128]{1,0:T(8,128)S(1)} %collective-permute-done.10.z_low_ref, f32[128,256]{1,0:T(8,128)S(1)} %get-tuple-element.74.refs_0_, ...), custom_call_target="tpu_custom_call" | custom-call | flops 1400000000 | tf_op jit(solution)/shard_map/final/pallas_call | solution.py:567
  (3 shorter events, 0.0 us)
Async XLA Ops:
  0.0 0.7 %copy-start.6 = (f32[24,256]{1,0:T(8,128)S(1)}, f32[24,256]{1,0:T(8,128)}, u32[]{:S(2)}) copy-start(f32[24,256]{1,0:T(8,128)} %constant.2.clone.const_ref) | copy-start | bytes 73732
  0.0 1.0 %copy-start = (f32[8,48,256]{2,1,0:T(8,128)S(1)}, f32[8,48,256]{2,1,0:T(8,128)}, u32[]{:S(2)}) copy-start(f32[8,48,256]{2,1,0:T(8,128)} %u_ref.1) | copy-start | bytes 1179652
  0.0 1.1 %copy-start.1 = (f32[8,48,256]{2,1,0:T(8,128)S(1)}, f32[8,48,256]{2,1,0:T(8,128)}, u32[]{:S(2)}) copy-start(f32[8,48,256]{2,1,0:T(8,128)} %l_ref.1) | copy-start | bytes 1179652
  0.3 0.8 %copy-start.3 = (f32[1,6,32]{2,0,1:T(1,128)S(1)}, f32[1,6,32]{2,0,1:T(1,128)}, u32[]{:S(2)}) copy-start(f32[1,6,32]{2,0,1:T(1,128)} %param.9) | copy-start | bytes 2308
  0.4 0.8 %copy-start.4 = (f32[1,32]{1,0:T(1,128)S(1)}, f32[1,32]{1,0:T(1,128)}, u32[]{:S(2)}) copy-start(f32[1,32]{1,0:T(1,128)} %cinv_ref.1) | copy-start | bytes 388
  2.5 5.6 %collective-permute-start = (f32[48,256]{1,0:T(8,128)S(1)}, f32[48,256]{1,0:T(8,128)S(1)}, u32[]{:S(2)}, u32[]{:S(2)}) collective-permute-start(f32[48,256]{1,0:T(8,128)S(1)} %get-tuple-element.47), channel_id=1, source_target_pairs={{0,16},{1,17},{2,18},{3,19},{4,20},{5,21},{6,22},{7,23},{8,24},{9,... | collective-permute-start | bytes 147464 | tf_op jit(solution)/shard_map/ppermute | solution.py:640
  5.5 5.5 %collective-permute-start.3 = (f32[8,256]{1,0:T(8,128)S(1)}, f32[8,256]{1,0:T(8,128)S(1)}, u32[]{:S(2)}, u32[]{:S(2)}) collective-permute-start(f32[8,256]{1,0:T(8,128)S(1)} %get-tuple-element.46.tab_ref), channel_id=1, source_target_pairs={{0,2},{1,3},{2,0},{3,1},{4,6},{5,7},{6,4},{7,5},{8,10},{9,11},{10,... | collective-permute-start | bytes 24584 | tf_op jit(solution)/shard_map/ppermute | solution.py:640
  8.1 1.7 %copy-start.2 = (f32[8,8]{1,0:T(8,128)S(1)}, f32[8,8]{1,0:T(8,128)}, u32[]{:S(2)}) copy-start(f32[8,8]{1,0:T(8,128)} %basis_ref.1) | copy-start | bytes 772
  8.1 2.9 %collective-permute-start.1 = (f32[16,256]{1,0:T(8,128)S(1)}, f32[16,256]{1,0:T(8,128)S(1)}, u32[]{:S(2)}, u32[]{:S(2)}) collective-permute-start(f32[16,256]{1,0:T(8,128)S(1)} %get-tuple-element.48._), channel_id=1, source_target_pairs={{0,4},{1,5},{2,6},{3,7},{4,0},{5,1},{6,2},{7,3},{8,12},{9,13},{10,... | collective-permute-start | bytes 49160 | tf_op jit(solution)/shard_map/ppermute | solution.py:640
  8.2 1.6 %copy-start.5 = (f32[8]{0:T(128)S(1)}, f32[8]{0:T(128)}, u32[]{:S(2)}) copy-start(f32[8]{0:T(128)} %param.11) | copy-start | bytes 100
  8.2 3.2 %collective-permute-start.2 = (f32[16,256]{1,0:T(8,128)S(1)}, f32[16,256]{1,0:T(8,128)S(1)}, u32[]{:S(2)}, u32[]{:S(2)}) collective-permute-start(f32[16,256]{1,0:T(8,128)S(1)} %get-tuple-element.52), channel_id=1, source_target_pairs={{0,12},{1,13},{2,14},{3,15},{4,8},{5,9},{6,10},{7,11},{8,4},{9,5},... | collective-permute-start | bytes 49160 | tf_op jit(solution)/shard_map/ppermute | solution.py:640
  11.8 3.9 %collective-permute-start.4 = (f32[64,128]{1,0:T(8,128)S(1)}, f32[64,128]{1,0:T(8,128)S(1)}, u32[]{:S(2)}, u32[]{:S(2)}) collective-permute-start(f32[64,128]{1,0:T(8,128)S(1)} %get-tuple-element.60), channel_id=1, source_target_pairs={{0,1},{1,0},{2,3},{3,2},{4,5},{5,4},{6,7},{7,6},{8,9},{9,8},{10,11... | collective-permute-start | bytes 98312 | tf_op jit(solution)/shard_map/ppermute | solution.py:640
  13.4 2.3 %collective-permute-start.5 = (f32[64,128]{1,0:T(8,128)S(1)}, f32[64,128]{1,0:T(8,128)S(1)}, u32[]{:S(2)}, u32[]{:S(2)}) collective-permute-start(f32[64,128]{1,0:T(8,128)S(1)} %get-tuple-element.61), channel_id=1, source_target_pairs={{0,4},{1,2},{2,1},{3,7},{4,0},{5,6},{6,5},{7,3},{8,12},{9,10},{10,... | collective-permute-start | bytes 98312 | tf_op jit(solution)/shard_map/ppermute | solution.py:640
  16.4 4.2 %collective-permute-start.6 = (f32[56,256]{1,0:T(8,128)S(1)}, f32[56,256]{1,0:T(8,128)S(1)}, u32[]{:S(2)}, u32[]{:S(2)}) collective-permute-start(f32[56,256]{1,0:T(8,128)S(1)} %get-tuple-element.64), channel_id=1, source_target_pairs={{0,16},{1,17},{2,18},{3,19},{4,20},{5,21},{6,22},{7,23},{8,24},{9,... | collective-permute-start | bytes 172040 | tf_op jit(solution)/shard_map/ppermute | solution.py:640
  20.7 1.7 %collective-permute-start.7 = (f32[16,256]{1,0:T(8,128)S(1)}, f32[16,256]{1,0:T(8,128)S(1)}, u32[]{:S(2)}, u32[]{:S(2)}) collective-permute-start(f32[16,256]{1,0:T(8,128)S(1)} %get-tuple-element.67), channel_id=1, source_target_pairs={{0,4},{1,5},{2,6},{3,7},{4,0},{5,1},{6,2},{7,3},{8,12},{9,13},{10,... | collective-permute-start | bytes 49160 | tf_op jit(solution)/shard_map/ppermute | solution.py:640
  20.8 3.2 %collective-permute-start.8 = (f32[16,256]{1,0:T(8,128)S(1)}, f32[16,256]{1,0:T(8,128)S(1)}, u32[]{:S(2)}, u32[]{:S(2)}) collective-permute-start(f32[16,256]{1,0:T(8,128)S(1)} %get-tuple-element.68), channel_id=1, source_target_pairs={{0,12},{1,13},{2,14},{3,15},{4,8},{5,9},{6,10},{7,11},{8,4},{9,5},... | collective-permute-start | bytes 49160 | tf_op jit(solution)/shard_map/ppermute | solution.py:640
  24.1 4.8 %collective-permute-start.10 = (f32[64,128]{1,0:T(8,128)S(1)}, f32[64,128]{1,0:T(8,128)S(1)}, u32[]{:S(2)}, u32[]{:S(2)}) collective-permute-start(f32[64,128]{1,0:T(8,128)S(1)} %get-tuple-element.73), channel_id=1, source_target_pairs={{0,1},{1,0},{2,3},{3,2},{4,5},{5,4},{6,7},{7,6},{8,9},{9,8},{10,11... | collective-permute-start | bytes 98312 | tf_op jit(solution)/shard_map/ppermute | solution.py:640
  26.9 2.0 %collective-permute-start.9 = (f32[64,128]{1,0:T(8,128)S(1)}, f32[64,128]{1,0:T(8,128)S(1)}, u32[]{:S(2)}, u32[]{:S(2)}) collective-permute-start(f32[64,128]{1,0:T(8,128)S(1)} %get-tuple-element.72), channel_id=1, source_target_pairs={{0,4},{1,2},{2,1},{3,7},{4,0},{5,6},{6,5},{7,3},{8,12},{9,10},{10,... | collective-permute-start | bytes 98312 | tf_op jit(solution)/shard_map/ppermute | solution.py:640
